TPU v7x, 32 devices: a whole 2x2x4 slice. The times are simulated.
32 devices in a mesh: slab: 2 (over x), sx: 4 (over y, core), sy: 4 (over z).
Axes of the slice: x: 2, y: 2, z: 4, core: 2. Of those that a mesh axis runs over, the one named last changes fastest.
Arguments:
- start_states: float32 [2, 512, 1024], P('slab', 'sx', 'sy'), may hold values from -6 to 6
- source: float32 [2, 512, 1024], P('slab', 'sx', 'sy'), may hold values from -5 to 5
- cond_field: float32 [512, 1024], P('sx', 'sy'), may hold values from 0.5 to 2
- materials: int32 [64, 128], P('sx', 'sy'), may hold values from 0 to 1
- conductivity: float32 [2], replicated, may hold values from 1 to 4
- sink_rate: float32 [2], replicated, may hold values from 0.5 to 3
Outputs:
- defect: float32 [2, 512, 1024], P('slab', 'sx', 'sy')
- gradient: float32 [2, 512, 1024], P('slab', 'sx', 'sy')
Inputs may be any that keep to these rules, and one draw needn't show every extreme that they name: `materials`: 0 marks mold, 1 marks gob.
All inputs are finite; a program needn't handle non-finite values.
Results may differ from a plain program's by a relative error of at most 0.0001.
Values sent between devices are 32-bit elements; how exact they have to be, the bound alone decides.
No kernel may reach another device: no remote copies, remote signals or barrier semaphores. Data moves between devices by JAX's collectives and lax.ppermute only.
A program may use at most 64 MiB of HBM per device.

v0:
```python
import jax
import jax.numpy as jnp
from jax import lax
from jax.sharding import PartitionSpec as P

BLOCK = 8
STEPS = 3
NEWTON = 2
JACOBI = 4


time_step = 2.0


def padded_2(block, sides, width):
    for axis, dim in sides:
        count = lax.axis_size(axis)
        forward = [(i, i + 1) for i in range(count - 1)]
        backward = [(target, source) for source, target in forward]
        low = lax.ppermute(
            lax.slice_in_dim(block, block.shape[dim] - width, None, axis=dim), axis, forward
        )
        high = lax.ppermute(lax.slice_in_dim(block, 0, width, axis=dim), axis, backward)
        block = jnp.concatenate([low, block, high], axis=dim)
    return block


def passed_along(value, axis, steps):
    count = lax.axis_size(axis)
    pairs = [(source, (source + steps) % count) for source in range(count)]
    return lax.ppermute(value, axis, pairs)


def edge_terms(kappa_padded):
    center = kappa_padded[1:-1, 1:-1]
    west_edge = 0.5 * (center + kappa_padded[:-2, 1:-1])
    east_edge = 0.5 * (center + kappa_padded[2:, 1:-1])
    south_edge = 0.5 * (center + kappa_padded[1:-1, :-2])
    north_edge = 0.5 * (center + kappa_padded[1:-1, 2:])
    return (west_edge, east_edge, south_edge, north_edge)


def factor(diagonal, east_edge):
    blocks = diagonal.shape[0] // BLOCK
    pivots_in = diagonal.reshape(blocks, BLOCK, diagonal.shape[1])
    upper = (-time_step * east_edge).reshape(blocks, BLOCK, diagonal.shape[1])
    inverse = [1.0 / pivots_in[:, 0]]
    ratios = [upper[:, 0] * inverse[0]]
    for position in range(1, BLOCK):
        pivot = pivots_in[:, position] - upper[:, position - 1] * ratios[position - 1]
        inverse.append(1.0 / pivot)
        if position < BLOCK - 1:
            ratios.append(upper[:, position] * inverse[position])
    return (upper, ratios, inverse)


def block_solve(factors, right):
    upper, ratios, inverse = factors
    blocks = right.shape[0] // BLOCK
    shaped = right.reshape(blocks, BLOCK, right.shape[1])
    forward_vals = [shaped[:, 0] * inverse[0]]
    for position in range(1, BLOCK):
        forward_vals.append(
            (shaped[:, position] - upper[:, position - 1] * forward_vals[position - 1])
            * inverse[position]
        )
    result = list(forward_vals)
    for position in range(BLOCK - 2, -1, -1):
        result[position] = forward_vals[position] - ratios[position] * result[position + 1]
    return jnp.stack(result, axis=1).reshape(right.shape)


def jacobi(factors, edges, first_row, last_row, right, pad_fn):
    west_edge, east_edge, south_edge, north_edge = edges
    answer = block_solve(factors, right)
    for counter in range(JACOBI - 1):
        padded = pad_fn(answer)
        coupled = (
            first_row * west_edge * padded[:-2, 1:-1]
            + last_row * east_edge * padded[2:, 1:-1]
            + south_edge * padded[1:-1, :-2]
            + north_edge * padded[1:-1, 2:]
        )
        answer = block_solve(factors, right + time_step * coupled)
    return answer


def implicit_step(previous, forcing, sink_node, edges, solver):
    west_edge, east_edge, south_edge, north_edge = edges
    edge_sum = west_edge + east_edge + south_edge + north_edge
    current = previous
    for newton_it in range(NEWTON):
        padded = state_pad(current)
        laplace = (
            edge_sum * current
            - west_edge * padded[:-2, 1:-1]
            - east_edge * padded[2:, 1:-1]
            - south_edge * padded[1:-1, :-2]
            - north_edge * padded[1:-1, 2:]
        )
        tangent = jnp.tanh(current)
        diagonal = 1.0 + time_step * (edge_sum + sink_node * (1.0 - tangent * tangent))
        residual = previous - current - time_step * (laplace + sink_node * tangent - forcing)
        current = current + solver(diagonal, residual)
    return current


def adjoint_step(state, weight, sink_node, edges, solver):
    west_edge, east_edge, south_edge, north_edge = edges
    edge_sum = west_edge + east_edge + south_edge + north_edge
    tangent = jnp.tanh(state)
    diagonal = 1.0 + time_step * (edge_sum + sink_node * (1.0 - tangent * tangent))
    return solver(diagonal, weight)


def state_pad(field):
    return padded_2(field, (("sx", 0), ("sy", 1)), 1)


def sweep_pad(field):
    return padded_2(field, (("sx", 0), ("sy", 1)), 1)


def per_device(start_states, source, cond_field, materials, conductivity, sink_rate):
    node_material = jnp.repeat(jnp.repeat(materials, BLOCK, axis=0), BLOCK, axis=1)
    kappa_node = jnp.where(node_material == 1, conductivity[1], conductivity[0]) * cond_field
    sink_node = jnp.where(node_material == 1, sink_rate[1], sink_rate[0])
    local_rows = kappa_node.shape[0]
    kappa_padded = padded_2(kappa_node, (("sx", 0), ("sy", 1)), 1)
    edges = edge_terms(kappa_padded)
    row_ids = jnp.arange(local_rows) % BLOCK
    first_row = jnp.where(row_ids == 0, 1.0, 0.0).astype(jnp.float32)[:, None]
    last_row = jnp.where(row_ids == BLOCK - 1, 1.0, 0.0).astype(jnp.float32)[:, None]

    def solver(diagonal, right):
        return jacobi(factor(diagonal, edges[1]), edges, first_row, last_row, right, sweep_pad)

    start_state = start_states[0]
    forcing = source[0]
    states = []
    current = start_state
    for step_no in range(STEPS):
        current = implicit_step(current, forcing, sink_node, edges, solver)
        states.append(current)
    previous_end = passed_along(states[STEPS - 1], "slab", 1)
    defect = previous_end - start_state
    following = passed_along(defect, "slab", -1)
    weight = following
    for step_no in range(STEPS - 1, -1, -1):
        weight = adjoint_step(states[step_no], weight, sink_node, edges, solver)
    return (defect[None], (weight - defect)[None])


def solution(mesh):
    placed = (P("slab", "sx", "sy"), P("slab", "sx", "sy"), P("sx", "sy"), P("sx", "sy"), P(), P())
    return jax.shard_map(
        per_device,
        mesh=mesh,
        in_specs=placed,
        out_specs=(P("slab", "sx", "sy"), P("slab", "sx", "sy")),
        check_vma=False,
    )
```

profile of v0, /device:TPU:1, one launch (start us, length us, event | category | flops | bytes accessed | tf_op | source)
XLA Modules:
  0.0 579.6 jit_solution(11372565955300268452)
XLA Ops:
  3.7 4.6 collective-permute-start.4
  34.3 6.3 %collective-permute-start.8 = (f32[1,256]{0,1:T(8,128)S(1)}, f32[1,256]{0,1:T(8,128)S(1)}, u32[]{:S(2)}, u32[]{:S(2)}) collective-permute-start(f32[1,256]{0,1:T(8,128)S(1)} %get-tuple-element.951), channel_id=1, source_target_pairs={{0,4},{4,8},{8,12},{1,5},{5,9},{9,13},{2,6},{6,10},{10,14},{3,7},{... | collective-permute-start | bytes 3080 | tf_op jit(solution)/shard_map/ppermute | solution.py:20
  42.6 4.3 collective-permute-done.9
  60.6 4.3 collective-permute-done.13
  77.1 4.3 collective-permute-done.17
  93.7 4.2 collective-permute-done.21
  110.2 4.3 collective-permute-done.25
  126.7 4.3 collective-permute-done.29
  143.2 4.3 collective-permute-done.33
  159.8 4.2 collective-permute-done.37
  176.3 4.3 collective-permute-done.41
  192.8 4.3 collective-permute-done.45
  209.2 4.3 collective-permute-done.49
  225.9 4.2 collective-permute-done.53
  242.4 4.3 collective-permute-done.57
  258.9 4.3 collective-permute-done.61
  275.3 4.3 collective-permute-done.65
  308.5 4.3 collective-permute-done.73
  324.9 4.3 collective-permute-done.77
  341.4 4.3 collective-permute-done.81
  374.6 4.3 collective-permute-done.89
  391.0 4.3 collective-permute-done.93
  407.5 4.3 collective-permute-done.97
  435.0 4.3 collective-permute-done.103
  451.7 4.3 collective-permute-done.107
  468.2 4.3 collective-permute-done.111
  484.9 4.3 collective-permute-done.115
  501.3 4.3 collective-permute-done.119
  517.7 4.3 collective-permute-done.123
  534.3 4.3 collective-permute-done.127
  550.7 4.3 collective-permute-done.131
  567.2 4.3 collective-permute-done.135
  (863 shorter events, 431.7 us)
Async XLA Ops:
  1.5 23.8 %collective-permute-start.5 = (f32[1,256]{0,1:T(8,128)S(1)}, f32[1,256]{0,1:T(8,128)S(1)}, u32[]{:S(2)}, u32[]{:S(2)}) collective-permute-start(f32[1,256]{0,1:T(8,128)S(1)} %copy.218), channel_id=1, source_target_pairs={{4,0},{8,4},{12,8},{5,1},{9,5},{13,9},{6,2},{10,6},{14,10},{7,3},{... | collective-permute-start | bytes 3080 | tf_op jit(solution)/shard_map/ppermute | solution.py:23
  3.7 21.6 %collective-permute-start.4 = (f32[1,256]{0,1:T(8,128)S(1)}, f32[1,256]{0,1:T(8,128)S(1)}, u32[]{:S(2)}, u32[]{:S(2)}) collective-permute-start(f32[1,256]{0,1:T(8,128)S(1)} %copy.217), channel_id=1, source_target_pairs={{0,4},{4,8},{8,12},{1,5},{5,9},{9,13},{2,6},{6,10},{10,14},{3,7},{... | collective-permute-start | bytes 3080 | tf_op jit(solution)/shard_map/ppermute | solution.py:20
  12.4 6.6 %collective-permute-start.1 = (f32[1,256]{0,1:T(8,128)S(1)}, f32[1,256]{0,1:T(8,128)S(1)}, u32[]{:S(2)}, u32[]{:S(2)}) collective-permute-start(f32[1,256]{0,1:T(8,128)S(1)} %get-tuple-element.978), channel_id=1, source_target_pairs={{4,0},{8,4},{12,8},{5,1},{9,5},{13,9},{6,2},{10,6},{14,10},{7,3},{... | collective-permute-start | bytes 3080 | tf_op jit(solution)/shard_map/ppermute | solution.py:23
  20.0 9.9 %collective-permute-start.3 = (f32[130,1]{0,1:T(1,128)S(1)}, f32[130,1]{0,1:T(1,128)S(1)}, u32[]{:S(2)}, u32[]{:S(2)}) collective-permute-start(f32[130,1]{0,1:T(1,128)S(1)} %get-tuple-element.575), channel_id=1, source_target_pairs={{1,0},{2,1},{3,2},{5,4},{6,5},{7,6},{9,8},{10,9},{11,10},{13,12},{... | collective-permute-start | bytes 1568 | tf_op jit(solution)/shard_map/ppermute | solution.py:23
  21.3 8.6 %collective-permute-start.2 = (f32[130,1]{0,1:T(1,128)S(1)}, f32[130,1]{0,1:T(1,128)S(1)}, u32[]{:S(2)}, u32[]{:S(2)}) collective-permute-start(f32[130,1]{0,1:T(1,128)S(1)} %get-tuple-element.576), channel_id=1, source_target_pairs={{0,1},{1,2},{2,3},{4,5},{5,6},{6,7},{8,9},{9,10},{10,11},{12,13},{... | collective-permute-start | bytes 1568 | tf_op jit(solution)/shard_map/ppermute | solution.py:20
  34.3 8.3 %collective-permute-start.8 = (f32[1,256]{0,1:T(8,128)S(1)}, f32[1,256]{0,1:T(8,128)S(1)}, u32[]{:S(2)}, u32[]{:S(2)}) collective-permute-start(f32[1,256]{0,1:T(8,128)S(1)} %get-tuple-element.951), channel_id=1, source_target_pairs={{0,4},{4,8},{8,12},{1,5},{5,9},{9,13},{2,6},{6,10},{10,14},{3,7},{... | collective-permute-start | bytes 3080 | tf_op jit(solution)/shard_map/ppermute | solution.py:20
  40.6 6.3 %collective-permute-start.9 = (f32[1,256]{0,1:T(8,128)S(1)}, f32[1,256]{0,1:T(8,128)S(1)}, u32[]{:S(2)}, u32[]{:S(2)}) collective-permute-start(f32[1,256]{0,1:T(8,128)S(1)} %get-tuple-element.952), channel_id=1, source_target_pairs={{4,0},{8,4},{12,8},{5,1},{9,5},{13,9},{6,2},{10,6},{14,10},{7,3},{... | collective-permute-start | bytes 3080 | tf_op jit(solution)/shard_map/ppermute | solution.py:23
  58.7 6.3 %collective-permute-start.13 = (f32[1,256]{0,1:T(8,128)S(1)}, f32[1,256]{0,1:T(8,128)S(1)}, u32[]{:S(2)}, u32[]{:S(2)}) collective-permute-start(f32[1,256]{0,1:T(8,128)S(1)} %get-tuple-element.942), channel_id=1, source_target_pairs={{4,0},{8,4},{12,8},{5,1},{9,5},{13,9},{6,2},{10,6},{14,10},{7,3},{... | collective-permute-start | bytes 3080 | tf_op jit(solution)/shard_map/ppermute | solution.py:23
  75.1 6.3 %collective-permute-start.17 = (f32[1,256]{0,1:T(8,128)S(1)}, f32[1,256]{0,1:T(8,128)S(1)}, u32[]{:S(2)}, u32[]{:S(2)}) collective-permute-start(f32[1,256]{0,1:T(8,128)S(1)} %get-tuple-element.932), channel_id=1, source_target_pairs={{4,0},{8,4},{12,8},{5,1},{9,5},{13,9},{6,2},{10,6},{14,10},{7,3},{... | collective-permute-start | bytes 3080 | tf_op jit(solution)/shard_map/ppermute | solution.py:23
  91.7 6.3 %collective-permute-start.21 = (f32[1,256]{0,1:T(8,128)S(1)}, f32[1,256]{0,1:T(8,128)S(1)}, u32[]{:S(2)}, u32[]{:S(2)}) collective-permute-start(f32[1,256]{0,1:T(8,128)S(1)} %get-tuple-element.922), channel_id=1, source_target_pairs={{4,0},{8,4},{12,8},{5,1},{9,5},{13,9},{6,2},{10,6},{14,10},{7,3},{... | collective-permute-start | bytes 3080 | tf_op jit(solution)/shard_map/ppermute | solution.py:23
  108.3 6.3 %collective-permute-start.25 = (f32[1,256]{0,1:T(8,128)S(1)}, f32[1,256]{0,1:T(8,128)S(1)}, u32[]{:S(2)}, u32[]{:S(2)}) collective-permute-start(f32[1,256]{0,1:T(8,128)S(1)} %get-tuple-element.904), channel_id=1, source_target_pairs={{4,0},{8,4},{12,8},{5,1},{9,5},{13,9},{6,2},{10,6},{14,10},{7,3},{... | collective-permute-start | bytes 3080 | tf_op jit(solution)/shard_map/ppermute | solution.py:23
  124.8 6.3 %collective-permute-start.29 = (f32[1,256]{0,1:T(8,128)S(1)}, f32[1,256]{0,1:T(8,128)S(1)}, u32[]{:S(2)}, u32[]{:S(2)}) collective-permute-start(f32[1,256]{0,1:T(8,128)S(1)} %get-tuple-element.894), channel_id=1, source_target_pairs={{4,0},{8,4},{12,8},{5,1},{9,5},{13,9},{6,2},{10,6},{14,10},{7,3},{... | collective-permute-start | bytes 3080 | tf_op jit(solution)/shard_map/ppermute | solution.py:23
  141.2 6.3 %collective-permute-start.33 = (f32[1,256]{0,1:T(8,128)S(1)}, f32[1,256]{0,1:T(8,128)S(1)}, u32[]{:S(2)}, u32[]{:S(2)}) collective-permute-start(f32[1,256]{0,1:T(8,128)S(1)} %get-tuple-element.884), channel_id=1, source_target_pairs={{4,0},{8,4},{12,8},{5,1},{9,5},{13,9},{6,2},{10,6},{14,10},{7,3},{... | collective-permute-start | bytes 3080 | tf_op jit(solution)/shard_map/ppermute | solution.py:23
  157.7 6.3 %collective-permute-start.37 = (f32[1,256]{0,1:T(8,128)S(1)}, f32[1,256]{0,1:T(8,128)S(1)}, u32[]{:S(2)}, u32[]{:S(2)}) collective-permute-start(f32[1,256]{0,1:T(8,128)S(1)} %get-tuple-element.874), channel_id=1, source_target_pairs={{4,0},{8,4},{12,8},{5,1},{9,5},{13,9},{6,2},{10,6},{14,10},{7,3},{... | collective-permute-start | bytes 3080 | tf_op jit(solution)/shard_map/ppermute | solution.py:23
  174.4 6.3 %collective-permute-start.41 = (f32[1,256]{0,1:T(8,128)S(1)}, f32[1,256]{0,1:T(8,128)S(1)}, u32[]{:S(2)}, u32[]{:S(2)}) collective-permute-start(f32[1,256]{0,1:T(8,128)S(1)} %get-tuple-element.856), channel_id=1, source_target_pairs={{4,0},{8,4},{12,8},{5,1},{9,5},{13,9},{6,2},{10,6},{14,10},{7,3},{... | collective-permute-start | bytes 3080 | tf_op jit(solution)/shard_map/ppermute | solution.py:23
  190.8 6.3 %collective-permute-start.45 = (f32[1,256]{0,1:T(8,128)S(1)}, f32[1,256]{0,1:T(8,128)S(1)}, u32[]{:S(2)}, u32[]{:S(2)}) collective-permute-start(f32[1,256]{0,1:T(8,128)S(1)} %get-tuple-element.846), channel_id=1, source_target_pairs={{4,0},{8,4},{12,8},{5,1},{9,5},{13,9},{6,2},{10,6},{14,10},{7,3},{... | collective-permute-start | bytes 3080 | tf_op jit(solution)/shard_map/ppermute | solution.py:23
  207.3 6.3 %collective-permute-start.49 = (f32[1,256]{0,1:T(8,128)S(1)}, f32[1,256]{0,1:T(8,128)S(1)}, u32[]{:S(2)}, u32[]{:S(2)}) collective-permute-start(f32[1,256]{0,1:T(8,128)S(1)} %get-tuple-element.836), channel_id=1, source_target_pairs={{4,0},{8,4},{12,8},{5,1},{9,5},{13,9},{6,2},{10,6},{14,10},{7,3},{... | collective-permute-start | bytes 3080 | tf_op jit(solution)/shard_map/ppermute | solution.py:23
  223.8 6.3 %collective-permute-start.53 = (f32[1,256]{0,1:T(8,128)S(1)}, f32[1,256]{0,1:T(8,128)S(1)}, u32[]{:S(2)}, u32[]{:S(2)}) collective-permute-start(f32[1,256]{0,1:T(8,128)S(1)} %get-tuple-element.826), channel_id=1, source_target_pairs={{4,0},{8,4},{12,8},{5,1},{9,5},{13,9},{6,2},{10,6},{14,10},{7,3},{... | collective-permute-start | bytes 3080 | tf_op jit(solution)/shard_map/ppermute | solution.py:23
  240.5 6.3 %collective-permute-start.57 = (f32[1,256]{0,1:T(8,128)S(1)}, f32[1,256]{0,1:T(8,128)S(1)}, u32[]{:S(2)}, u32[]{:S(2)}) collective-permute-start(f32[1,256]{0,1:T(8,128)S(1)} %get-tuple-element.808), channel_id=1, source_target_pairs={{4,0},{8,4},{12,8},{5,1},{9,5},{13,9},{6,2},{10,6},{14,10},{7,3},{... | collective-permute-start | bytes 3080 | tf_op jit(solution)/shard_map/ppermute | solution.py:23
  256.9 6.3 %collective-permute-start.61 = (f32[1,256]{0,1:T(8,128)S(1)}, f32[1,256]{0,1:T(8,128)S(1)}, u32[]{:S(2)}, u32[]{:S(2)}) collective-permute-start(f32[1,256]{0,1:T(8,128)S(1)} %get-tuple-element.798), channel_id=1, source_target_pairs={{4,0},{8,4},{12,8},{5,1},{9,5},{13,9},{6,2},{10,6},{14,10},{7,3},{... | collective-permute-start | bytes 3080 | tf_op jit(solution)/shard_map/ppermute | solution.py:23
  273.4 6.3 %collective-permute-start.65 = (f32[1,256]{0,1:T(8,128)S(1)}, f32[1,256]{0,1:T(8,128)S(1)}, u32[]{:S(2)}, u32[]{:S(2)}) collective-permute-start(f32[1,256]{0,1:T(8,128)S(1)} %get-tuple-element.788), channel_id=1, source_target_pairs={{4,0},{8,4},{12,8},{5,1},{9,5},{13,9},{6,2},{10,6},{14,10},{7,3},{... | collective-permute-start | bytes 3080 | tf_op jit(solution)/shard_map/ppermute | solution.py:23
  289.9 6.3 %collective-permute-start.69 = (f32[1,256]{0,1:T(8,128)S(1)}, f32[1,256]{0,1:T(8,128)S(1)}, u32[]{:S(2)}, u32[]{:S(2)}) collective-permute-start(f32[1,256]{0,1:T(8,128)S(1)} %get-tuple-element.778), channel_id=1, source_target_pairs={{4,0},{8,4},{12,8},{5,1},{9,5},{13,9},{6,2},{10,6},{14,10},{7,3},{... | collective-permute-start | bytes 3080 | tf_op jit(solution)/shard_map/ppermute | solution.py:23
  306.5 6.3 %collective-permute-start.73 = (f32[1,256]{0,1:T(8,128)S(1)}, f32[1,256]{0,1:T(8,128)S(1)}, u32[]{:S(2)}, u32[]{:S(2)}) collective-permute-start(f32[1,256]{0,1:T(8,128)S(1)} %get-tuple-element.760), channel_id=1, source_target_pairs={{4,0},{8,4},{12,8},{5,1},{9,5},{13,9},{6,2},{10,6},{14,10},{7,3},{... | collective-permute-start | bytes 3080 | tf_op jit(solution)/shard_map/ppermute | solution.py:23
  323.0 6.3 %collective-permute-start.77 = (f32[1,256]{0,1:T(8,128)S(1)}, f32[1,256]{0,1:T(8,128)S(1)}, u32[]{:S(2)}, u32[]{:S(2)}) collective-permute-start(f32[1,256]{0,1:T(8,128)S(1)} %get-tuple-element.750), channel_id=1, source_target_pairs={{4,0},{8,4},{12,8},{5,1},{9,5},{13,9},{6,2},{10,6},{14,10},{7,3},{... | collective-permute-start | bytes 3080 | tf_op jit(solution)/shard_map/ppermute | solution.py:23
  339.5 6.3 %collective-permute-start.81 = (f32[1,256]{0,1:T(8,128)S(1)}, f32[1,256]{0,1:T(8,128)S(1)}, u32[]{:S(2)}, u32[]{:S(2)}) collective-permute-start(f32[1,256]{0,1:T(8,128)S(1)} %get-tuple-element.740), channel_id=1, source_target_pairs={{4,0},{8,4},{12,8},{5,1},{9,5},{13,9},{6,2},{10,6},{14,10},{7,3},{... | collective-permute-start | bytes 3080 | tf_op jit(solution)/shard_map/ppermute | solution.py:23
  356.0 6.3 %collective-permute-start.85 = (f32[1,256]{0,1:T(8,128)S(1)}, f32[1,256]{0,1:T(8,128)S(1)}, u32[]{:S(2)}, u32[]{:S(2)}) collective-permute-start(f32[1,256]{0,1:T(8,128)S(1)} %get-tuple-element.730), channel_id=1, source_target_pairs={{4,0},{8,4},{12,8},{5,1},{9,5},{13,9},{6,2},{10,6},{14,10},{7,3},{... | collective-permute-start | bytes 3080 | tf_op jit(solution)/shard_map/ppermute | solution.py:23
  372.6 6.3 %collective-permute-start.89 = (f32[1,256]{0,1:T(8,128)S(1)}, f32[1,256]{0,1:T(8,128)S(1)}, u32[]{:S(2)}, u32[]{:S(2)}) collective-permute-start(f32[1,256]{0,1:T(8,128)S(1)} %get-tuple-element.712), channel_id=1, source_target_pairs={{4,0},{8,4},{12,8},{5,1},{9,5},{13,9},{6,2},{10,6},{14,10},{7,3},{... | collective-permute-start | bytes 3080 | tf_op jit(solution)/shard_map/ppermute | solution.py:23
  389.1 6.3 %collective-permute-start.93 = (f32[1,256]{0,1:T(8,128)S(1)}, f32[1,256]{0,1:T(8,128)S(1)}, u32[]{:S(2)}, u32[]{:S(2)}) collective-permute-start(f32[1,256]{0,1:T(8,128)S(1)} %get-tuple-element.702), channel_id=1, source_target_pairs={{4,0},{8,4},{12,8},{5,1},{9,5},{13,9},{6,2},{10,6},{14,10},{7,3},{... | collective-permute-start | bytes 3080 | tf_op jit(solution)/shard_map/ppermute | solution.py:23
  405.5 6.3 %collective-permute-start.97 = (f32[1,256]{0,1:T(8,128)S(1)}, f32[1,256]{0,1:T(8,128)S(1)}, u32[]{:S(2)}, u32[]{:S(2)}) collective-permute-start(f32[1,256]{0,1:T(8,128)S(1)} %get-tuple-element.692), channel_id=1, source_target_pairs={{4,0},{8,4},{12,8},{5,1},{9,5},{13,9},{6,2},{10,6},{14,10},{7,3},{... | collective-permute-start | bytes 3080 | tf_op jit(solution)/shard_map/ppermute | solution.py:23
  433.0 6.3 %collective-permute-start.103 = (f32[1,256]{0,1:T(8,128)S(1)}, f32[1,256]{0,1:T(8,128)S(1)}, u32[]{:S(2)}, u32[]{:S(2)}) collective-permute-start(f32[1,256]{0,1:T(8,128)S(1)} %get-tuple-element.666), channel_id=1, source_target_pairs={{4,0},{8,4},{12,8},{5,1},{9,5},{13,9},{6,2},{10,6},{14,10},{7,3},{... | collective-permute-start | bytes 3080 | tf_op jit(solution)/shard_map/ppermute | solution.py:23
  449.8 6.3 %collective-permute-start.107 = (f32[1,256]{0,1:T(8,128)S(1)}, f32[1,256]{0,1:T(8,128)S(1)}, u32[]{:S(2)}, u32[]{:S(2)}) collective-permute-start(f32[1,256]{0,1:T(8,128)S(1)} %get-tuple-element.656), channel_id=1, source_target_pairs={{4,0},{8,4},{12,8},{5,1},{9,5},{13,9},{6,2},{10,6},{14,10},{7,3},{... | collective-permute-start | bytes 3080 | tf_op jit(solution)/shard_map/ppermute | solution.py:23
  532.3 6.3 %collective-permute-start.127 = (f32[1,256]{0,1:T(8,128)S(1)}, f32[1,256]{0,1:T(8,128)S(1)}, u32[]{:S(2)}, u32[]{:S(2)}) collective-permute-start(f32[1,256]{0,1:T(8,128)S(1)} %get-tuple-element.606), channel_id=1, source_target_pairs={{4,0},{8,4},{12,8},{5,1},{9,5},{13,9},{6,2},{10,6},{14,10},{7,3},{... | collective-permute-start | bytes 3080 | tf_op jit(solution)/shard_map/ppermute | solution.py:23
  (112 other events, 490.7 us)
where the time goes:
time: 591 us; the launch traced here: 580 us
  starting transfers between devices  288 us (49%)
  waiting for transfers between devices  243 us (41%)
  local copies, waits for them, and re-layouts  22.5 us (4%)
  other arithmetic  18.9 us (3%)
  between operations  6.95 us (1%)
    ppermute x68, waiting for transfers between devices, padded_2(): lax.ppermute(lax.slice_in_dim(block, 0, width, axis=dim), axis, backward)  235 us
    ppermute x68, starting transfers between devices, padded_2(): lax.ppermute(lax.slice_in_dim(block, block.shape[dim] - width, None, axis...  176 us
    ppermute x68, starting transfers between devices, padded_2(): lax.ppermute(lax.slice_in_dim(block, 0, width, axis=dim), axis, backward)  110 us
  transfers between devices with their start and end apart: 138, of which 68 were waited for; matrix products, arithmetic and copies ran while one was open for 1% of the time, Pallas kernels for 0%

commit v1 on v0

v1 whole, which is shorter than its diff:
```python
import functools

import jax
import jax.numpy as jnp
from jax import lax
from jax.experimental import pallas as pl
from jax.experimental.pallas import tpu as pltpu
from jax.sharding import PartitionSpec as P

BLOCK = 8
STEPS = 3
NEWTON = 2
JACOBI = 4
LANES = 128
HALO = 32
STRIP = LANES - 2 * HALO
CHUNK = 16

time_step = 2.0
half_step = 0.5 * time_step

VMEM = pl.BlockSpec(memory_space=pltpu.VMEM)
SMEM = pl.BlockSpec(memory_space=pltpu.SMEM)
F32 = jnp.float32


def roll(x, shift):
    return pltpu.roll(x, shift % LANES, axis=x.ndim - 1)


def lanes_of(x):
    return lax.broadcasted_iota(jnp.int32, x.shape, x.ndim - 1)


def pick(test, a, b):
    return jnp.where(test, a, b)


TILE = 3 * BLOCK + 1
HALF = BLOCK + 1
WIDE = 4 * BLOCK + 1


def first_pack(s, f, k):
    at = lanes_of(s)
    far = jnp.where(at == 96, roll(s, 64), roll(k, 65))
    return jnp.where(at < 32, s, jnp.where(at < 64, roll(f, 32), jnp.where(at < 96, roll(k, 64), far)))


def last_pack(s, f, k):
    at = lanes_of(s)
    far = jnp.where(at == 96, roll(s, 1), roll(k, 2))
    return jnp.where(at < 32, roll(s, 32), jnp.where(at < 64, roll(f, 64), jnp.where(at < 96, roll(k, 96), far)))


def pack_kernel(pos, conductivity, start, source, cond, materials, own, flip, along, across, split):
    y = pos[0]
    count, cells = materials.shape
    width = start.shape[1]
    column = lax.broadcasted_iota(jnp.int32, (cells, width), 1)
    cell = lax.broadcasted_iota(jnp.int32, (cells, width), 0)
    spread = jnp.where(column // BLOCK == cell, 1.0, 0.0).astype(F32)
    material = jnp.dot(materials[...].astype(F32), spread, preferred_element_type=F32)
    is_gob = material > 0.5
    factor = jnp.where(is_gob, conductivity[1], conductivity[0])
    m0, m1 = material[:, :LANES], material[:, LANES:]
    lower = y == 0

    def place(p, tiles, packs):
        (first0, last0, first1, last1) = packs
        if tiles is not None:
            for a, (x0, x1) in enumerate(tiles):
                own[a * BLOCK + p] = pick(lower, x0, x1)
                flip[a * BLOCK + p] = pick(lower, x1, x0)
        own[TILE + p] = pick(lower, first1, last0)
        flip[TILE + p] = pick(lower, last0, first1)
        along[p] = pick(lower, last1, first0)
        across[p] = pick(lower, first0, last1)

    for a, ref in enumerate((start, source, cond)):
        split[2 * a] = ref[:, :LANES]
        split[2 * a + 1] = ref[:, LANES:]
    for p in range(BLOCK):
        rows = pl.ds(p, count, stride=BLOCK)
        s0, s1, f0, f1, k0, k1 = (split[a, rows, :] for a in range(6))
        k0, k1 = k0 * factor[:, :LANES], k1 * factor[:, LANES:]
        packs = (first_pack(s0, f0, k0), last_pack(s0, f0, k0), first_pack(s1, f1, k1), last_pack(s1, f1, k1))
        place(p, ((s0, s1), (f0, f1), (k0, k1)), packs)
    own[3 * BLOCK] = pick(lower, m0, m1)
    flip[3 * BLOCK] = pick(lower, m1, m0)
    place(BLOCK, None, (m0, roll(m0, 32), m1, roll(m1, 32)))


def window_kernel(pos, own, other, along, across, mine, theirs):
    lower = pos[0] == 0
    even = pos[1] == 0
    at = lax.broadcasted_iota(jnp.int32, own.shape[1:], 1)

    def put(slot, index, left, right):
        mine[slot, index] = pick(even, left, right)
        theirs[slot, index] = pick(even, right, left)

    for slot, (tile, outer) in enumerate(((own, along), (other, across))):
        for p in range(BLOCK + 1):
            inner, far = tile[TILE + p], outer[p]
            west, east = pick(lower, far, inner), pick(lower, inner, far)
            if p == BLOCK:
                m = tile[3 * BLOCK]
                put(slot, 4 * BLOCK, jnp.where(at < 32, west, roll(m, 32)), jnp.where(at >= 96, roll(east, 96), roll(m, 96)))
                continue
            s, f, k = tile[p], tile[BLOCK + p], tile[2 * BLOCK + p]
            for a, x in enumerate((s, f, k)):
                left = jnp.where(at < 32, roll(west, -32 * a), roll(x, 32))
                right = jnp.where(at >= 96, roll(east, 96 - 32 * a), roll(x, 96))
                put(slot, a * BLOCK + p, left, right)
            left = jnp.where(at < 2, roll(west, 32), jnp.where(at == 127, roll(s, 31), roll(k, 30)))
            right = jnp.where(at == 0, roll(s, 97), jnp.where(at == 1, roll(k, 98), jnp.where(at == 127, roll(east, 31), roll(east, 29))))
            put(slot, 3 * BLOCK + p, left, right)


def chunks(lines):
    for first in range(0, lines, CHUNK):
        yield first


def shifted(ref, p, first, by):
    return ref[p, pl.ds(BLOCK + first + by, CHUNK), :]


def padded(ref, p, first):
    return ref[p, pl.ds(BLOCK + first, CHUNK), :]


def put_padded(ref, p, first, value):
    ref[p, pl.ds(BLOCK + first, CHUNK), :] = value


def clear_ends(ref, lines):
    zero = jnp.zeros((BLOCK, LANES), F32)
    for p in (0, BLOCK - 1):
        ref[p, 0:BLOCK, :] = zero
        ref[p, BLOCK + lines : 2 * BLOCK + lines, :] = zero


def factor_and_solve(first, diagonal, right, south, north, east, west, scaled, answer):
    at = pl.ds(first, CHUNK)
    keep_right, keep_south, keep_north, keep_lower, keep_upper, keep_ends = scaled
    values = []
    ratio = None
    value = None
    edge = None
    for p in range(BLOCK):
        pivot = diagonal(p)
        if p:
            pivot = pivot - edge * ratio
        inverse = 1.0 / pivot
        scaled_right = right(p) * inverse
        keep_right[p, at, :] = scaled_right
        keep_south[p, at, :] = south[p, at, :] * inverse
        keep_north[p, at, :] = north[p, at, :] * inverse
        if p == 0:
            keep_ends[0, at, :] = west[at, :] * inverse
            value = scaled_right
        else:
            lower = edge * inverse
            keep_lower[p, at, :] = lower
            value = scaled_right + lower * value
        edge = east[p, at, :]
        ratio = edge * inverse
        if p < BLOCK - 1:
            keep_upper[p, at, :] = ratio
        else:
            keep_ends[1, at, :] = ratio
        values.append(value)
    back_substitute(first, values, keep_upper, lambda p, z: put_padded(answer, p, first, z))


def back_substitute(first, values, upper, store):
    at = pl.ds(first, CHUNK)
    z = values[BLOCK - 1]
    store(BLOCK - 1, z)
    for p in range(BLOCK - 2, -1, -1):
        z = values[p] + upper[p, at, :] * z
        store(p, z)


def sweep(lines, scaled, old, store):
    keep_right, keep_south, keep_north, keep_lower, keep_upper, keep_ends = scaled
    for first in chunks(lines):
        at = pl.ds(first, CHUNK)
        values = []
        for p in range(BLOCK):
            z = padded(old, p, first)
            value = keep_right[p, at, :] + keep_south[p, at, :] * roll(z, 1) + keep_north[p, at, :] * roll(z, -1)
            if p == 0:
                value = value + keep_ends[0, at, :] * shifted(old, BLOCK - 1, first, -1)
            if p == BLOCK - 1:
                value = value + keep_ends[1, at, :] * shifted(old, 0, first, 1)
            if p:
                value = value + keep_lower[p, at, :] * values[-1]
            values.append(value)
        back_substitute(first, values, keep_upper, functools.partial(store, first))


def put_into(ref):
    return lambda first, p, z: put_padded(ref, p, first, z)


def forward_kernel(pos, sinks, mine, theirs, states, south, north, east, west, base, sink, level, forcing, kappa, edge, previous, old, new, *scaled):
    y, c, strip, strips = pos[0], pos[1], pos[2], pos[3]
    lines = base.shape[1]
    count = mine.shape[2]
    for ref in (level, kappa, old, new):
        clear_ends(ref, lines)
    lane = lax.broadcasted_iota(jnp.int32, (count, LANES), 1)
    column = strip * STRIP - HALO + lane
    inside = (column >= 0) & (column < strips * STRIP)

    for ref, core in ((mine, c), (theirs, 1 - c)):
        for slot in range(2):
            chip = y if slot == 0 else 1 - y
            first = pl.multiple_of((2 * chip + core) * count, BLOCK)
            for p in range(BLOCK):
                level[p, pl.ds(BLOCK + first, count), :] = ref[slot, p]
                forcing[p, pl.ds(first, count), :] = time_step * ref[slot, BLOCK + p]
                kappa[p, pl.ds(BLOCK + first, count), :] = jnp.where(inside, ref[slot, 2 * BLOCK + p], 0.0)
                edge[p, pl.ds(first, count), :] = ref[slot, 3 * BLOCK + p]
            sink[pl.ds(first, count), :] = time_step * jnp.where(ref[slot, 4 * BLOCK] > 0.5, sinks[1], sinks[0])

    lane = lax.broadcasted_iota(jnp.int32, (CHUNK, LANES), 1)
    column = strip * STRIP - HALO + lane
    is_first = lane == 0
    is_last = lane == LANES - 1
    has_south = column != 0
    has_north = column != strips * STRIP - 1
    before = strip * STRIP - HALO > 0
    after = strip * STRIP - HALO + LANES < strips * STRIP

    for first in chunks(lines):
        at = pl.ds(first, CHUNK)
        k = [padded(kappa, p, first) for p in range(BLOCK)]
        wests = [half_step * (k[0] + shifted(kappa, BLOCK - 1, first, -1))]
        wests += [half_step * (k[p] + k[p - 1]) for p in range(1, BLOCK)]
        wests += [half_step * (k[BLOCK - 1] + shifted(kappa, 0, first, 1))]
        west[at, :] = wests[0]
        for p in range(BLOCK):
            side = edge[p, at, :]
            below = jnp.where(is_first, jnp.where(before, roll(side, -1), 0.0), roll(k[p], 1))
            above = jnp.where(is_last, jnp.where(after, roll(side, 1), 0.0), roll(k[p], -1))
            s = half_step * (k[p] + below)
            n = half_step * (k[p] + above)
            base[p, at, :] = 1.0 + (wests[p] + wests[p + 1] + s + n)
            south[p, at, :] = jnp.where(has_south, s, 0.0)
            north[p, at, :] = jnp.where(has_north, n, 0.0)
            east[p, at, :] = wests[p + 1]

    def newton(from_previous):
        for first in chunks(lines):
            at = pl.ds(first, CHUNK)
            sink_here = sink[at, :]
            tangents = {}
            currents = {}

            def state(p):
                if p not in currents:
                    currents[p] = padded(level, p, first)
                    tangents[p] = jnp.tanh(currents[p])
                return currents[p], tangents[p]

            def diagonal(p):
                _, tangent = state(p)
                return base[p, at, :] + sink_here * (1.0 - tangent * tangent)

            def right(p):
                current, tangent = state(p)
                side = edge[p, at, :]
                below = jnp.where(is_first, side, roll(current, 1))
                above = jnp.where(is_last, side, roll(current, -1))
                behind = padded(level, p - 1, first) if p else shifted(level, BLOCK - 1, first, -1)
                ahead = padded(level, p + 1, first) if p < BLOCK - 1 else shifted(level, 0, first, 1)
                behind_edge = east[p - 1, at, :] if p else west[at, :]
                pulled = (south[p, at, :] * below + north[p, at, :] * above + behind_edge * behind + east[p, at, :] * ahead)
                if from_previous:
                    held = (1.0 - base[p, at, :]) * current
                else:
                    held = previous[p, at, :] - base[p, at, :] * current
                return held + pulled - sink_here * tangent + forcing[p, at, :]

            factor_and_solve(first, diagonal, right, south, north, east, west, scaled, old)
        sweep(lines, scaled, old, put_into(new))
        sweep(lines, scaled, new, put_into(old))
        sweep(lines, scaled, old, lambda first, p, z: put_padded(level, p, first, padded(level, p, first) + z))

    def step(number, carry):
        for p in range(BLOCK):
            previous[p] = level[p, pl.ds(BLOCK, lines), :]
        newton(True)
        for _ in range(1, NEWTON):
            newton(False)
        for p in range(BLOCK):
            states[number * BLOCK + p] = level[p, pl.ds(BLOCK, lines), :]
        return carry

    lax.fori_loop(0, STEPS, step, 0)


def adjoint_kernel(states, weight, south, north, east, west, base, sink, out, old, new, given, *scaled):
    lines = base.shape[1]
    for ref in (old, new):
        clear_ends(ref, lines)
    for p in range(BLOCK):
        given[p] = weight[p]

    def step(number, carry):
        level = STEPS - 1 - number
        for first in chunks(lines):
            at = pl.ds(first, CHUNK)
            sink_here = sink[at, :]

            def diagonal(p):
                tangent = jnp.tanh(states[level * BLOCK + p, at, :])
                return base[p, at, :] + sink_here * (1.0 - tangent * tangent)

            def right(p):
                return given[p, at, :]

            factor_and_solve(first, diagonal, right, south, north, east, west, scaled, old)
        sweep(lines, scaled, old, put_into(new))
        sweep(lines, scaled, new, put_into(old))

        def store(first, p, z):
            given[p, pl.ds(first, CHUNK), :] = z

        sweep(lines, scaled, old, store)
        return carry

    lax.fori_loop(0, STEPS, step, 0)
    count = out.shape[2]
    at = lax.broadcasted_iota(jnp.int32, (count, LANES), 1)
    for core in range(2):
        for p in range(BLOCK):
            low = given[p, pl.ds(core * count, count), :]
            high = given[p, pl.ds((2 + core) * count, count), :]
            out[core, p] = jnp.where(at < STRIP, roll(low, -HALO), roll(high, HALO))


def defect_kernel(pos, states, mine, theirs, weight, out):
    y, c = pos[0], pos[1]
    count = mine.shape[2]
    at = lax.broadcasted_iota(jnp.int32, (count, LANES), 1)
    for ref, core in ((mine, c), (theirs, 1 - c)):
        for p in range(BLOCK):
            ends = []
            for slot in range(2):
                chip = y if slot == 0 else 1 - y
                first = pl.multiple_of((2 * chip + core) * count, BLOCK)
                value = states[(STEPS - 1) * BLOCK + p, pl.ds(first, count), :] - ref[slot, p]
                weight[p, pl.ds(first, count), :] = value
                ends.append(value)
            low, high = pick(y == 0, ends[0], ends[1]), pick(y == 0, ends[1], ends[0])
            out[core, p] = jnp.where(at < STRIP, roll(low, -HALO), roll(high, HALO))


def swap_kernel(pos, adjoint, defect, keep, send):
    c = pos[1]
    for p in range(BLOCK):
        for a in range(2):
            other = defect[1 - c, p]
            held = defect[c, p]
            if a == 0:
                other = adjoint[1 - c, p] - other
                held = adjoint[c, p] - held
            keep[a, p] = held
            send[a, p] = other


def tile_kernel(pos, mine, theirs, keep, send):
    y, c = pos[0], pos[1]
    count = mine.shape[2]
    at = lax.broadcasted_iota(jnp.int32, (count, LANES), 1)
    for a in range(2):
        for p in range(BLOCK):
            even = pick(c == 0, mine[a, p], theirs[a, p])
            odd = pick(c == 0, theirs[a, p], mine[a, p])
            chip0 = jnp.where(at < STRIP, even, roll(odd, STRIP))
            chip1 = jnp.where(at < STRIP, roll(even, STRIP), odd)
            rows = pl.ds(p, count, stride=BLOCK)
            keep[a, rows, :] = pick(y == 0, chip0, chip1)
            send[a, rows, :] = pick(y == 0, chip1, chip0)


def join_kernel(pos, mine, theirs, gradient, defect):
    lower = pos[0] == 0
    for a, ref in enumerate((gradient, defect)):
        ref[:, :LANES] = pick(lower, mine[a], theirs[a])
        ref[:, LANES:] = pick(lower, theirs[a], mine[a])


def per_device(slabs, strips_y, start_states, source, cond_field, materials, conductivity, sink_rate):
    sx = lax.axis_index("sx")
    z = lax.axis_index("sy")
    y, c = sx // 2, sx % 2
    pos = jnp.stack([y, c, 4 * z + sx, jnp.int32(4 * strips_y)]).astype(jnp.int32)
    start, forcing = start_states[0], source[0]
    rows = start.shape[0]
    count = rows // BLOCK
    lines = 4 * count
    shape = lambda *dims: jax.ShapeDtypeStruct(dims, F32)
    params = pltpu.CompilerParams(vmem_limit_bytes=48 * 1024 * 1024)

    def call(body, outs, ins, scratch=(), flops=0):
        specs = [SMEM if s else VMEM for s in ins]
        cost = pl.CostEstimate(flops=flops, bytes_accessed=1 << 20, transcendentals=0)
        return pl.pallas_call(body, out_shape=outs, in_specs=specs, out_specs=[VMEM] * len(outs), scratch_shapes=list(scratch), compiler_params=params, cost_estimate=cost)

    def joint(y_, c_, z_):
        return (2 * y_ + c_) * strips_y + z_

    everyone = [(a, b, d) for a in range(2) for b in range(2) for d in range(strips_y)]
    top = strips_y - 1

    def along_to(a, b, d):
        if a == 1:
            return (1, b, d - 1) if d > 0 else (0, b, d)
        return (0, b, d + 1) if d < top else (1, b, d)

    def across_to(a, b, d):
        if a == 1:
            return (0, b, d + 1) if d < top else (1, b, d)
        return (1, b, d - 1) if d > 0 else (0, b, d)

    along_pairs = [(joint(*v), joint(*along_to(*v))) for v in everyone]
    across_pairs = [(joint(*v), joint(*across_to(*v))) for v in everyone]
    flip_pairs = [(0, 2), (1, 3), (2, 0), (3, 1)]
    core_pairs = [(0, 1), (1, 0), (2, 3), (3, 2)]
    forth = [(i, (i + 1) % slabs) for i in range(slabs)]
    back = [(b, a) for a, b in forth]

    own, flip, along, across = call(
        pack_kernel,
        [shape(TILE + HALF, count, LANES)] * 2 + [shape(HALF, count, LANES)] * 2,
        (1, 1, 0, 0, 0, 0),
        [pltpu.VMEM((6, rows, LANES), F32)],
    )(pos, conductivity, start, forcing, cond_field, materials)
    other = lax.ppermute(flip, "sx", flip_pairs)
    along = lax.ppermute(along, ("sx", "sy"), along_pairs)
    across = lax.ppermute(across, ("sx", "sy"), across_pairs)

    mine, send = call(window_kernel, [shape(2, WIDE, count, LANES)] * 2, (1, 0, 0, 0, 0))(pos, own, other, along, across)
    theirs = lax.ppermute(send, "sx", core_pairs)

    starts = jnp.stack([mine[:, :BLOCK], theirs[:, :BLOCK]])
    next_starts = lax.ppermute(starts, "slab", back)

    whole = shape(BLOCK, lines, LANES)
    flat = shape(lines, LANES)
    buffer = pltpu.VMEM((BLOCK, lines + 2 * BLOCK, LANES), F32)
    plain = pltpu.VMEM((BLOCK, lines, LANES), F32)
    ends = pltpu.VMEM((2, lines, LANES), F32)
    scaled = [plain] * 5 + [ends]
    states, south, north, east, west, base, sink = call(
        forward_kernel,
        [shape(STEPS * BLOCK, lines, LANES), whole, whole, whole, flat, whole, flat],
        (1, 1, 0, 0),
        [buffer, plain, buffer, plain, plain, buffer, buffer] + scaled,
        flops=20_000_000,
    )(pos, sink_rate, mine, theirs)

    pair = shape(2, BLOCK, count, LANES)
    weight, ends_here = call(defect_kernel, [whole, pair], (1, 0, 0, 0))(pos, states, next_starts[0], next_starts[1])
    defect = lax.ppermute(ends_here, "slab", forth)

    (adjoint,) = call(adjoint_kernel, [pair], (0,) * 8, [buffer, buffer, plain] + scaled, flops=10_000_000)(
        states, weight, south, north, east, west, base, sink
    )

    keep, send = call(swap_kernel, [pair] * 2, (1, 0, 0))(pos, adjoint, defect)
    got = lax.ppermute(send, "sx", core_pairs)
    keep, send = call(tile_kernel, [shape(2, rows, LANES)] * 2, (1, 0, 0))(pos, keep, got)
    got = lax.ppermute(send, "sx", flip_pairs)
    gradient, defect = call(join_kernel, [shape(rows, 2 * LANES)] * 2, (1, 0, 0))(pos, keep, got)
    return (defect[None], gradient[None])


def solution(mesh):
    placed = (P("slab", "sx", "sy"), P("slab", "sx", "sy"), P("sx", "sy"), P("sx", "sy"), P(), P())
    return jax.shard_map(
        functools.partial(per_device, mesh.shape["slab"], mesh.shape["sy"]),
        mesh=mesh,
        in_specs=placed,
        out_specs=(P("slab", "sx", "sy"), P("slab", "sx", "sy")),
        check_vma=False,
    )
```

time: 591 us -> 43.6 us (0.07)
  the two profiles are of different devices: /device:TPU:1 before, /device:TPU:0 now
where the time goes in v1:
time: 43.6 us; the launch traced here: 43.4 us
  waiting for transfers between devices  15.2 us (35%)
  Pallas kernels  13.1 us (30%)
  starting transfers between devices  10.8 us (25%)
  local copies, waits for them, and re-layouts  3.41 us (8%)
  between operations  0.77 us (2%)
    ppermute x1, waiting for transfers between devices, per_device(): along = lax.ppermute(along, ('sx', 'sy'), along_pairs)  6 us
    pallas_call x1, Pallas kernels, per_device(): call(forward_kernel, [shape(STEPS * BLOCK, lines, LANES), whole, whole, w...  5.42 us
    ppermute x1, waiting for transfers between devices, per_device(): got = lax.ppermute(send, 'sx', flip_pairs)  3.82 us
    unnamed x12, local copies, waits for them, and re-layouts  3.38 us
    ppermute x1, starting transfers between devices, per_device(): other = lax.ppermute(flip, 'sx', flip_pairs)  3.03 us
    pallas_call x1, Pallas kernels, per_device(): call(adjoint_kernel, [pair], (0,) * 8, [buffer, buffer, plain] + scaled,...  2.32 us
    ppermute x1, waiting for transfers between devices, per_device(): theirs = lax.ppermute(send, 'sx', core_pairs)  1.9 us
    ppermute x1, starting transfers between devices, per_device(): got = lax.ppermute(send, 'sx', flip_pairs)  1.8 us
  transfers between devices with their start and end apart: 8, of which 6 were waited for; matrix products, arithmetic and copies ran while one was open for 0% of the time, Pallas kernels for 18%

profile of v1, /device:TPU:0, one launch (start us, length us, event | category | flops | bytes accessed | tf_op | source)
XLA Modules:
  0.0 43.4 jit_solution(2390348287900079618)
XLA Ops:
  0.6 0.0 copy-start.3
  0.7 0.1 pad_add_fusion.pos
  0.7 0.6 %copy-done.3 = s32[16,32]{1,0:T(8,128)S(1)} copy-done((s32[16,32]{1,0:T(8,128)S(1)}, s32[16,32]{1,0:T(8,128)}, u32[]{:S(2)}) %copy-start.3) | copy-done | bytes 2072
  1.3 0.1 copy-done.5
  1.4 0.9 %copy-done = f32[1,128,256]{2,1,0:T(8,128)S(1)} copy-done((f32[1,128,256]{2,1,0:T(8,128)S(1)}, f32[1,128,256]{2,1,0:T(8,128)}, u32[]{:S(2)}) %copy-start) | copy-done | bytes 131096
  2.3 0.9 %copy-done.1 = f32[1,128,256]{2,1,0:T(8,128)S(1)} copy-done((f32[1,128,256]{2,1,0:T(8,128)S(1)}, f32[1,128,256]{2,1,0:T(8,128)}, u32[]{:S(2)}) %copy-start.1) | copy-done | bytes 131096
  3.2 0.9 %copy-done.2 = f32[128,256]{1,0:T(8,128)S(1)} copy-done((f32[128,256]{1,0:T(8,128)S(1)}, f32[128,256]{1,0:T(8,128)}, u32[]{:S(2)}) %copy-start.2) | copy-done | bytes 131096
  4.1 1.0 %shard_map.77 = (f32[34,16,128]{2,1,0:T(8,128)S(1)}, f32[34,16,128]{2,1,0:T(8,128)S(1)}, f32[9,16,128]{2,1,0:T(8,128)S(1)}, f32[9,16,128]{2,1,0:T(8,128)S(1)}) custom-call(s32[4]{0:T(128)S(1)} %pad_add_fusion.pos, f32[2]{0:T(128)S(1)} %copy-done.5, f32[128,256]{1,0:T(8,128)S(1)} %bitcast.15, f32[128,256]{1,0:T(8,128)S(1)} %bitcast.16, ...), custom_call_target="tpu_custom_call" | custom-call | bytes 1048576 | tf_op jit(solution)/shard_map/pallas_call | solution.py:439
  5.1 3.0 %collective-permute-start = (f32[34,16,128]{2,1,0:T(8,128)S(1)}, f32[34,16,128]{2,1,0:T(8,128)S(1)}, u32[]{:S(2)}, u32[]{:S(2)}) collective-permute-start(f32[34,16,128]{2,1,0:T(8,128)S(1)} %get-tuple-element.24), channel_id=1, source_target_pairs={{0,8},{4,12},{8,0},{12,4},{1,9},{5,13},{9,1},{13,5},{2,10},{6,14},... | collective-permute-start | bytes 835592 | tf_op jit(solution)/shard_map/ppermute | solution.py:445
  8.1 1.6 %collective-permute-start.1 = (f32[9,16,128]{2,1,0:T(8,128)S(1)}, f32[9,16,128]{2,1,0:T(8,128)S(1)}, u32[]{:S(2)}, u32[]{:S(2)}) collective-permute-start(f32[9,16,128]{2,1,0:T(8,128)S(1)} %get-tuple-element.25), channel_id=1, source_target_pairs={{0,1},{1,2},{2,3},{3,11},{4,5},{5,6},{6,7},{7,15},{8,0},{9,8},{10,... | collective-permute-start | bytes 221192 | tf_op jit(solution)/shard_map/ppermute | solution.py:446
  9.7 0.7 %collective-permute-start.2 = (f32[9,16,128]{2,1,0:T(8,128)S(1)}, f32[9,16,128]{2,1,0:T(8,128)S(1)}, u32[]{:S(2)}, u32[]{:S(2)}) collective-permute-start(f32[9,16,128]{2,1,0:T(8,128)S(1)} %get-tuple-element.26), channel_id=1, source_target_pairs={{0,0},{1,8},{2,9},{3,10},{4,4},{5,12},{6,13},{7,14},{8,1},{9,2},{1... | collective-permute-start | bytes 221192 | tf_op jit(solution)/shard_map/ppermute | solution.py:447
  10.4 6.0 %collective-permute-done.1.along = f32[9,16,128]{2,1,0:T(8,128)S(1)} collective-permute-done((f32[9,16,128]{2,1,0:T(8,128)S(1)}, f32[9,16,128]{2,1,0:T(8,128)S(1)}, u32[]{:S(2)}, u32[]{:S(2)}) %collective-permute-start.1) | collective-permute-done | bytes 73760 | tf_op jit(solution)/shard_map/ppermute | solution.py:446
  16.4 0.0 collective-permute-done.2.across
  16.4 0.0 collective-permute-done.other
  16.4 1.2 %shard_map.78 = (f32[2,33,16,128]{3,2,1,0:T(8,128)S(1)}, f32[2,33,16,128]{3,2,1,0:T(8,128)S(1)}) custom-call(s32[4]{0:T(128)S(1)} %pad_add_fusion.pos, f32[34,16,128]{2,1,0:T(8,128)S(1)} %get-tuple-element.23.own, f32[34,16,128]{2,1,0:T(8,128)S(1)} %collective-permute-done.other, f32[9,16,128]{2,1,0:T(8,128)S(1)} %collective-permute-done.1.along, ...), custom_call_target="tpu_custom_call" | custom-call | bytes 1048576 | tf_op jit(solution)/shard_map/pallas_call | solution.py:449
  17.6 0.1 collective-permute-start.3
  17.7 1.9 %collective-permute-done.3.theirs = f32[2,33,16,128]{3,2,1,0:T(8,128)S(1)} collective-permute-done((f32[2,33,16,128]{3,2,1,0:T(8,128)S(1)}, f32[2,33,16,128]{3,2,1,0:T(8,128)S(1)}, u32[]{:S(2)}, u32[]{:S(2)}) %collective-permute-start.3) | collective-permute-done | bytes 540704 | tf_op jit(solution)/shard_map/ppermute | solution.py:450
  19.6 0.0 copy-start.4
  19.7 1.8 %collective-permute-start.4 = (f32[2,2,8,16,128]{4,3,2,1,0:T(8,128)S(1)}, f32[2,2,8,16,128]{4,3,2,1,0:T(8,128)S(1)}, u32[]{:S(2)}, u32[]{:S(2)}) collective-permute-start(f32[2,2,8,16,128]{4,3,2,1,0:T(8,128)S(1)} %pad_maximum_fusion), channel_id=1, source_target_pairs={{16,0},{0,16},{17,1},{1,17},{18,2},{2,18},{19,3},{3,19},{20,4},{4,... | collective-permute-start | bytes 786440 | tf_op jit(solution)/shard_map/ppermute | solution.py:453
  21.4 5.4 %shard_map.79 = (f32[24,64,128]{2,1,0:T(8,128)S(1)}, f32[8,64,128]{2,1,0:T(8,128)S(1)}, f32[8,64,128]{2,1,0:T(8,128)S(1)}, f32[8,64,128]{2,1,0:T(8,128)S(1)}, f3...) custom-call(s32[4]{0:T(128)S(1)} %pad_add_fusion.pos, f32[2]{0:T(128)S(1)} %copy-done.4, ...), custom_call_target="tpu_custom_call" | custom-call | flops 20000000 | bytes 1048576 | tf_op jit(solution)/shard_map/pallas_call | solution.py:461
  26.9 1.2 %collective-permute-done.4 = f32[2,2,8,16,128]{4,3,2,1,0:T(8,128)S(1)} collective-permute-done((f32[2,2,8,16,128]{4,3,2,1,0:T(8,128)S(1)}, f32[2,2,8,16,128]{4,3,2,1,0:T(8,128)S(1)}, u32[]{:S(2)}, u32[]{:S(2)}) %collective-permute-start.4) | collective-permute-done | bytes 262176 | tf_op jit(solution)/shard_map/ppermute | solution.py:453
  28.1 0.7 %shard_map.80 = (f32[8,64,128]{2,1,0:T(8,128)S(1)}, f32[2,8,16,128]{3,2,1,0:T(8,128)S(1)}) custom-call(s32[4]{0:T(128)S(1)} %pad_add_fusion.pos, f32[24,64,128]{2,1,0:T(8,128)S(1)} %get-tuple-element.29.states, f32[2,8,16,128]{3,2,1,0:T(8,128)S(1)} %get-tuple-element.45.mine, f32[2,8,16,128]{3,2,1,0:T(8,128)S(1)} %get-tuple-element.44.theirs), custom_call_target="tpu_custom_call" | custom-call | bytes 1048576 | tf_op jit(solution)/shard_map/pallas_call | solution.py:470
  28.8 1.8 %collective-permute-start.5 = (f32[2,8,16,128]{3,2,1,0:T(8,128)S(1)}, f32[2,8,16,128]{3,2,1,0:T(8,128)S(1)}, u32[]{:S(2)}, u32[]{:S(2)}) collective-permute-start(f32[2,8,16,128]{3,2,1,0:T(8,128)S(1)} %get-tuple-element.37), channel_id=1, source_target_pairs={{0,16},{16,0},{1,17},{17,1},{2,18},{18,2},{3,19},{19,3},{4,20},{20... | collective-permute-start | bytes 393224 | tf_op jit(solution)/shard_map/ppermute | solution.py:471
  30.6 2.3 %shard_map.81.adjoint = f32[2,8,16,128]{3,2,1,0:T(8,128)S(1)} custom-call(f32[24,64,128]{2,1,0:T(8,128)S(1)} %get-tuple-element.29.states, f32[8,64,128]{2,1,0:T(8,128)S(1)} %get-tuple-element.30.weight, f32[8,64,128]{2,1,0:T(8,128)S(1)} %get-tuple-element.31.south, f32[8,64,128]{2,1,0:T(8,128)S(1)} %get-tuple-element.32.north, ...), custom_call_target="tpu_custom_call" | custom-call | flops 10000000 | bytes 1048576 | tf_op jit(solution)/shard_map/pallas_call | solution.py:473
  32.9 0.9 %collective-permute-done.5.defect = f32[2,8,16,128]{3,2,1,0:T(8,128)S(1)} collective-permute-done((f32[2,8,16,128]{3,2,1,0:T(8,128)S(1)}, f32[2,8,16,128]{3,2,1,0:T(8,128)S(1)}, u32[]{:S(2)}, u32[]{:S(2)}) %collective-permute-start.5) | collective-permute-done | bytes 131104 | tf_op jit(solution)/shard_map/ppermute | solution.py:471
  33.8 0.6 %shard_map.82 = (f32[2,8,16,128]{3,2,1,0:T(8,128)S(1)}, f32[2,8,16,128]{3,2,1,0:T(8,128)S(1)}) custom-call(s32[4]{0:T(128)S(1)} %pad_add_fusion.pos, f32[2,8,16,128]{3,2,1,0:T(8,128)S(1)} %shard_map.81.adjoint, f32[2,8,16,128]{3,2,1,0:T(8,128)S(1)} %collective-permute-done.5.defect), custom_call_target="tpu_custom_call" | custom-call | bytes 1048576 | tf_op jit(solution)/shard_map/pallas_call | solution.py:477
  34.4 0.1 collective-permute-start.6
  34.5 1.3 %collective-permute-done.6.theirs = f32[2,8,16,128]{3,2,1,0:T(8,128)S(1)} collective-permute-done((f32[2,8,16,128]{3,2,1,0:T(8,128)S(1)}, f32[2,8,16,128]{3,2,1,0:T(8,128)S(1)}, u32[]{:S(2)}, u32[]{:S(2)}) %collective-permute-start.6) | collective-permute-done | bytes 131104 | tf_op jit(solution)/shard_map/ppermute | solution.py:478
  35.8 0.7 %shard_map.83 = (f32[2,128,128]{2,1,0:T(8,128)S(1)}, f32[2,128,128]{2,1,0:T(8,128)S(1)}) custom-call(s32[4]{0:T(128)S(1)} %pad_add_fusion.pos, f32[2,8,16,128]{3,2,1,0:T(8,128)S(1)} %get-tuple-element.38.mine, f32[2,8,16,128]{3,2,1,0:T(8,128)S(1)} %collective-permute-done.6.theirs), custom_call_target="tpu_custom_call" | custom-call | bytes 1048576 | tf_op jit(solution)/shard_map/pallas_call | solution.py:479
  36.5 1.8 %collective-permute-start.7 = (f32[2,128,128]{2,1,0:T(8,128)S(1)}, f32[2,128,128]{2,1,0:T(8,128)S(1)}, u32[]{:S(2)}, u32[]{:S(2)}) collective-permute-start(f32[2,128,128]{2,1,0:T(8,128)S(1)} %get-tuple-element.41), channel_id=1, source_target_pairs={{0,8},{4,12},{8,0},{12,4},{1,9},{5,13},{9,1},{13,5},{2,10},{6,14},... | collective-permute-start | bytes 393224 | tf_op jit(solution)/shard_map/ppermute | solution.py:480
  38.3 3.8 %collective-permute-done.7.theirs = f32[2,128,128]{2,1,0:T(8,128)S(1)} collective-permute-done((f32[2,128,128]{2,1,0:T(8,128)S(1)}, f32[2,128,128]{2,1,0:T(8,128)S(1)}, u32[]{:S(2)}, u32[]{:S(2)}) %collective-permute-start.7) | collective-permute-done | bytes 131104 | tf_op jit(solution)/shard_map/ppermute | solution.py:480
  42.1 1.3 %shard_map.84 = (f32[128,256]{1,0:T(8,128)}, f32[128,256]{1,0:T(8,128)}) custom-call(s32[4]{0:T(128)S(1)} %pad_add_fusion.pos, f32[2,128,128]{2,1,0:T(8,128)S(1)} %get-tuple-element.40.mine, f32[2,128,128]{2,1,0:T(8,128)S(1)} %collective-permute-done.7.theirs), custom_call_target="tpu_custom_call" | custom-call | bytes 1048576 | tf_op jit(solution)/shard_map/pallas_call | solution.py:481
  (9 shorter events, 0.1 us)
Async XLA Ops:
  0.6 0.7 %copy-start.3 = (s32[16,32]{1,0:T(8,128)S(1)}, s32[16,32]{1,0:T(8,128)}, u32[]{:S(2)}) copy-start(s32[16,32]{1,0:T(8,128)} %materials.1) | copy-start | bytes 6148
  0.7 0.7 %copy-start.5 = (f32[2]{0:T(128)S(1)}, f32[2]{0:T(128)}, u32[]{:S(2)}) copy-start(f32[2]{0:T(128)} %conductivity.1) | copy-start | bytes 28
  1.4 0.9 %copy-start = (f32[1,128,256]{2,1,0:T(8,128)S(1)}, f32[1,128,256]{2,1,0:T(8,128)}, u32[]{:S(2)}) copy-start(f32[1,128,256]{2,1,0:T(8,128)} %param.6) | copy-start | bytes 393220
  2.3 0.9 %copy-start.1 = (f32[1,128,256]{2,1,0:T(8,128)S(1)}, f32[1,128,256]{2,1,0:T(8,128)}, u32[]{:S(2)}) copy-start(f32[1,128,256]{2,1,0:T(8,128)} %param.7) | copy-start | bytes 393220
  3.2 0.9 %copy-start.2 = (f32[128,256]{1,0:T(8,128)S(1)}, f32[128,256]{1,0:T(8,128)}, u32[]{:S(2)}) copy-start(f32[128,256]{1,0:T(8,128)} %cond.1) | copy-start | bytes 393220
  5.1 11.3 %collective-permute-start = (f32[34,16,128]{2,1,0:T(8,128)S(1)}, f32[34,16,128]{2,1,0:T(8,128)S(1)}, u32[]{:S(2)}, u32[]{:S(2)}) collective-permute-start(f32[34,16,128]{2,1,0:T(8,128)S(1)} %get-tuple-element.24), channel_id=1, source_target_pairs={{0,8},{4,12},{8,0},{12,4},{1,9},{5,13},{9,1},{13,5},{2,10},{6,14},... | collective-permute-start | bytes 835592 | tf_op jit(solution)/shard_map/ppermute | solution.py:445
  8.1 8.2 %collective-permute-start.1 = (f32[9,16,128]{2,1,0:T(8,128)S(1)}, f32[9,16,128]{2,1,0:T(8,128)S(1)}, u32[]{:S(2)}, u32[]{:S(2)}) collective-permute-start(f32[9,16,128]{2,1,0:T(8,128)S(1)} %get-tuple-element.25), channel_id=1, source_target_pairs={{0,1},{1,2},{2,3},{3,11},{4,5},{5,6},{6,7},{7,15},{8,0},{9,8},{10,... | collective-permute-start | bytes 221192 | tf_op jit(solution)/shard_map/ppermute | solution.py:446
  9.7 6.7 %collective-permute-start.2 = (f32[9,16,128]{2,1,0:T(8,128)S(1)}, f32[9,16,128]{2,1,0:T(8,128)S(1)}, u32[]{:S(2)}, u32[]{:S(2)}) collective-permute-start(f32[9,16,128]{2,1,0:T(8,128)S(1)} %get-tuple-element.26), channel_id=1, source_target_pairs={{0,0},{1,8},{2,9},{3,10},{4,4},{5,12},{6,13},{7,14},{8,1},{9,2},{1... | collective-permute-start | bytes 221192 | tf_op jit(solution)/shard_map/ppermute | solution.py:447
  17.6 2.0 %collective-permute-start.3 = (f32[2,33,16,128]{3,2,1,0:T(8,128)S(1)}, f32[2,33,16,128]{3,2,1,0:T(8,128)S(1)}, u32[]{:S(2)}, u32[]{:S(2)}) collective-permute-start(f32[2,33,16,128]{3,2,1,0:T(8,128)S(1)} %get-tuple-element.28), channel_id=1, source_target_pairs={{0,4},{4,0},{8,12},{12,8},{1,5},{5,1},{9,13},{13,9},{2,6},{6,2},{1... | collective-permute-start | bytes 1622024 | tf_op jit(solution)/shard_map/ppermute | solution.py:450
  19.6 1.8 %copy-start.4 = (f32[2]{0:T(128)S(1)}, f32[2]{0:T(128)}, u32[]{:S(2)}) copy-start(f32[2]{0:T(128)} %sinks.1) | copy-start | bytes 28
  19.7 8.4 %collective-permute-start.4 = (f32[2,2,8,16,128]{4,3,2,1,0:T(8,128)S(1)}, f32[2,2,8,16,128]{4,3,2,1,0:T(8,128)S(1)}, u32[]{:S(2)}, u32[]{:S(2)}) collective-permute-start(f32[2,2,8,16,128]{4,3,2,1,0:T(8,128)S(1)} %pad_maximum_fusion), channel_id=1, source_target_pairs={{16,0},{0,16},{17,1},{1,17},{18,2},{2,18},{19,3},{3,19},{20,4},{4,... | collective-permute-start | bytes 786440 | tf_op jit(solution)/shard_map/ppermute | solution.py:453
  28.8 5.0 %collective-permute-start.5 = (f32[2,8,16,128]{3,2,1,0:T(8,128)S(1)}, f32[2,8,16,128]{3,2,1,0:T(8,128)S(1)}, u32[]{:S(2)}, u32[]{:S(2)}) collective-permute-start(f32[2,8,16,128]{3,2,1,0:T(8,128)S(1)} %get-tuple-element.37), channel_id=1, source_target_pairs={{0,16},{16,0},{1,17},{17,1},{2,18},{18,2},{3,19},{19,3},{4,20},{20... | collective-permute-start | bytes 393224 | tf_op jit(solution)/shard_map/ppermute | solution.py:471
  34.4 1.4 %collective-permute-start.6 = (f32[2,8,16,128]{3,2,1,0:T(8,128)S(1)}, f32[2,8,16,128]{3,2,1,0:T(8,128)S(1)}, u32[]{:S(2)}, u32[]{:S(2)}) collective-permute-start(f32[2,8,16,128]{3,2,1,0:T(8,128)S(1)} %get-tuple-element.39), channel_id=1, source_target_pairs={{0,4},{4,0},{8,12},{12,8},{1,5},{5,1},{9,13},{13,9},{2,6},{6,2},{1... | collective-permute-start | bytes 393224 | tf_op jit(solution)/shard_map/ppermute | solution.py:478
  36.5 5.6 %collective-permute-start.7 = (f32[2,128,128]{2,1,0:T(8,128)S(1)}, f32[2,128,128]{2,1,0:T(8,128)S(1)}, u32[]{:S(2)}, u32[]{:S(2)}) collective-permute-start(f32[2,128,128]{2,1,0:T(8,128)S(1)} %get-tuple-element.41), channel_id=1, source_target_pairs={{0,8},{4,12},{8,0},{12,4},{1,9},{5,13},{9,1},{13,5},{2,10},{6,14},... | collective-permute-start | bytes 393224 | tf_op jit(solution)/shard_map/ppermute | solution.py:480

commit v2 on v1

--- a/solution.py
+++ b/solution.py
@@ -21,6 +21,7 @@
 
 VMEM = pl.BlockSpec(memory_space=pltpu.VMEM)
 SMEM = pl.BlockSpec(memory_space=pltpu.SMEM)
+HBM = pl.BlockSpec(memory_space=pltpu.HBM)
 F32 = jnp.float32
 
 
@@ -53,13 +54,22 @@
     return jnp.where(at < 32, roll(s, 32), jnp.where(at < 64, roll(f, 64), jnp.where(at < 96, roll(k, 96), far)))
 
 
-def pack_kernel(pos, conductivity, start, source, cond, materials, own, flip, along, across, split):
+def pack_kernel(pos, scales, start, source, cond, elements, own, flip, along, across, home, conductivity, materials, split, done):
     y = pos[0]
+    copies = [pltpu.make_async_copy(scales, conductivity, done.at[7]), pltpu.make_async_copy(elements, materials, done.at[0])]
+    for a, ref in enumerate((start, source, cond)):
+        for half in range(2):
+            part = ref.at[:, pl.ds(half * LANES, LANES)]
+            copies.append(pltpu.make_async_copy(part, split.at[2 * a + half], done.at[1 + 2 * a + half]))
+    for copy in copies:
+        copy.start()
     count, cells = materials.shape
     width = start.shape[1]
     column = lax.broadcasted_iota(jnp.int32, (cells, width), 1)
     cell = lax.broadcasted_iota(jnp.int32, (cells, width), 0)
     spread = jnp.where(column // BLOCK == cell, 1.0, 0.0).astype(F32)
+    copies[0].wait()
+    copies[1].wait()
     material = jnp.dot(materials[...].astype(F32), spread, preferred_element_type=F32)
     is_gob = material > 0.5
     factor = jnp.where(is_gob, conductivity[1], conductivity[0])
@@ -77,9 +87,10 @@
         along[p] = pick(lower, last1, first0)
         across[p] = pick(lower, first0, last1)
 
-    for a, ref in enumerate((start, source, cond)):
-        split[2 * a] = ref[:, :LANES]
-        split[2 * a + 1] = ref[:, LANES:]
+    for copy in copies[2:]:
+        copy.wait()
+    home[0] = split[0]
+    home[1] = split[1]
     for p in range(BLOCK):
         rows = pl.ds(p, count, stride=BLOCK)
         s0, s1, f0, f1, k0, k1 = (split[a, rows, :] for a in range(6))
@@ -206,7 +217,7 @@
     return lambda first, p, z: put_padded(ref, p, first, z)
 
 
-def forward_kernel(pos, sinks, mine, theirs, states, south, north, east, west, base, sink, level, forcing, kappa, edge, previous, old, new, *scaled):
+def forward_kernel(pos, sinks, mine, theirs, states, ends, south, north, east, west, base, sink, level, forcing, kappa, edge, previous, old, new, *scaled):
     y, c, strip, strips = pos[0], pos[1], pos[2], pos[3]
     lines = base.shape[1]
     count = mine.shape[2]
@@ -302,14 +313,30 @@
         return carry
 
     lax.fori_loop(0, STEPS, step, 0)
-
-
-def adjoint_kernel(states, weight, south, north, east, west, base, sink, out, old, new, given, *scaled):
+    pack_strip(lambda p, first: level[p, pl.ds(BLOCK + first, count), :], ends)
+
+
+def pack_strip(read, out):
+    count = out.shape[2]
+    at = lax.broadcasted_iota(jnp.int32, (count, LANES), 1)
+    for core in range(2):
+        for p in range(BLOCK):
+            low, high = read(p, core * count), read(p, (2 + core) * count)
+            out[core, p] = jnp.where(at < STRIP, roll(low, -HALO), roll(high, HALO))
+
+
+def adjoint_kernel(pos, states, mine, theirs, south, north, east, west, base, sink, out, old, new, given, *scaled):
+    y, c = pos[0], pos[1]
     lines = base.shape[1]
+    count = mine.shape[2]
     for ref in (old, new):
         clear_ends(ref, lines)
-    for p in range(BLOCK):
-        given[p] = weight[p]
+    for ref, core in ((mine, c), (theirs, 1 - c)):
+        for slot in range(2):
+            chip = y if slot == 0 else 1 - y
+            at = pl.ds(pl.multiple_of((2 * chip + core) * count, BLOCK), count)
+            for p in range(BLOCK):
+                given[p, at, :] = states[(STEPS - 1) * BLOCK + p, at, :] - ref[slot, p]
 
     def step(number, carry):
         level = STEPS - 1 - number
@@ -335,65 +362,39 @@
         return carry
 
     lax.fori_loop(0, STEPS, step, 0)
-    count = out.shape[2]
+    pack_strip(lambda p, first: given[p, pl.ds(first, count), :], out)
+
+
+def send_kernel(pos, adjoint, previous, keep, core, flip, both):
+    y, c = pos[0], pos[1]
+    count = adjoint.shape[2]
     at = lax.broadcasted_iota(jnp.int32, (count, LANES), 1)
-    for core in range(2):
-        for p in range(BLOCK):
-            low = given[p, pl.ds(core * count, count), :]
-            high = given[p, pl.ds((2 + core) * count, count), :]
-            out[core, p] = jnp.where(at < STRIP, roll(low, -HALO), roll(high, HALO))
-
-
-def defect_kernel(pos, states, mine, theirs, weight, out):
+    for p in range(BLOCK):
+        rows = pl.ds(p, count, stride=BLOCK)
+        for owner, (same, other) in ((c, (keep, flip)), (1 - c, (core, both))):
+            a, e = adjoint[owner, p], previous[owner, p]
+            chip0 = jnp.where(at < STRIP, a, roll(e, STRIP))
+            chip1 = jnp.where(at < STRIP, roll(a, STRIP), e)
+            same[rows, :] = pick(y == 0, chip0, chip1)
+            other[rows, :] = pick(y == 0, chip1, chip0)
+
+
+def join_kernel(pos, home, keep, core, flip, both, defect, gradient, built, done):
     y, c = pos[0], pos[1]
-    count = mine.shape[2]
-    at = lax.broadcasted_iota(jnp.int32, (count, LANES), 1)
-    for ref, core in ((mine, c), (theirs, 1 - c)):
-        for p in range(BLOCK):
-            ends = []
-            for slot in range(2):
-                chip = y if slot == 0 else 1 - y
-                first = pl.multiple_of((2 * chip + core) * count, BLOCK)
-                value = states[(STEPS - 1) * BLOCK + p, pl.ds(first, count), :] - ref[slot, p]
-                weight[p, pl.ds(first, count), :] = value
-                ends.append(value)
-            low, high = pick(y == 0, ends[0], ends[1]), pick(y == 0, ends[1], ends[0])
-            out[core, p] = jnp.where(at < STRIP, roll(low, -HALO), roll(high, HALO))
-
-
-def swap_kernel(pos, adjoint, defect, keep, send):
-    c = pos[1]
-    for p in range(BLOCK):
-        for a in range(2):
-            other = defect[1 - c, p]
-            held = defect[c, p]
-            if a == 0:
-                other = adjoint[1 - c, p] - other
-                held = adjoint[c, p] - held
-            keep[a, p] = held
-            send[a, p] = other
-
-
-def tile_kernel(pos, mine, theirs, keep, send):
-    y, c = pos[0], pos[1]
-    count = mine.shape[2]
-    at = lax.broadcasted_iota(jnp.int32, (count, LANES), 1)
-    for a in range(2):
-        for p in range(BLOCK):
-            even = pick(c == 0, mine[a, p], theirs[a, p])
-            odd = pick(c == 0, theirs[a, p], mine[a, p])
-            chip0 = jnp.where(at < STRIP, even, roll(odd, STRIP))
-            chip1 = jnp.where(at < STRIP, roll(even, STRIP), odd)
-            rows = pl.ds(p, count, stride=BLOCK)
-            keep[a, rows, :] = pick(y == 0, chip0, chip1)
-            send[a, rows, :] = pick(y == 0, chip1, chip0)
-
-
-def join_kernel(pos, mine, theirs, gradient, defect):
-    lower = pos[0] == 0
-    for a, ref in enumerate((gradient, defect)):
-        ref[:, :LANES] = pick(lower, mine[a], theirs[a])
-        ref[:, LANES:] = pick(lower, theirs[a], mine[a])
+    at = lax.broadcasted_iota(jnp.int32, keep.shape, 1)
+    copies = []
+    for chip in range(2):
+        here = y == chip
+        one, two = pick(here, keep[...], flip[...]), pick(here, core[...], both[...])
+        even, odd = pick(c == 0, one, two), pick(c == 0, two, one)
+        missed = jnp.where(at < STRIP, roll(even, STRIP), odd) - home[chip]
+        built[0, chip] = missed
+        built[1, chip] = jnp.where(at < STRIP, even, roll(odd, STRIP)) - missed
+        for a, out in enumerate((defect, gradient)):
+            copies.append(pltpu.make_async_copy(built.at[a, chip], out.at[:, pl.ds(chip * LANES, LANES)], done.at[a, chip]))
+            copies[-1].start()
+    for copy in copies:
+        copy.wait()
 
 
 def per_device(slabs, strips_y, start_states, source, cond_field, materials, conductivity, sink_rate):
@@ -408,10 +409,11 @@
     shape = lambda *dims: jax.ShapeDtypeStruct(dims, F32)
     params = pltpu.CompilerParams(vmem_limit_bytes=48 * 1024 * 1024)
 
-    def call(body, outs, ins, scratch=(), flops=0):
-        specs = [SMEM if s else VMEM for s in ins]
+    def call(body, outs, ins, scratch=(), flops=0, out_specs=None):
+        specs = [{"s": SMEM, "v": VMEM, "h": HBM}[kind] for kind in ins]
         cost = pl.CostEstimate(flops=flops, bytes_accessed=1 << 20, transcendentals=0)
-        return pl.pallas_call(body, out_shape=outs, in_specs=specs, out_specs=[VMEM] * len(outs), scratch_shapes=list(scratch), compiler_params=params, cost_estimate=cost)
+        out_specs = out_specs or [VMEM] * len(outs)
+        return pl.pallas_call(body, out_shape=outs, in_specs=specs, out_specs=out_specs, scratch_shapes=list(scratch), compiler_params=params, cost_estimate=cost)
 
     def joint(y_, c_, z_):
         return (2 * y_ + c_) * strips_y + z_
@@ -436,17 +438,19 @@
     forth = [(i, (i + 1) % slabs) for i in range(slabs)]
     back = [(b, a) for a, b in forth]
 
-    own, flip, along, across = call(
+    diagonal_pairs = [(0, 3), (1, 2), (2, 1), (3, 0)]
+
+    own, flip, along, across, home = call(
         pack_kernel,
-        [shape(TILE + HALF, count, LANES)] * 2 + [shape(HALF, count, LANES)] * 2,
-        (1, 1, 0, 0, 0, 0),
-        [pltpu.VMEM((6, rows, LANES), F32)],
-    )(pos, conductivity, start, forcing, cond_field, materials)
+        [shape(TILE + HALF, count, LANES)] * 2 + [shape(HALF, count, LANES)] * 2 + [shape(2, rows, LANES)],
+        "shhhhh",
+        [pltpu.SMEM((2,), F32), pltpu.VMEM(materials.shape, jnp.int32), pltpu.VMEM((6, rows, LANES), F32), pltpu.SemaphoreType.DMA((8,))],
+    )(pos, *(pltpu.with_memory_space_constraint(x, pltpu.HBM) for x in (conductivity, start, forcing, cond_field, materials)))
     other = lax.ppermute(flip, "sx", flip_pairs)
     along = lax.ppermute(along, ("sx", "sy"), along_pairs)
     across = lax.ppermute(across, ("sx", "sy"), across_pairs)
 
-    mine, send = call(window_kernel, [shape(2, WIDE, count, LANES)] * 2, (1, 0, 0, 0, 0))(pos, own, other, along, across)
+    mine, send = call(window_kernel, [shape(2, WIDE, count, LANES)] * 2, "svvvv")(pos, own, other, along, across)
     theirs = lax.ppermute(send, "sx", core_pairs)
 
     starts = jnp.stack([mine[:, :BLOCK], theirs[:, :BLOCK]])
@@ -454,31 +458,34 @@
 
     whole = shape(BLOCK, lines, LANES)
     flat = shape(lines, LANES)
+    strip = shape(2, BLOCK, count, LANES)
     buffer = pltpu.VMEM((BLOCK, lines + 2 * BLOCK, LANES), F32)
     plain = pltpu.VMEM((BLOCK, lines, LANES), F32)
-    ends = pltpu.VMEM((2, lines, LANES), F32)
-    scaled = [plain] * 5 + [ends]
-    states, south, north, east, west, base, sink = call(
+    scaled = [plain] * 5 + [pltpu.VMEM((2, lines, LANES), F32)]
+    states, ends, south, north, east, west, base, sink = call(
         forward_kernel,
-        [shape(STEPS * BLOCK, lines, LANES), whole, whole, whole, flat, whole, flat],
-        (1, 1, 0, 0),
+        [shape(STEPS * BLOCK, lines, LANES), strip, whole, whole, whole, flat, whole, flat],
+        "ssvv",
         [buffer, plain, buffer, plain, plain, buffer, buffer] + scaled,
         flops=20_000_000,
     )(pos, sink_rate, mine, theirs)
-
-    pair = shape(2, BLOCK, count, LANES)
-    weight, ends_here = call(defect_kernel, [whole, pair], (1, 0, 0, 0))(pos, states, next_starts[0], next_starts[1])
-    defect = lax.ppermute(ends_here, "slab", forth)
-
-    (adjoint,) = call(adjoint_kernel, [pair], (0,) * 8, [buffer, buffer, plain] + scaled, flops=10_000_000)(
-        states, weight, south, north, east, west, base, sink
+    previous = lax.ppermute(ends, "slab", forth)
+
+    (adjoint,) = call(adjoint_kernel, [strip], "s" + "v" * 9, [buffer, buffer, plain] + scaled, flops=10_000_000)(
+        pos, states, next_starts[0], next_starts[1], south, north, east, west, base, sink
     )
 
-    keep, send = call(swap_kernel, [pair] * 2, (1, 0, 0))(pos, adjoint, defect)
-    got = lax.ppermute(send, "sx", core_pairs)
-    keep, send = call(tile_kernel, [shape(2, rows, LANES)] * 2, (1, 0, 0))(pos, keep, got)
-    got = lax.ppermute(send, "sx", flip_pairs)
-    gradient, defect = call(join_kernel, [shape(rows, 2 * LANES)] * 2, (1, 0, 0))(pos, keep, got)
+    keep, core, flip, both = call(send_kernel, [shape(rows, LANES)] * 4, "svv")(pos, adjoint, previous)
+    flip = lax.ppermute(flip, "sx", flip_pairs)
+    both = lax.ppermute(both, "sx", diagonal_pairs)
+    core = lax.ppermute(core, "sx", core_pairs)
+    defect, gradient = call(
+        join_kernel,
+        [shape(rows, 2 * LANES)] * 2,
+        "svvvvv",
+        [pltpu.VMEM((2, 2, rows, LANES), F32), pltpu.SemaphoreType.DMA((2, 2))],
+        out_specs=[HBM] * 2,
+    )(pos, home, keep, core, flip, both)
     return (defect[None], gradient[None])
 
 

time: 43.6 us -> 38.2 us (0.88)
  local copies, waits for them, and re-layouts: 3.41 us -> 0.04 us
  waiting for transfers between devices: 15.2 us -> 13.4 us
  starting transfers between devices: 10.8 us -> 9.66 us
  Pallas kernels: 13.1 us -> 14 us
    unnamed x12 -> x2, local copies, waits for them, and re-layouts: 3.38 us -> 0.01 us
    ppermute x3 -> x4, starting transfers between devices: 3.64 us -> 2.55 us  [the longest x1 1.57 us: per_device(): flip = lax.ppermute(flip, 'sx', flip_pairs)]
    pallas_call x1, Pallas kernels: 0.97 us -> 2.01 us  [per_device(): call(pack_kernel, [shape(TILE + HALF, count, LANES)] * 2 + [shape(HALF, c...]
    ppermute x1, waiting for transfers between devices: 1.21 us -> 0.21 us  [per_device(): next_starts = lax.ppermute(starts, 'slab', back)]
    ppermute x3 -> x4, waiting for transfers between devices: 6.08 us -> 5.3 us  [the longest x1 2.64 us: per_device(): flip = lax.ppermute(flip, 'sx', flip_pairs)]
    pallas_call x7 -> x5, Pallas kernels: 12.1 us -> 12 us  [the longest x1 5.79 us: per_device(): call(forward_kernel, [shape(STEPS * BLOCK, lines, LANES), strip, whole, w...]
  transfers between devices with their start and end apart: 8 -> 9, of which waited for: 6 -> 6; matrix products, arithmetic and copies ran while one was open for 0% -> 0% of each run, Pallas kernels for 18% -> 23%
where the time goes in v2:
time: 38.2 us; the launch traced here: 38 us
  Pallas kernels  14 us (37%)
  waiting for transfers between devices  13.4 us (35%)
  starting transfers between devices  9.66 us (25%)
  between operations  0.74 us (2%)
    ppermute x1, waiting for transfers between devices, per_device(): along = lax.ppermute(along, ('sx', 'sy'), along_pairs)  6 us
    pallas_call x1, Pallas kernels, per_device(): call(forward_kernel, [shape(STEPS * BLOCK, lines, LANES), strip, whole, w...  5.79 us
    ppermute x1, starting transfers between devices, per_device(): other = lax.ppermute(flip, 'sx', flip_pairs)  3.03 us
    pallas_call x1, Pallas kernels, per_device(): call(adjoint_kernel, [strip], 's' + 'v' * 9, [buffer, buffer, plain] + sc...  2.93 us
    ppermute x1, waiting for transfers between devices, per_device(): flip = lax.ppermute(flip, 'sx', flip_pairs)  2.64 us
    pallas_call x1, Pallas kernels, per_device(): call(pack_kernel, [shape(TILE + HALF, count, LANES)] * 2 + [shape(HALF, c...  2.01 us
    ppermute x1, waiting for transfers between devices, per_device(): theirs = lax.ppermute(send, 'sx', core_pairs)  1.9 us
    ppermute x1, starting transfers between devices, per_device(): next_starts = lax.ppermute(starts, 'slab', back)  1.78 us
  transfers between devices with their start and end apart: 9, of which 6 were waited for; matrix products, arithmetic and copies ran while one was open for 0% of the time, Pallas kernels for 23%

profile of v2, /device:TPU:0, one launch (start us, length us, event | category | flops | bytes accessed | tf_op | source)
XLA Modules:
  0.0 38.0 jit_solution(12163787643788765392)
XLA Ops:
  0.6 0.1 pad_add_fusion.pos
  0.7 2.0 %shard_map.77 = (f32[34,16,128]{2,1,0:T(8,128)S(1)}, f32[34,16,128]{2,1,0:T(8,128)S(1)}, f32[9,16,128]{2,1,0:T(8,128)S(1)}, f32[9,16,128]{2,1,0:T(8,128)S(1)}, f32[2,128,128]{2,1,0:T(8,128)S(1)}) custom-call(s32[4]{0:T(128)S(1)} %pad_add_fusion.pos, f32[2]{0:T(128)} %scales.1, f32[128,256]{1,0:T(8,128)} %bitcast.15, f32[128,256]{1,0:T(8,128)} %bitcast.16, ...), custom_call_target="tpu_custom_call" | custom-call | bytes 1048576 | tf_op jit(solution)/shard_map/pallas_call | solution.py:443
  2.7 3.0 %collective-permute-start = (f32[34,16,128]{2,1,0:T(8,128)S(1)}, f32[34,16,128]{2,1,0:T(8,128)S(1)}, u32[]{:S(2)}, u32[]{:S(2)}) collective-permute-start(f32[34,16,128]{2,1,0:T(8,128)S(1)} %get-tuple-element.25), channel_id=1, source_target_pairs={{0,8},{4,12},{8,0},{12,4},{1,9},{5,13},{9,1},{13,5},{2,10},{6,14},... | collective-permute-start | bytes 835592 | tf_op jit(solution)/shard_map/ppermute | solution.py:449
  5.8 1.6 %collective-permute-start.1 = (f32[9,16,128]{2,1,0:T(8,128)S(1)}, f32[9,16,128]{2,1,0:T(8,128)S(1)}, u32[]{:S(2)}, u32[]{:S(2)}) collective-permute-start(f32[9,16,128]{2,1,0:T(8,128)S(1)} %get-tuple-element.26), channel_id=1, source_target_pairs={{0,1},{1,2},{2,3},{3,11},{4,5},{5,6},{6,7},{7,15},{8,0},{9,8},{10,... | collective-permute-start | bytes 221192 | tf_op jit(solution)/shard_map/ppermute | solution.py:450
  7.4 0.7 %collective-permute-start.2 = (f32[9,16,128]{2,1,0:T(8,128)S(1)}, f32[9,16,128]{2,1,0:T(8,128)S(1)}, u32[]{:S(2)}, u32[]{:S(2)}) collective-permute-start(f32[9,16,128]{2,1,0:T(8,128)S(1)} %get-tuple-element.27), channel_id=1, source_target_pairs={{0,0},{1,8},{2,9},{3,10},{4,4},{5,12},{6,13},{7,14},{8,1},{9,2},{1... | collective-permute-start | bytes 221192 | tf_op jit(solution)/shard_map/ppermute | solution.py:451
  8.0 6.0 %collective-permute-done.1.along = f32[9,16,128]{2,1,0:T(8,128)S(1)} collective-permute-done((f32[9,16,128]{2,1,0:T(8,128)S(1)}, f32[9,16,128]{2,1,0:T(8,128)S(1)}, u32[]{:S(2)}, u32[]{:S(2)}) %collective-permute-start.1) | collective-permute-done | bytes 73760 | tf_op jit(solution)/shard_map/ppermute | solution.py:450
  14.0 0.0 collective-permute-done.2.across
  14.0 0.0 collective-permute-done.other
  14.0 1.2 %shard_map.78 = (f32[2,33,16,128]{3,2,1,0:T(8,128)S(1)}, f32[2,33,16,128]{3,2,1,0:T(8,128)S(1)}) custom-call(s32[4]{0:T(128)S(1)} %pad_add_fusion.pos, f32[34,16,128]{2,1,0:T(8,128)S(1)} %get-tuple-element.24.own, f32[34,16,128]{2,1,0:T(8,128)S(1)} %collective-permute-done.other, f32[9,16,128]{2,1,0:T(8,128)S(1)} %collective-permute-done.1.along, ...), custom_call_target="tpu_custom_call" | custom-call | bytes 1048576 | tf_op jit(solution)/shard_map/pallas_call | solution.py:453
  15.3 0.1 collective-permute-start.3
  15.4 1.9 %collective-permute-done.3.theirs = f32[2,33,16,128]{3,2,1,0:T(8,128)S(1)} collective-permute-done((f32[2,33,16,128]{3,2,1,0:T(8,128)S(1)}, f32[2,33,16,128]{3,2,1,0:T(8,128)S(1)}, u32[]{:S(2)}, u32[]{:S(2)}) %collective-permute-start.3) | collective-permute-done | bytes 540704 | tf_op jit(solution)/shard_map/ppermute | solution.py:454
  17.3 0.0 copy-start
  17.3 1.8 %collective-permute-start.4 = (f32[2,2,8,16,128]{4,3,2,1,0:T(8,128)S(1)}, f32[2,2,8,16,128]{4,3,2,1,0:T(8,128)S(1)}, u32[]{:S(2)}, u32[]{:S(2)}) collective-permute-start(f32[2,2,8,16,128]{4,3,2,1,0:T(8,128)S(1)} %pad_maximum_fusion), channel_id=1, source_target_pairs={{16,0},{0,16},{17,1},{1,17},{18,2},{2,18},{19,3},{3,19},{20,4},{4,... | collective-permute-start | bytes 786440 | tf_op jit(solution)/shard_map/ppermute | solution.py:457
  19.1 0.0 copy-done
  19.1 5.8 %shard_map.79 = (f32[24,64,128]{2,1,0:T(8,128)S(1)}, f32[2,8,16,128]{3,2,1,0:T(8,128)S(1)}, f32[8,64,128]{2,1,0:T(8,128)S(1)}, f32[8,64,128]{2,1,0:T(8,128)S(1)}...) custom-call(s32[4]{0:T(128)S(1)} %pad_add_fusion.pos, ...), custom_call_target="tpu_custom_call" | custom-call | flops 20000000 | bytes 1048576 | tf_op jit(solution)/shard_map/pallas_call | solution.py:465
  24.9 0.6 %collective-permute-start.5 = (f32[2,8,16,128]{3,2,1,0:T(8,128)S(1)}, f32[2,8,16,128]{3,2,1,0:T(8,128)S(1)}, u32[]{:S(2)}, u32[]{:S(2)}) collective-permute-start(f32[2,8,16,128]{3,2,1,0:T(8,128)S(1)} %get-tuple-element.37), channel_id=1, source_target_pairs={{0,16},{16,0},{1,17},{17,1},{2,18},{18,2},{3,19},{19,3},{4,20},{20... | collective-permute-start | bytes 393224 | tf_op jit(solution)/shard_map/ppermute | solution.py:472
  25.5 0.2 collective-permute-done.4
  25.7 2.9 %shard_map.80.adjoint = f32[2,8,16,128]{3,2,1,0:T(8,128)S(1)} custom-call(s32[4]{0:T(128)S(1)} %pad_add_fusion.pos, f32[24,64,128]{2,1,0:T(8,128)S(1)} %get-tuple-element.30.states, f32[2,8,16,128]{3,2,1,0:T(8,128)S(1)} %get-tuple-element.45.mine, f32[2,8,16,128]{3,2,1,0:T(8,128)S(1)} %get-tuple-element.44.theirs, ...), custom_call_target="tpu_custom_call" | custom-call | flops 10000000 | bytes 1048576 | tf_op jit(solution)/shard_map/pallas_call | solution.py:474
  28.7 1.5 %collective-permute-done.5.previous = f32[2,8,16,128]{3,2,1,0:T(8,128)S(1)} collective-permute-done((f32[2,8,16,128]{3,2,1,0:T(8,128)S(1)}, f32[2,8,16,128]{3,2,1,0:T(8,128)S(1)}, u32[]{:S(2)}, u32[]{:S(2)}) %collective-permute-start.5) | collective-permute-done | bytes 131104 | tf_op jit(solution)/shard_map/ppermute | solution.py:472
  30.2 0.7 %shard_map.81 = (f32[128,128]{1,0:T(8,128)S(1)}, f32[128,128]{1,0:T(8,128)S(1)}, f32[128,128]{1,0:T(8,128)S(1)}, f32[128,128]{1,0:T(8,128)S(1)}) custom-call(s32[4]{0:T(128)S(1)} %pad_add_fusion.pos, f32[2,8,16,128]{3,2,1,0:T(8,128)S(1)} %shard_map.80.adjoint, f32[2,8,16,128]{3,2,1,0:T(8,128)S(1)} %collective-permute-done.5.previous), custom_call_target="tpu_custom_call" | custom-call | bytes 1048576 | tf_op jit(solution)/shard_map/pallas_call | solution.py:478
  30.9 0.1 collective-permute-start.6
  31.0 1.6 %collective-permute-start.7 = (f32[128,128]{1,0:T(8,128)S(1)}, f32[128,128]{1,0:T(8,128)S(1)}, u32[]{:S(2)}, u32[]{:S(2)}) collective-permute-start(f32[128,128]{1,0:T(8,128)S(1)} %get-tuple-element.40), channel_id=1, source_target_pairs={{0,8},{4,12},{8,0},{12,4},{1,9},{5,13},{9,1},{13,5},{2,10},{6,14},... | collective-permute-start | bytes 196616 | tf_op jit(solution)/shard_map/ppermute | solution.py:479
  32.6 0.3 collective-permute-start.8
  32.8 0.0 collective-permute-done.6.core
  32.8 2.6 %collective-permute-done.7.flip = f32[128,128]{1,0:T(8,128)S(1)} collective-permute-done((f32[128,128]{1,0:T(8,128)S(1)}, f32[128,128]{1,0:T(8,128)S(1)}, u32[]{:S(2)}, u32[]{:S(2)}) %collective-permute-start.7) | collective-permute-done | bytes 65568 | tf_op jit(solution)/shard_map/ppermute | solution.py:479
  35.5 1.1 %collective-permute-done.8.both = f32[128,128]{1,0:T(8,128)S(1)} collective-permute-done((f32[128,128]{1,0:T(8,128)S(1)}, f32[128,128]{1,0:T(8,128)S(1)}, u32[]{:S(2)}, u32[]{:S(2)}) %collective-permute-start.8) | collective-permute-done | bytes 65568 | tf_op jit(solution)/shard_map/ppermute | solution.py:480
  36.6 1.4 %shard_map.82 = (f32[128,256]{1,0:T(8,128)}, f32[128,256]{1,0:T(8,128)}) custom-call(s32[4]{0:T(128)S(1)} %pad_add_fusion.pos, f32[2,128,128]{2,1,0:T(8,128)S(1)} %get-tuple-element.23.home, f32[128,128]{1,0:T(8,128)S(1)} %get-tuple-element.38.keep, f32[128,128]{1,0:T(8,128)S(1)} %collective-permute-done.6.core, f32[128,128]{1,0:T(8,128)S(1)} %collective-permute-done.7.flip, ...), custom_call_target="tpu_custom_call" | custom-call | bytes 1048576 | tf_op jit(solution)/shard_map/pallas_call | solution.py:482
  (4 shorter events, 0.1 us)
Async XLA Ops:
  2.7 11.3 %collective-permute-start = (f32[34,16,128]{2,1,0:T(8,128)S(1)}, f32[34,16,128]{2,1,0:T(8,128)S(1)}, u32[]{:S(2)}, u32[]{:S(2)}) collective-permute-start(f32[34,16,128]{2,1,0:T(8,128)S(1)} %get-tuple-element.25), channel_id=1, source_target_pairs={{0,8},{4,12},{8,0},{12,4},{1,9},{5,13},{9,1},{13,5},{2,10},{6,14},... | collective-permute-start | bytes 835592 | tf_op jit(solution)/shard_map/ppermute | solution.py:449
  5.8 8.2 %collective-permute-start.1 = (f32[9,16,128]{2,1,0:T(8,128)S(1)}, f32[9,16,128]{2,1,0:T(8,128)S(1)}, u32[]{:S(2)}, u32[]{:S(2)}) collective-permute-start(f32[9,16,128]{2,1,0:T(8,128)S(1)} %get-tuple-element.26), channel_id=1, source_target_pairs={{0,1},{1,2},{2,3},{3,11},{4,5},{5,6},{6,7},{7,15},{8,0},{9,8},{10,... | collective-permute-start | bytes 221192 | tf_op jit(solution)/shard_map/ppermute | solution.py:450
  7.4 6.7 %collective-permute-start.2 = (f32[9,16,128]{2,1,0:T(8,128)S(1)}, f32[9,16,128]{2,1,0:T(8,128)S(1)}, u32[]{:S(2)}, u32[]{:S(2)}) collective-permute-start(f32[9,16,128]{2,1,0:T(8,128)S(1)} %get-tuple-element.27), channel_id=1, source_target_pairs={{0,0},{1,8},{2,9},{3,10},{4,4},{5,12},{6,13},{7,14},{8,1},{9,2},{1... | collective-permute-start | bytes 221192 | tf_op jit(solution)/shard_map/ppermute | solution.py:451
  15.3 2.0 %collective-permute-start.3 = (f32[2,33,16,128]{3,2,1,0:T(8,128)S(1)}, f32[2,33,16,128]{3,2,1,0:T(8,128)S(1)}, u32[]{:S(2)}, u32[]{:S(2)}) collective-permute-start(f32[2,33,16,128]{3,2,1,0:T(8,128)S(1)} %get-tuple-element.29), channel_id=1, source_target_pairs={{0,4},{4,0},{8,12},{12,8},{1,5},{5,1},{9,13},{13,9},{2,6},{6,2},{1... | collective-permute-start | bytes 1622024 | tf_op jit(solution)/shard_map/ppermute | solution.py:454
  17.3 1.8 %copy-start = (f32[2]{0:T(128)S(1)}, f32[2]{0:T(128)}, u32[]{:S(2)}) copy-start(f32[2]{0:T(128)} %sinks.1) | copy-start | bytes 28
  17.3 8.4 %collective-permute-start.4 = (f32[2,2,8,16,128]{4,3,2,1,0:T(8,128)S(1)}, f32[2,2,8,16,128]{4,3,2,1,0:T(8,128)S(1)}, u32[]{:S(2)}, u32[]{:S(2)}) collective-permute-start(f32[2,2,8,16,128]{4,3,2,1,0:T(8,128)S(1)} %pad_maximum_fusion), channel_id=1, source_target_pairs={{16,0},{0,16},{17,1},{1,17},{18,2},{2,18},{19,3},{3,19},{20,4},{4,... | collective-permute-start | bytes 786440 | tf_op jit(solution)/shard_map/ppermute | solution.py:457
  24.9 5.3 %collective-permute-start.5 = (f32[2,8,16,128]{3,2,1,0:T(8,128)S(1)}, f32[2,8,16,128]{3,2,1,0:T(8,128)S(1)}, u32[]{:S(2)}, u32[]{:S(2)}) collective-permute-start(f32[2,8,16,128]{3,2,1,0:T(8,128)S(1)} %get-tuple-element.37), channel_id=1, source_target_pairs={{0,16},{16,0},{1,17},{17,1},{2,18},{18,2},{3,19},{19,3},{4,20},{20... | collective-permute-start | bytes 393224 | tf_op jit(solution)/shard_map/ppermute | solution.py:472
  30.9 1.9 %collective-permute-start.6 = (f32[128,128]{1,0:T(8,128)S(1)}, f32[128,128]{1,0:T(8,128)S(1)}, u32[]{:S(2)}, u32[]{:S(2)}) collective-permute-start(f32[128,128]{1,0:T(8,128)S(1)} %get-tuple-element.39), channel_id=1, source_target_pairs={{0,4},{4,0},{8,12},{12,8},{1,5},{5,1},{9,13},{13,9},{2,6},{6,2},{1... | collective-permute-start | bytes 196616 | tf_op jit(solution)/shard_map/ppermute | solution.py:481
  31.0 4.5 %collective-permute-start.7 = (f32[128,128]{1,0:T(8,128)S(1)}, f32[128,128]{1,0:T(8,128)S(1)}, u32[]{:S(2)}, u32[]{:S(2)}) collective-permute-start(f32[128,128]{1,0:T(8,128)S(1)} %get-tuple-element.40), channel_id=1, source_target_pairs={{0,8},{4,12},{8,0},{12,4},{1,9},{5,13},{9,1},{13,5},{2,10},{6,14},... | collective-permute-start | bytes 196616 | tf_op jit(solution)/shard_map/ppermute | solution.py:479
  32.6 4.0 %collective-permute-start.8 = (f32[128,128]{1,0:T(8,128)S(1)}, f32[128,128]{1,0:T(8,128)S(1)}, u32[]{:S(2)}, u32[]{:S(2)}) collective-permute-start(f32[128,128]{1,0:T(8,128)S(1)} %get-tuple-element.41), channel_id=1, source_target_pairs={{0,12},{4,8},{8,4},{12,0},{1,13},{5,9},{9,5},{13,1},{2,14},{6,10},... | collective-permute-start | bytes 196616 | tf_op jit(solution)/shard_map/ppermute | solution.py:480

commit v3 on v2

--- a/solution.py
+++ b/solution.py
@@ -33,6 +33,11 @@
     return lax.broadcasted_iota(jnp.int32, x.shape, x.ndim - 1)
 
 
+def position():
+    sx = lax.axis_index("sx")
+    return sx // 2, lax.rem(sx, 2), 4 * lax.axis_index("sy") + sx
+
+
 def pick(test, a, b):
     return jnp.where(test, a, b)
 
@@ -54,9 +59,10 @@
     return jnp.where(at < 32, roll(s, 32), jnp.where(at < 64, roll(f, 64), jnp.where(at < 96, roll(k, 96), far)))
 
 
-def pack_kernel(pos, scales, start, source, cond, elements, own, flip, along, across, home, conductivity, materials, split, done):
-    y = pos[0]
-    copies = [pltpu.make_async_copy(scales, conductivity, done.at[7]), pltpu.make_async_copy(elements, materials, done.at[0])]
+def pack_kernel(scales, rates, start, source, cond, elements, own, flip, along, across, home, conductivity, sinks, materials, split, done):
+    y, _, _ = position()
+    copies = [pltpu.make_async_copy(scales, conductivity, done.at[7]), pltpu.make_async_copy(rates, sinks, done.at[8])]
+    copies.append(pltpu.make_async_copy(elements, materials, done.at[0]))
     for a, ref in enumerate((start, source, cond)):
         for half in range(2):
             part = ref.at[:, pl.ds(half * LANES, LANES)]
@@ -68,12 +74,13 @@
     column = lax.broadcasted_iota(jnp.int32, (cells, width), 1)
     cell = lax.broadcasted_iota(jnp.int32, (cells, width), 0)
     spread = jnp.where(column // BLOCK == cell, 1.0, 0.0).astype(F32)
-    copies[0].wait()
-    copies[1].wait()
+    for copy in copies[:3]:
+        copy.wait()
     material = jnp.dot(materials[...].astype(F32), spread, preferred_element_type=F32)
     is_gob = material > 0.5
     factor = jnp.where(is_gob, conductivity[1], conductivity[0])
-    m0, m1 = material[:, :LANES], material[:, LANES:]
+    sink = time_step * jnp.where(is_gob, sinks[1], sinks[0])
+    m0, m1 = sink[:, :LANES], sink[:, LANES:]
     lower = y == 0
 
     def place(p, tiles, packs):
@@ -87,7 +94,7 @@
         along[p] = pick(lower, last1, first0)
         across[p] = pick(lower, first0, last1)
 
-    for copy in copies[2:]:
+    for copy in copies[3:]:
         copy.wait()
     home[0] = split[0]
     home[1] = split[1]
@@ -102,15 +109,24 @@
     place(BLOCK, None, (m0, roll(m0, 32), m1, roll(m1, 32)))
 
 
-def window_kernel(pos, own, other, along, across, mine, theirs):
-    lower = pos[0] == 0
-    even = pos[1] == 0
+def window_kernel(own, other, along, across, mine, theirs, rest, beside, done):
+    y, c, _ = position()
+    lower, even = y == 0, c == 0
     at = lax.broadcasted_iota(jnp.int32, own.shape[1:], 1)
 
     def put(slot, index, left, right):
         mine[slot, index] = pick(even, left, right)
         theirs[slot, index] = pick(even, right, left)
 
+    for p in range(BLOCK):
+        west0, east0 = pick(lower, along[p], own[TILE + p]), pick(lower, own[TILE + p], along[p])
+        west1, east1 = pick(lower, across[p], other[TILE + p]), pick(lower, other[TILE + p], across[p])
+        high = jnp.where(at < 96, roll(west1, 64), roll(east1, 96))
+        beside[p] = jnp.where(at < 32, west0, jnp.where(at < 64, roll(east0, 32), high))
+    parts = ((other.at[pl.ds(0, BLOCK)], 0), (beside, 1))
+    copies = [pltpu.make_async_copy(part, rest.at[pl.ds(i * BLOCK, BLOCK)], done.at[i]) for part, i in parts]
+    for copy in copies:
+        copy.start()
     for slot, (tile, outer) in enumerate(((own, along), (other, across))):
         for p in range(BLOCK + 1):
             inner, far = tile[TILE + p], outer[p]
@@ -127,6 +143,8 @@
             left = jnp.where(at < 2, roll(west, 32), jnp.where(at == 127, roll(s, 31), roll(k, 30)))
             right = jnp.where(at == 0, roll(s, 97), jnp.where(at == 1, roll(k, 98), jnp.where(at == 127, roll(east, 31), roll(east, 29))))
             put(slot, 3 * BLOCK + p, left, right)
+    for copy in copies:
+        copy.wait()
 
 
 def chunks(lines):
@@ -217,8 +235,8 @@
     return lambda first, p, z: put_padded(ref, p, first, z)
 
 
-def forward_kernel(pos, sinks, mine, theirs, states, ends, south, north, east, west, base, sink, level, forcing, kappa, edge, previous, old, new, *scaled):
-    y, c, strip, strips = pos[0], pos[1], pos[2], pos[3]
+def forward_kernel(strips, mine, theirs, states, ends, south, north, east, west, base, sink, level, forcing, kappa, edge, previous, old, new, *scaled):
+    y, c, strip = position()
     lines = base.shape[1]
     count = mine.shape[2]
     for ref in (level, kappa, old, new):
@@ -236,7 +254,7 @@
                 forcing[p, pl.ds(first, count), :] = time_step * ref[slot, BLOCK + p]
                 kappa[p, pl.ds(BLOCK + first, count), :] = jnp.where(inside, ref[slot, 2 * BLOCK + p], 0.0)
                 edge[p, pl.ds(first, count), :] = ref[slot, 3 * BLOCK + p]
-            sink[pl.ds(first, count), :] = time_step * jnp.where(ref[slot, 4 * BLOCK] > 0.5, sinks[1], sinks[0])
+            sink[pl.ds(first, count), :] = ref[slot, 4 * BLOCK]
 
     lane = lax.broadcasted_iota(jnp.int32, (CHUNK, LANES), 1)
     column = strip * STRIP - HALO + lane
@@ -313,30 +331,41 @@
         return carry
 
     lax.fori_loop(0, STEPS, step, 0)
-    pack_strip(lambda p, first: level[p, pl.ds(BLOCK + first, count), :], ends)
-
-
-def pack_strip(read, out):
+    pack_strip(lambda p, first: level[p, pl.ds(BLOCK + first, count), :], ends, True)
+
+
+def pack_strip(read, out, swapped=False):
     count = out.shape[2]
     at = lax.broadcasted_iota(jnp.int32, (count, LANES), 1)
     for core in range(2):
         for p in range(BLOCK):
             low, high = read(p, core * count), read(p, (2 + core) * count)
+            if swapped:
+                low, high = high, low
             out[core, p] = jnp.where(at < STRIP, roll(low, -HALO), roll(high, HALO))
 
 
-def adjoint_kernel(pos, states, mine, theirs, south, north, east, west, base, sink, out, old, new, given, *scaled):
-    y, c = pos[0], pos[1]
+def adjoint_kernel(states, own, rest, their_own, their_rest, south, north, east, west, base, sink, out, old, new, given, *scaled):
+    y, c, _ = position()
     lines = base.shape[1]
-    count = mine.shape[2]
+    count = own.shape[1]
     for ref in (old, new):
         clear_ends(ref, lines)
-    for ref, core in ((mine, c), (theirs, 1 - c)):
+    lane = lax.broadcasted_iota(jnp.int32, (count, LANES), 1)
+    even = c == 0
+    turn = jnp.where(even, HALO, LANES - HALO)
+    edge = jnp.where(even, lane, lane - (LANES - HALO))
+    from_side = (edge >= 0) & (edge < HALO)
+    for first_tile, others, core in ((own, rest, c), (their_own, their_rest, 1 - c)):
         for slot in range(2):
             chip = y if slot == 0 else 1 - y
             at = pl.ds(pl.multiple_of((2 * chip + core) * count, BLOCK), count)
+            side_turn = jnp.where(even, (LANES - 2 * HALO * slot) % LANES, (2 * LANES - 2 * HALO - 2 * HALO * slot) % LANES)
             for p in range(BLOCK):
-                given[p, at, :] = states[(STEPS - 1) * BLOCK + p, at, :] - ref[slot, p]
+                tile = pltpu.roll((others if slot else first_tile)[p], turn, axis=1)
+                side = pltpu.roll(others[BLOCK + p], side_turn, axis=1)
+                start = jnp.where(from_side, side, tile)
+                given[p, at, :] = states[(STEPS - 1) * BLOCK + p, at, :] - start
 
     def step(number, carry):
         level = STEPS - 1 - number
@@ -365,31 +394,21 @@
     pack_strip(lambda p, first: given[p, pl.ds(first, count), :], out)
 
 
-def send_kernel(pos, adjoint, previous, keep, core, flip, both):
-    y, c = pos[0], pos[1]
-    count = adjoint.shape[2]
+def join_kernel(home, keep, core, flip, both, defect, gradient, built, done):
+    y, c, _ = position()
+    count = keep.shape[1]
     at = lax.broadcasted_iota(jnp.int32, (count, LANES), 1)
-    for p in range(BLOCK):
-        rows = pl.ds(p, count, stride=BLOCK)
-        for owner, (same, other) in ((c, (keep, flip)), (1 - c, (core, both))):
-            a, e = adjoint[owner, p], previous[owner, p]
-            chip0 = jnp.where(at < STRIP, a, roll(e, STRIP))
-            chip1 = jnp.where(at < STRIP, roll(a, STRIP), e)
-            same[rows, :] = pick(y == 0, chip0, chip1)
-            other[rows, :] = pick(y == 0, chip1, chip0)
-
-
-def join_kernel(pos, home, keep, core, flip, both, defect, gradient, built, done):
-    y, c = pos[0], pos[1]
-    at = lax.broadcasted_iota(jnp.int32, keep.shape, 1)
     copies = []
     for chip in range(2):
         here = y == chip
-        one, two = pick(here, keep[...], flip[...]), pick(here, core[...], both[...])
-        even, odd = pick(c == 0, one, two), pick(c == 0, two, one)
-        missed = jnp.where(at < STRIP, roll(even, STRIP), odd) - home[chip]
-        built[0, chip] = missed
-        built[1, chip] = jnp.where(at < STRIP, even, roll(odd, STRIP)) - missed
+        for p in range(BLOCK):
+            one, two = pick(here, keep[p], flip[p]), pick(here, core[p], both[p])
+            even, odd = pick(c == 0, one, two), pick(c == 0, two, one)
+            low, high = jnp.where(at < STRIP, even, roll(odd, STRIP)), jnp.where(at < STRIP, roll(even, STRIP), odd)
+            rows = pl.ds(p, count, stride=BLOCK)
+            missed = pick(y == 0, high, low) - home[chip, rows, :]
+            built[0, chip, rows, :] = missed
+            built[1, chip, rows, :] = pick(y == 0, low, high) - missed
         for a, out in enumerate((defect, gradient)):
             copies.append(pltpu.make_async_copy(built.at[a, chip], out.at[:, pl.ds(chip * LANES, LANES)], done.at[a, chip]))
             copies[-1].start()
@@ -399,15 +418,13 @@
 
 def per_device(slabs, strips_y, start_states, source, cond_field, materials, conductivity, sink_rate):
     sx = lax.axis_index("sx")
-    z = lax.axis_index("sy")
     y, c = sx // 2, sx % 2
-    pos = jnp.stack([y, c, 4 * z + sx, jnp.int32(4 * strips_y)]).astype(jnp.int32)
     start, forcing = start_states[0], source[0]
     rows = start.shape[0]
     count = rows // BLOCK
     lines = 4 * count
     shape = lambda *dims: jax.ShapeDtypeStruct(dims, F32)
-    params = pltpu.CompilerParams(vmem_limit_bytes=48 * 1024 * 1024)
+    params = pltpu.CompilerParams(vmem_limit_bytes=16 * 1024 * 1024)
 
     def call(body, outs, ins, scratch=(), flops=0, out_specs=None):
         specs = [{"s": SMEM, "v": VMEM, "h": HBM}[kind] for kind in ins]
@@ -428,8 +445,8 @@
 
     def across_to(a, b, d):
         if a == 1:
-            return (0, b, d + 1) if d < top else (1, b, d)
-        return (1, b, d - 1) if d > 0 else (0, b, d)
+            return (0, b, d + 1) if d < top else (0, b, 0)
+        return (1, b, d - 1) if d > 0 else (1, b, top)
 
     along_pairs = [(joint(*v), joint(*along_to(*v))) for v in everyone]
     across_pairs = [(joint(*v), joint(*across_to(*v))) for v in everyone]
@@ -438,23 +455,35 @@
     forth = [(i, (i + 1) % slabs) for i in range(slabs)]
     back = [(b, a) for a, b in forth]
 
+    both_pairs = [(s * 4 + a, (s - 1) % slabs * 4 + b) for s in range(slabs) for a, b in core_pairs]
     diagonal_pairs = [(0, 3), (1, 2), (2, 1), (3, 0)]
 
     own, flip, along, across, home = call(
         pack_kernel,
         [shape(TILE + HALF, count, LANES)] * 2 + [shape(HALF, count, LANES)] * 2 + [shape(2, rows, LANES)],
-        "shhhhh",
-        [pltpu.SMEM((2,), F32), pltpu.VMEM(materials.shape, jnp.int32), pltpu.VMEM((6, rows, LANES), F32), pltpu.SemaphoreType.DMA((8,))],
-    )(pos, *(pltpu.with_memory_space_constraint(x, pltpu.HBM) for x in (conductivity, start, forcing, cond_field, materials)))
+        "hhhhhh",
+        [pltpu.SMEM((2,), F32), pltpu.SMEM((2,), F32), pltpu.VMEM(materials.shape, jnp.int32), pltpu.VMEM((6, rows, LANES), F32), pltpu.SemaphoreType.DMA((9,))],
+    )(*(pltpu.with_memory_space_constraint(x, pltpu.HBM) for x in (conductivity, sink_rate, start, forcing, cond_field, materials)))
     other = lax.ppermute(flip, "sx", flip_pairs)
     along = lax.ppermute(along, ("sx", "sy"), along_pairs)
     across = lax.ppermute(across, ("sx", "sy"), across_pairs)
 
-    mine, send = call(window_kernel, [shape(2, WIDE, count, LANES)] * 2, "svvvv")(pos, own, other, along, across)
+    next_own = lax.ppermute(own[:BLOCK], "slab", back)
+    other, along, across, next_own = lax.optimization_barrier((other, along, across, next_own))
+    mine, send, rest = call(
+        window_kernel,
+        [shape(2, WIDE, count, LANES)] * 2 + [shape(2 * BLOCK, count, LANES)],
+        "vvvv",
+        [pltpu.VMEM((BLOCK, count, LANES), F32), pltpu.SemaphoreType.DMA((2,))],
+        out_specs=[VMEM, VMEM, HBM],
+    )(own, other, along, across)
     theirs = lax.ppermute(send, "sx", core_pairs)
 
-    starts = jnp.stack([mine[:, :BLOCK], theirs[:, :BLOCK]])
-    next_starts = lax.ppermute(starts, "slab", back)
+    their_own = lax.ppermute(next_own, "sx", core_pairs)
+    next_rest = lax.ppermute(rest, "slab", back)
+    their_rest = lax.ppermute(rest, ("slab", "sx"), both_pairs)
+
+    theirs, their_own = lax.optimization_barrier((theirs, their_own))
 
     whole = shape(BLOCK, lines, LANES)
     flat = shape(lines, LANES)
@@ -463,29 +492,35 @@
     plain = pltpu.VMEM((BLOCK, lines, LANES), F32)
     scaled = [plain] * 5 + [pltpu.VMEM((2, lines, LANES), F32)]
     states, ends, south, north, east, west, base, sink = call(
-        forward_kernel,
+        functools.partial(forward_kernel, 4 * strips_y),
         [shape(STEPS * BLOCK, lines, LANES), strip, whole, whole, whole, flat, whole, flat],
-        "ssvv",
+        "vv",
         [buffer, plain, buffer, plain, plain, buffer, buffer] + scaled,
         flops=20_000_000,
-    )(pos, sink_rate, mine, theirs)
+    )(mine, theirs)
     previous = lax.ppermute(ends, "slab", forth)
-
-    (adjoint,) = call(adjoint_kernel, [strip], "s" + "v" * 9, [buffer, buffer, plain] + scaled, flops=10_000_000)(
-        pos, states, next_starts[0], next_starts[1], south, north, east, west, base, sink
+    (adjoint,) = call(adjoint_kernel, [strip], "v" * 11, [buffer, buffer, plain] + scaled, flops=10_000_000)(
+        states, next_own, next_rest, their_own, their_rest, south, north, east, west, base, sink
     )
 
-    keep, core, flip, both = call(send_kernel, [shape(rows, LANES)] * 4, "svv")(pos, adjoint, previous)
+    low_lanes = lax.broadcasted_iota(jnp.int32, (BLOCK, count, LANES), 2) < STRIP
+
+    def strip_for(chip, owner):
+        a = lax.dynamic_index_in_dim(adjoint, owner, 0, keepdims=False)
+        e = lax.dynamic_index_in_dim(previous, owner, 0, keepdims=False)
+        return jnp.where(low_lanes == (chip == 0), a, e)
+
+    keep, core, flip, both = (strip_for(*to) for to in ((y, c), (y, 1 - c), (1 - y, c), (1 - y, 1 - c)))
     flip = lax.ppermute(flip, "sx", flip_pairs)
     both = lax.ppermute(both, "sx", diagonal_pairs)
     core = lax.ppermute(core, "sx", core_pairs)
     defect, gradient = call(
         join_kernel,
         [shape(rows, 2 * LANES)] * 2,
-        "svvvvv",
+        "vvvvv",
         [pltpu.VMEM((2, 2, rows, LANES), F32), pltpu.SemaphoreType.DMA((2, 2))],
         out_specs=[HBM] * 2,
-    )(pos, home, keep, core, flip, both)
+    )(home, keep, core, flip, both)
     return (defect[None], gradient[None])
 
 

time: 38.2 us -> 35.5 us (0.929)
  starting transfers between devices: 9.66 us -> 14.3 us
  waiting for transfers between devices: 13.4 us -> 9.78 us
  Pallas kernels: 14 us -> 10.5 us
    ppermute x1, waiting for transfers between devices: 6 us -> 1.55 us  [per_device(): along = lax.ppermute(along, ('sx', 'sy'), along_pairs)]
    pallas_call x5 -> x4, Pallas kernels: 12 us -> 9.01 us  [the longest x1 4.7 us: per_device(): call(functools.partial(forward_kernel, 4 * strips_y), [shape(STEPS * BLOC...]
    ppermute x1 -> x4, waiting for transfers between devices: 0.21 us -> 2.78 us  [the longest x1 2.77 us: per_device(): next_own = lax.ppermute(own[:BLOCK], 'slab', back)]
    ppermute x1 -> x4, starting transfers between devices: 1.78 us -> 3.7 us  [the longest x1 1.71 us: per_device(): next_rest = lax.ppermute(rest, 'slab', back)]
    ppermute x1, waiting for transfers between devices: 1.9 us -> 0.01 us  [per_device(): theirs = lax.ppermute(send, 'sx', core_pairs)]
    ppermute x1, starting transfers between devices: 0.65 us -> 2.42 us  [per_device(): across = lax.ppermute(across, ('sx', 'sy'), across_pairs)]
    ppermute x1, starting transfers between devices: 1.57 us -> 0.2 us  [per_device(): flip = lax.ppermute(flip, 'sx', flip_pairs)]
    ppermute x1, starting transfers between devices: 0.29 us -> 1.66 us  [per_device(): both = lax.ppermute(both, 'sx', diagonal_pairs)]
  transfers between devices with their start and end apart: 9 -> 12, of which waited for: 6 -> 5; matrix products, arithmetic and copies ran while one was open for 0% -> 0% of each run, Pallas kernels for 23% -> 20%
where the time goes in v3:
time: 35.5 us; the launch traced here: 35.3 us
  starting transfers between devices  14.3 us (40%)
  Pallas kernels  10.5 us (30%)
  waiting for transfers between devices  9.78 us (28%)
  between operations  0.71 us (2%)
    pallas_call x1, Pallas kernels, per_device(): call(functools.partial(forward_kernel, 4 * strips_y), [shape(STEPS * BLOC...  4.7 us
    ppermute x1, waiting for transfers between devices, per_device(): flip = lax.ppermute(flip, 'sx', flip_pairs)  3.09 us
    ppermute x1, starting transfers between devices, per_device(): other = lax.ppermute(flip, 'sx', flip_pairs)  3.03 us
    ppermute x1, waiting for transfers between devices, per_device(): next_own = lax.ppermute(own[:BLOCK], 'slab', back)  2.77 us
    pallas_call x1, Pallas kernels, per_device(): call(adjoint_kernel, [strip], 'v' * 11, [buffer, buffer, plain] + scaled,...  2.46 us
    ppermute x1, starting transfers between devices, per_device(): across = lax.ppermute(across, ('sx', 'sy'), across_pairs)  2.42 us
    ppermute x1, waiting for transfers between devices, per_device(): previous = lax.ppermute(ends, 'slab', forth)  1.84 us
    ppermute x1, starting transfers between devices, per_device(): next_rest = lax.ppermute(rest, 'slab', back)  1.71 us
  transfers between devices with their start and end apart: 12, of which 5 were waited for; matrix products, arithmetic and copies ran while one was open for 0% of the time, Pallas kernels for 20%

profile of v3, /device:TPU:0, one launch (start us, length us, event | category | flops | bytes accessed | tf_op | source)
XLA Modules:
  0.0 35.3 jit_solution(14667836566010241071)
XLA Ops:
  0.6 1.5 %shard_map.77 = (f32[34,16,128]{2,1,0:T(8,128)S(1)}, f32[34,16,128]{2,1,0:T(8,128)S(1)}, f32[9,16,128]{2,1,0:T(8,128)S(1)}, f32[9,16,128]{2,1,0:T(8,128)S(1)}, f32[2,128,128]{2,1,0:T(8,128)S(1)}) custom-call(f32[2]{0:T(128)} %scales.1, f32[2]{0:T(128)} %rates.1, f32[128,256]{1,0:T(8,128)} %bitcast.16, f32[128,256]{1,0:T(8,128)} %bitcast.17, ...), custom_call_target="tpu_custom_call" | custom-call | bytes 1048576 | tf_op jit(solution)/shard_map/pallas_call | solution.py:461
  2.1 3.0 %collective-permute-start = (f32[34,16,128]{2,1,0:T(8,128)S(1)}, f32[34,16,128]{2,1,0:T(8,128)S(1)}, u32[]{:S(2)}, u32[]{:S(2)}) collective-permute-start(f32[34,16,128]{2,1,0:T(8,128)S(1)} %get-tuple-element.28), channel_id=1, source_target_pairs={{0,8},{4,12},{8,0},{12,4},{1,9},{5,13},{9,1},{13,5},{2,10},{6,14},... | collective-permute-start | bytes 835592 | tf_op jit(solution)/shard_map/ppermute | solution.py:467
  5.2 1.6 %collective-permute-start.1 = (f32[9,16,128]{2,1,0:T(8,128)S(1)}, f32[9,16,128]{2,1,0:T(8,128)S(1)}, u32[]{:S(2)}, u32[]{:S(2)}) collective-permute-start(f32[9,16,128]{2,1,0:T(8,128)S(1)} %get-tuple-element.29), channel_id=1, source_target_pairs={{0,1},{1,2},{2,3},{3,11},{4,5},{5,6},{6,7},{7,15},{8,0},{9,8},{10,... | collective-permute-start | bytes 221192 | tf_op jit(solution)/shard_map/ppermute | solution.py:468
  6.7 2.4 %collective-permute-start.2 = (f32[9,16,128]{2,1,0:T(8,128)S(1)}, f32[9,16,128]{2,1,0:T(8,128)S(1)}, u32[]{:S(2)}, u32[]{:S(2)}) collective-permute-start(f32[9,16,128]{2,1,0:T(8,128)S(1)} %get-tuple-element.30), channel_id=1, source_target_pairs={{0,11},{1,8},{2,9},{3,10},{4,15},{5,12},{6,13},{7,14},{8,1},{9,2},... | collective-permute-start | bytes 221192 | tf_op jit(solution)/shard_map/ppermute | solution.py:469
  9.2 1.5 %collective-permute-start.3 = (f32[8,16,128]{2,1,0:T(8,128)S(1)}, f32[8,16,128]{2,1,0:T(8,128)S(1)}, u32[]{:S(2)}, u32[]{:S(2)}) collective-permute-start(f32[8,16,128]{2,1,0:T(8,128)S(1)} %slice.3), channel_id=1, source_target_pairs={{16,0},{0,16},{17,1},{1,17},{18,2},{2,18},{19,3},{3,19},{20,4},{4,... | collective-permute-start | bytes 196616 | tf_op jit(solution)/shard_map/ppermute | solution.py:471
  10.6 2.8 %collective-permute-done.3.own = f32[8,16,128]{2,1,0:T(8,128)S(1)} collective-permute-done((f32[8,16,128]{2,1,0:T(8,128)S(1)}, f32[8,16,128]{2,1,0:T(8,128)S(1)}, u32[]{:S(2)}, u32[]{:S(2)}) %collective-permute-start.3) | collective-permute-done | bytes 65568 | tf_op jit(solution)/shard_map/ppermute | solution.py:471
  13.4 1.5 %collective-permute-done.1.along = f32[9,16,128]{2,1,0:T(8,128)S(1)} collective-permute-done((f32[9,16,128]{2,1,0:T(8,128)S(1)}, f32[9,16,128]{2,1,0:T(8,128)S(1)}, u32[]{:S(2)}, u32[]{:S(2)}) %collective-permute-start.1) | collective-permute-done | bytes 73760 | tf_op jit(solution)/shard_map/ppermute | solution.py:468
  15.0 0.0 collective-permute-done.2.across
  15.0 0.0 collective-permute-done.other
  15.0 1.0 %shard_map.78 = (f32[2,33,16,128]{3,2,1,0:T(8,128)S(1)}, f32[2,33,16,128]{3,2,1,0:T(8,128)S(1)}, f32[16,16,128]{2,1,0:T(8,128)S(1)}) custom-call(f32[34,16,128]{2,1,0:T(8,128)S(1)} %get-tuple-element.27.own, f32[34,16,128]{2,1,0:T(8,128)S(1)} %collective-permute-done.other, f32[9,16,128]{2,1,0:T(8,128)S(1)} %collective-permute-done.1.along, ...), custom_call_target="tpu_custom_call" | custom-call | bytes 1048576 | tf_op jit(solution)/shard_map/pallas_call | solution.py:473
  16.0 0.1 collective-permute-start.4
  16.1 0.5 %collective-permute-start.5 = (f32[8,16,128]{2,1,0:T(8,128)S(1)}, f32[8,16,128]{2,1,0:T(8,128)S(1)}, u32[]{:S(2)}, u32[]{:S(2)}) collective-permute-start(f32[8,16,128]{2,1,0:T(8,128)S(1)} %collective-permute-done.3.own), channel_id=1, source_target_pairs={{0,4},{4,0},{8,12},{12,8},{1,5},{5,1},{9,13},{13,9},{2,6},{6,2},{1... | collective-permute-start | bytes 196616 | tf_op jit(solution)/shard_map/ppermute | solution.py:482
  16.6 1.7 %collective-permute-start.6 = (f32[16,16,128]{2,1,0:T(8,128)S(1)}, f32[16,16,128]{2,1,0:T(8,128)S(1)}, u32[]{:S(2)}, u32[]{:S(2)}) collective-permute-start(f32[16,16,128]{2,1,0:T(8,128)S(1)} %get-tuple-element.39), channel_id=1, source_target_pairs={{16,0},{0,16},{17,1},{1,17},{18,2},{2,18},{19,3},{3,19},{20,4},{4,... | collective-permute-start | bytes 393224 | tf_op jit(solution)/shard_map/ppermute | solution.py:483
  18.3 0.0 collective-permute-start.7
  18.3 0.0 collective-permute-done.5.their_own
  18.3 0.0 collective-permute-done.4.theirs
  18.3 4.7 %shard_map.79 = (f32[24,64,128]{2,1,0:T(8,128)S(1)}, f32[2,8,16,128]{3,2,1,0:T(8,128)S(1)}, f32[8,64,128]{2,1,0:T(8,128)S(1)}, f32[8,64,128]{2,1,0:T(8,128)S(1)}...) custom-call(f32[2,33,16,128]{3,2,1,0:T(8,128)S(1)} %get-tuple-element.34, ...), custom_call_target="tpu_custom_call" | custom-call | flops 20000000 | bytes 1048576 | tf_op jit(solution)/shard_map/pallas_call | solution.py:494
  23.0 1.6 %collective-permute-start.8 = (f32[2,8,16,128]{3,2,1,0:T(8,128)S(1)}, f32[2,8,16,128]{3,2,1,0:T(8,128)S(1)}, u32[]{:S(2)}, u32[]{:S(2)}) collective-permute-start(f32[2,8,16,128]{3,2,1,0:T(8,128)S(1)} %get-tuple-element.47), channel_id=1, source_target_pairs={{0,16},{16,0},{1,17},{17,1},{2,18},{18,2},{3,19},{19,3},{4,20},{20... | collective-permute-start | bytes 393224 | tf_op jit(solution)/shard_map/ppermute | solution.py:501
  24.6 0.0 collective-permute-done.6.rest
  24.6 0.0 collective-permute-done.7.their_rest
  24.6 2.5 %shard_map.80 = f32[2,8,16,128]{3,2,1,0:T(8,128)S(1)} custom-call(f32[24,64,128]{2,1,0:T(8,128)S(1)} %get-tuple-element.38.states, f32[8,16,128]{2,1,0:T(8,128)S(1)} %collective-permute-done.3.own, f32[16,16,128]{2,1,0:T(8,128)S(1)} %collective-permute-done.6.rest, f32[8,16,128]{2,1,0:T(8,128)S(1)} %collective-permute-done.5.their_own, ...), custom_call_target="tpu_custom_call" | custom-call | flops 10000000 | bytes 1048576 | tf_op jit(solution)/shard_map/pallas_call | solution.py:502
  27.1 1.8 %collective-permute-done.8 = f32[2,8,16,128]{3,2,1,0:T(8,128)S(1)} collective-permute-done((f32[2,8,16,128]{3,2,1,0:T(8,128)S(1)}, f32[2,8,16,128]{3,2,1,0:T(8,128)S(1)}, u32[]{:S(2)}, u32[]{:S(2)}) %collective-permute-start.8) | collective-permute-done | bytes 131104 | tf_op jit(solution)/shard_map/ppermute | solution.py:501
  28.9 0.1 collective-permute-start.9
  29.0 0.2 collective-permute-start.10
  29.2 1.7 %collective-permute-start.11 = (f32[8,16,128]{2,1,0:T(8,128)S(1)}, f32[8,16,128]{2,1,0:T(8,128)S(1)}, u32[]{:S(2)}, u32[]{:S(2)}) collective-permute-start(f32[8,16,128]{2,1,0:T(8,128)S(1)} %get-tuple-element.50), channel_id=1, source_target_pairs={{0,12},{4,8},{8,4},{12,0},{1,13},{5,9},{9,5},{13,1},{2,14},{6,10},... | collective-permute-start | bytes 196616 | tf_op jit(solution)/shard_map/ppermute | solution.py:515
  30.9 0.0 collective-permute-done.9.core
  30.9 3.1 %collective-permute-done.10.flip = f32[8,16,128]{2,1,0:T(8,128)S(1)} collective-permute-done((f32[8,16,128]{2,1,0:T(8,128)S(1)}, f32[8,16,128]{2,1,0:T(8,128)S(1)}, u32[]{:S(2)}, u32[]{:S(2)}) %collective-permute-start.10) | collective-permute-done | bytes 65568 | tf_op jit(solution)/shard_map/ppermute | solution.py:514
  34.0 0.5 %collective-permute-done.11.both = f32[8,16,128]{2,1,0:T(8,128)S(1)} collective-permute-done((f32[8,16,128]{2,1,0:T(8,128)S(1)}, f32[8,16,128]{2,1,0:T(8,128)S(1)}, u32[]{:S(2)}, u32[]{:S(2)}) %collective-permute-start.11) | collective-permute-done | bytes 65568 | tf_op jit(solution)/shard_map/ppermute | solution.py:515
  34.5 0.8 %shard_map.81 = (f32[128,256]{1,0:T(8,128)}, f32[128,256]{1,0:T(8,128)}) custom-call(f32[2,128,128]{2,1,0:T(8,128)S(1)} %get-tuple-element.26.home, f32[8,16,128]{2,1,0:T(8,128)S(1)} %get-tuple-element.54.keep, f32[8,16,128]{2,1,0:T(8,128)S(1)} %collective-permute-done.9.core, f32[8,16,128]{2,1,0:T(8,128)S(1)} %collective-permute-done.10.flip, ...), custom_call_target="tpu_custom_call" | custom-call | bytes 1048576 | tf_op jit(solution)/shard_map/pallas_call | solution.py:517
  (3 shorter events, 0.0 us)
Async XLA Ops:
  2.1 12.9 %collective-permute-start = (f32[34,16,128]{2,1,0:T(8,128)S(1)}, f32[34,16,128]{2,1,0:T(8,128)S(1)}, u32[]{:S(2)}, u32[]{:S(2)}) collective-permute-start(f32[34,16,128]{2,1,0:T(8,128)S(1)} %get-tuple-element.28), channel_id=1, source_target_pairs={{0,8},{4,12},{8,0},{12,4},{1,9},{5,13},{9,1},{13,5},{2,10},{6,14},... | collective-permute-start | bytes 835592 | tf_op jit(solution)/shard_map/ppermute | solution.py:467
  5.2 9.8 %collective-permute-start.1 = (f32[9,16,128]{2,1,0:T(8,128)S(1)}, f32[9,16,128]{2,1,0:T(8,128)S(1)}, u32[]{:S(2)}, u32[]{:S(2)}) collective-permute-start(f32[9,16,128]{2,1,0:T(8,128)S(1)} %get-tuple-element.29), channel_id=1, source_target_pairs={{0,1},{1,2},{2,3},{3,11},{4,5},{5,6},{6,7},{7,15},{8,0},{9,8},{10,... | collective-permute-start | bytes 221192 | tf_op jit(solution)/shard_map/ppermute | solution.py:468
  6.7 8.2 %collective-permute-start.2 = (f32[9,16,128]{2,1,0:T(8,128)S(1)}, f32[9,16,128]{2,1,0:T(8,128)S(1)}, u32[]{:S(2)}, u32[]{:S(2)}) collective-permute-start(f32[9,16,128]{2,1,0:T(8,128)S(1)} %get-tuple-element.30), channel_id=1, source_target_pairs={{0,11},{1,8},{2,9},{3,10},{4,15},{5,12},{6,13},{7,14},{8,1},{9,2},... | collective-permute-start | bytes 221192 | tf_op jit(solution)/shard_map/ppermute | solution.py:469
  9.2 4.3 %collective-permute-start.3 = (f32[8,16,128]{2,1,0:T(8,128)S(1)}, f32[8,16,128]{2,1,0:T(8,128)S(1)}, u32[]{:S(2)}, u32[]{:S(2)}) collective-permute-start(f32[8,16,128]{2,1,0:T(8,128)S(1)} %slice.3), channel_id=1, source_target_pairs={{16,0},{0,16},{17,1},{1,17},{18,2},{2,18},{19,3},{3,19},{20,4},{4,... | collective-permute-start | bytes 196616 | tf_op jit(solution)/shard_map/ppermute | solution.py:471
  16.0 2.3 %collective-permute-start.4 = (f32[2,33,16,128]{3,2,1,0:T(8,128)S(1)}, f32[2,33,16,128]{3,2,1,0:T(8,128)S(1)}, u32[]{:S(2)}, u32[]{:S(2)}) collective-permute-start(f32[2,33,16,128]{3,2,1,0:T(8,128)S(1)} %get-tuple-element.35), channel_id=1, source_target_pairs={{0,4},{4,0},{8,12},{12,8},{1,5},{5,1},{9,13},{13,9},{2,6},{6,2},{1... | collective-permute-start | bytes 1622024 | tf_op jit(solution)/shard_map/ppermute | solution.py:480
  16.1 2.2 %collective-permute-start.5 = (f32[8,16,128]{2,1,0:T(8,128)S(1)}, f32[8,16,128]{2,1,0:T(8,128)S(1)}, u32[]{:S(2)}, u32[]{:S(2)}) collective-permute-start(f32[8,16,128]{2,1,0:T(8,128)S(1)} %collective-permute-done.3.own), channel_id=1, source_target_pairs={{0,4},{4,0},{8,12},{12,8},{1,5},{5,1},{9,13},{13,9},{2,6},{6,2},{1... | collective-permute-start | bytes 196616 | tf_op jit(solution)/shard_map/ppermute | solution.py:482
  16.6 8.0 %collective-permute-start.6 = (f32[16,16,128]{2,1,0:T(8,128)S(1)}, f32[16,16,128]{2,1,0:T(8,128)S(1)}, u32[]{:S(2)}, u32[]{:S(2)}) collective-permute-start(f32[16,16,128]{2,1,0:T(8,128)S(1)} %get-tuple-element.39), channel_id=1, source_target_pairs={{16,0},{0,16},{17,1},{1,17},{18,2},{2,18},{19,3},{3,19},{20,4},{4,... | collective-permute-start | bytes 393224 | tf_op jit(solution)/shard_map/ppermute | solution.py:483
  18.3 6.3 %collective-permute-start.7 = (f32[16,16,128]{2,1,0:T(8,128)S(1)}, f32[16,16,128]{2,1,0:T(8,128)S(1)}, u32[]{:S(2)}, u32[]{:S(2)}) collective-permute-start(f32[16,16,128]{2,1,0:T(8,128)S(1)} %get-tuple-element.39), channel_id=1, source_target_pairs={{0,20},{4,16},{8,28},{12,24},{16,4},{20,0},{24,12},{28,8},{1,21},{... | collective-permute-start | bytes 393224 | tf_op jit(solution)/shard_map/ppermute | solution.py:484
  23.0 5.9 %collective-permute-start.8 = (f32[2,8,16,128]{3,2,1,0:T(8,128)S(1)}, f32[2,8,16,128]{3,2,1,0:T(8,128)S(1)}, u32[]{:S(2)}, u32[]{:S(2)}) collective-permute-start(f32[2,8,16,128]{3,2,1,0:T(8,128)S(1)} %get-tuple-element.47), channel_id=1, source_target_pairs={{0,16},{16,0},{1,17},{17,1},{2,18},{18,2},{3,19},{19,3},{4,20},{20... | collective-permute-start | bytes 393224 | tf_op jit(solution)/shard_map/ppermute | solution.py:501
  28.9 1.9 %collective-permute-start.9 = (f32[8,16,128]{2,1,0:T(8,128)S(1)}, f32[8,16,128]{2,1,0:T(8,128)S(1)}, u32[]{:S(2)}, u32[]{:S(2)}) collective-permute-start(f32[8,16,128]{2,1,0:T(8,128)S(1)} %get-tuple-element.55), channel_id=1, source_target_pairs={{0,4},{4,0},{8,12},{12,8},{1,5},{5,1},{9,13},{13,9},{2,6},{6,2},{1... | collective-permute-start | bytes 196616 | tf_op jit(solution)/shard_map/ppermute | solution.py:516
  29.0 5.0 %collective-permute-start.10 = (f32[8,16,128]{2,1,0:T(8,128)S(1)}, f32[8,16,128]{2,1,0:T(8,128)S(1)}, u32[]{:S(2)}, u32[]{:S(2)}) collective-permute-start(f32[8,16,128]{2,1,0:T(8,128)S(1)} %get-tuple-element.51), channel_id=1, source_target_pairs={{0,8},{4,12},{8,0},{12,4},{1,9},{5,13},{9,1},{13,5},{2,10},{6,14},... | collective-permute-start | bytes 196616 | tf_op jit(solution)/shard_map/ppermute | solution.py:514
  29.2 5.3 %collective-permute-start.11 = (f32[8,16,128]{2,1,0:T(8,128)S(1)}, f32[8,16,128]{2,1,0:T(8,128)S(1)}, u32[]{:S(2)}, u32[]{:S(2)}) collective-permute-start(f32[8,16,128]{2,1,0:T(8,128)S(1)} %get-tuple-element.50), channel_id=1, source_target_pairs={{0,12},{4,8},{8,4},{12,0},{1,13},{5,9},{9,5},{13,1},{2,14},{6,10},... | collective-permute-start | bytes 196616 | tf_op jit(solution)/shard_map/ppermute | solution.py:515

commit v4 on v3

--- a/solution.py
+++ b/solution.py
@@ -445,8 +445,8 @@
 
     def across_to(a, b, d):
         if a == 1:
-            return (0, b, d + 1) if d < top else (0, b, 0)
-        return (1, b, d - 1) if d > 0 else (1, b, top)
+            return (0, b, d + 1) if d < top else (1, 1 - b, d)
+        return (1, b, d - 1) if d > 0 else (0, 1 - b, d)
 
     along_pairs = [(joint(*v), joint(*along_to(*v))) for v in everyone]
     across_pairs = [(joint(*v), joint(*across_to(*v))) for v in everyone]

time: 35.5 us -> 34.3 us (0.966)
  starting transfers between devices: 14.3 us -> 12 us
  waiting for transfers between devices: 9.78 us -> 10.9 us
    ppermute x1, starting transfers between devices: 2.42 us -> 0.01 us  [per_device(): across = lax.ppermute(across, ('sx', 'sy'), across_pairs)]
    ppermute x1, starting transfers between devices: 0.2 us -> 1.78 us  [per_device(): flip = lax.ppermute(flip, 'sx', flip_pairs)]
    ppermute x1, starting transfers between devices: 1.66 us -> 0.08 us  [per_device(): both = lax.ppermute(both, 'sx', diagonal_pairs)]
    ppermute x1, waiting for transfers between devices: 0.5 us -> 1.32 us  [per_device(): both = lax.ppermute(both, 'sx', diagonal_pairs)]
    ppermute x1, waiting for transfers between devices: 1.55 us -> 2.14 us  [per_device(): along = lax.ppermute(along, ('sx', 'sy'), along_pairs)]
    ppermute x1, waiting for transfers between devices: 3.09 us -> 2.64 us  [per_device(): flip = lax.ppermute(flip, 'sx', flip_pairs)]
  transfers between devices with their start and end apart: 12 -> 12, of which waited for: 5 -> 5; matrix products, arithmetic and copies ran while one was open for 0% -> 0% of each run, Pallas kernels for 20% -> 21%
where the time goes in v4:
time: 34.3 us; the launch traced here: 34.1 us
  starting transfers between devices  12 us (35%)
  waiting for transfers between devices  10.9 us (32%)
  Pallas kernels  10.5 us (31%)
  between operations  0.71 us (2%)
    pallas_call x1, Pallas kernels, per_device(): call(functools.partial(forward_kernel, 4 * strips_y), [shape(STEPS * BLOC...  4.7 us
    ppermute x1, starting transfers between devices, per_device(): other = lax.ppermute(flip, 'sx', flip_pairs)  3.03 us
    ppermute x1, waiting for transfers between devices, per_device(): next_own = lax.ppermute(own[:BLOCK], 'slab', back)  2.95 us
    ppermute x1, waiting for transfers between devices, per_device(): flip = lax.ppermute(flip, 'sx', flip_pairs)  2.64 us
    pallas_call x1, Pallas kernels, per_device(): call(adjoint_kernel, [strip], 'v' * 11, [buffer, buffer, plain] + scaled,...  2.46 us
    ppermute x1, waiting for transfers between devices, per_device(): along = lax.ppermute(along, ('sx', 'sy'), along_pairs)  2.14 us
    ppermute x1, waiting for transfers between devices, per_device(): previous = lax.ppermute(ends, 'slab', forth)  1.84 us
    ppermute x1, starting transfers between devices, per_device(): flip = lax.ppermute(flip, 'sx', flip_pairs)  1.78 us
  transfers between devices with their start and end apart: 12, of which 5 were waited for; matrix products, arithmetic and copies ran while one was open for 0% of the time, Pallas kernels for 21%

profile of v4, /device:TPU:0, one launch (start us, length us, event | category | flops | bytes accessed | tf_op | source)
XLA Modules:
  0.0 34.1 jit_solution(9243514089021530042)
XLA Ops:
  0.6 1.5 %shard_map.77 = (f32[34,16,128]{2,1,0:T(8,128)S(1)}, f32[34,16,128]{2,1,0:T(8,128)S(1)}, f32[9,16,128]{2,1,0:T(8,128)S(1)}, f32[9,16,128]{2,1,0:T(8,128)S(1)}, f32[2,128,128]{2,1,0:T(8,128)S(1)}) custom-call(f32[2]{0:T(128)} %scales.1, f32[2]{0:T(128)} %rates.1, f32[128,256]{1,0:T(8,128)} %bitcast.16, f32[128,256]{1,0:T(8,128)} %bitcast.17, ...), custom_call_target="tpu_custom_call" | custom-call | bytes 1048576 | tf_op jit(solution)/shard_map/pallas_call | solution.py:461
  2.1 3.0 %collective-permute-start = (f32[34,16,128]{2,1,0:T(8,128)S(1)}, f32[34,16,128]{2,1,0:T(8,128)S(1)}, u32[]{:S(2)}, u32[]{:S(2)}) collective-permute-start(f32[34,16,128]{2,1,0:T(8,128)S(1)} %get-tuple-element.28), channel_id=1, source_target_pairs={{0,8},{4,12},{8,0},{12,4},{1,9},{5,13},{9,1},{13,5},{2,10},{6,14},... | collective-permute-start | bytes 835592 | tf_op jit(solution)/shard_map/ppermute | solution.py:467
  5.2 1.6 %collective-permute-start.1 = (f32[9,16,128]{2,1,0:T(8,128)S(1)}, f32[9,16,128]{2,1,0:T(8,128)S(1)}, u32[]{:S(2)}, u32[]{:S(2)}) collective-permute-start(f32[9,16,128]{2,1,0:T(8,128)S(1)} %get-tuple-element.29), channel_id=1, source_target_pairs={{0,1},{1,2},{2,3},{3,11},{4,5},{5,6},{6,7},{7,15},{8,0},{9,8},{10,... | collective-permute-start | bytes 221192 | tf_op jit(solution)/shard_map/ppermute | solution.py:468
  6.7 0.0 collective-permute-start.2
  6.7 1.6 %collective-permute-start.3 = (f32[8,16,128]{2,1,0:T(8,128)S(1)}, f32[8,16,128]{2,1,0:T(8,128)S(1)}, u32[]{:S(2)}, u32[]{:S(2)}) collective-permute-start(f32[8,16,128]{2,1,0:T(8,128)S(1)} %slice.3), channel_id=1, source_target_pairs={{16,0},{0,16},{17,1},{1,17},{18,2},{2,18},{19,3},{3,19},{20,4},{4,... | collective-permute-start | bytes 196616 | tf_op jit(solution)/shard_map/ppermute | solution.py:471
  8.3 2.9 %collective-permute-done.3.own = f32[8,16,128]{2,1,0:T(8,128)S(1)} collective-permute-done((f32[8,16,128]{2,1,0:T(8,128)S(1)}, f32[8,16,128]{2,1,0:T(8,128)S(1)}, u32[]{:S(2)}, u32[]{:S(2)}) %collective-permute-start.3) | collective-permute-done | bytes 65568 | tf_op jit(solution)/shard_map/ppermute | solution.py:471
  11.2 2.1 %collective-permute-done.1.along = f32[9,16,128]{2,1,0:T(8,128)S(1)} collective-permute-done((f32[9,16,128]{2,1,0:T(8,128)S(1)}, f32[9,16,128]{2,1,0:T(8,128)S(1)}, u32[]{:S(2)}, u32[]{:S(2)}) %collective-permute-start.1) | collective-permute-done | bytes 73760 | tf_op jit(solution)/shard_map/ppermute | solution.py:468
  13.4 0.0 collective-permute-done.2.across
  13.4 0.0 collective-permute-done.other
  13.4 1.0 %shard_map.78 = (f32[2,33,16,128]{3,2,1,0:T(8,128)S(1)}, f32[2,33,16,128]{3,2,1,0:T(8,128)S(1)}, f32[16,16,128]{2,1,0:T(8,128)S(1)}) custom-call(f32[34,16,128]{2,1,0:T(8,128)S(1)} %get-tuple-element.27.own, f32[34,16,128]{2,1,0:T(8,128)S(1)} %collective-permute-done.other, f32[9,16,128]{2,1,0:T(8,128)S(1)} %collective-permute-done.1.along, ...), custom_call_target="tpu_custom_call" | custom-call | bytes 1048576 | tf_op jit(solution)/shard_map/pallas_call | solution.py:473
  14.4 0.1 collective-permute-start.4
  14.5 0.5 %collective-permute-start.5 = (f32[8,16,128]{2,1,0:T(8,128)S(1)}, f32[8,16,128]{2,1,0:T(8,128)S(1)}, u32[]{:S(2)}, u32[]{:S(2)}) collective-permute-start(f32[8,16,128]{2,1,0:T(8,128)S(1)} %collective-permute-done.3.own), channel_id=1, source_target_pairs={{0,4},{4,0},{8,12},{12,8},{1,5},{5,1},{9,13},{13,9},{2,6},{6,2},{1... | collective-permute-start | bytes 196616 | tf_op jit(solution)/shard_map/ppermute | solution.py:482
  15.0 1.7 %collective-permute-start.6 = (f32[16,16,128]{2,1,0:T(8,128)S(1)}, f32[16,16,128]{2,1,0:T(8,128)S(1)}, u32[]{:S(2)}, u32[]{:S(2)}) collective-permute-start(f32[16,16,128]{2,1,0:T(8,128)S(1)} %get-tuple-element.39), channel_id=1, source_target_pairs={{16,0},{0,16},{17,1},{1,17},{18,2},{2,18},{19,3},{3,19},{20,4},{4,... | collective-permute-start | bytes 393224 | tf_op jit(solution)/shard_map/ppermute | solution.py:483
  16.7 0.0 collective-permute-start.7
  16.7 0.0 collective-permute-done.5.their_own
  16.7 0.0 collective-permute-done.4.theirs
  16.7 4.7 %shard_map.79 = (f32[24,64,128]{2,1,0:T(8,128)S(1)}, f32[2,8,16,128]{3,2,1,0:T(8,128)S(1)}, f32[8,64,128]{2,1,0:T(8,128)S(1)}, f32[8,64,128]{2,1,0:T(8,128)S(1)}...) custom-call(f32[2,33,16,128]{3,2,1,0:T(8,128)S(1)} %get-tuple-element.34, ...), custom_call_target="tpu_custom_call" | custom-call | flops 20000000 | bytes 1048576 | tf_op jit(solution)/shard_map/pallas_call | solution.py:494
  21.4 1.6 %collective-permute-start.8 = (f32[2,8,16,128]{3,2,1,0:T(8,128)S(1)}, f32[2,8,16,128]{3,2,1,0:T(8,128)S(1)}, u32[]{:S(2)}, u32[]{:S(2)}) collective-permute-start(f32[2,8,16,128]{3,2,1,0:T(8,128)S(1)} %get-tuple-element.47), channel_id=1, source_target_pairs={{0,16},{16,0},{1,17},{17,1},{2,18},{18,2},{3,19},{19,3},{4,20},{20... | collective-permute-start | bytes 393224 | tf_op jit(solution)/shard_map/ppermute | solution.py:501
  23.0 0.0 collective-permute-done.6.rest
  23.0 0.0 collective-permute-done.7.their_rest
  23.0 2.5 %shard_map.80 = f32[2,8,16,128]{3,2,1,0:T(8,128)S(1)} custom-call(f32[24,64,128]{2,1,0:T(8,128)S(1)} %get-tuple-element.38.states, f32[8,16,128]{2,1,0:T(8,128)S(1)} %collective-permute-done.3.own, f32[16,16,128]{2,1,0:T(8,128)S(1)} %collective-permute-done.6.rest, f32[8,16,128]{2,1,0:T(8,128)S(1)} %collective-permute-done.5.their_own, ...), custom_call_target="tpu_custom_call" | custom-call | flops 10000000 | bytes 1048576 | tf_op jit(solution)/shard_map/pallas_call | solution.py:502
  25.5 1.8 %collective-permute-done.8 = f32[2,8,16,128]{3,2,1,0:T(8,128)S(1)} collective-permute-done((f32[2,8,16,128]{3,2,1,0:T(8,128)S(1)}, f32[2,8,16,128]{3,2,1,0:T(8,128)S(1)}, u32[]{:S(2)}, u32[]{:S(2)}) %collective-permute-start.8) | collective-permute-done | bytes 131104 | tf_op jit(solution)/shard_map/ppermute | solution.py:501
  27.3 0.1 collective-permute-start.9
  27.4 1.8 %collective-permute-start.10 = (f32[8,16,128]{2,1,0:T(8,128)S(1)}, f32[8,16,128]{2,1,0:T(8,128)S(1)}, u32[]{:S(2)}, u32[]{:S(2)}) collective-permute-start(f32[8,16,128]{2,1,0:T(8,128)S(1)} %get-tuple-element.51), channel_id=1, source_target_pairs={{0,8},{4,12},{8,0},{12,4},{1,9},{5,13},{9,1},{13,5},{2,10},{6,14},... | collective-permute-start | bytes 196616 | tf_op jit(solution)/shard_map/ppermute | solution.py:514
  29.2 0.1 collective-permute-start.11
  29.3 0.0 collective-permute-done.9.core
  29.3 2.6 %collective-permute-done.10.flip = f32[8,16,128]{2,1,0:T(8,128)S(1)} collective-permute-done((f32[8,16,128]{2,1,0:T(8,128)S(1)}, f32[8,16,128]{2,1,0:T(8,128)S(1)}, u32[]{:S(2)}, u32[]{:S(2)}) %collective-permute-start.10) | collective-permute-done | bytes 65568 | tf_op jit(solution)/shard_map/ppermute | solution.py:514
  31.9 1.3 %collective-permute-done.11.both = f32[8,16,128]{2,1,0:T(8,128)S(1)} collective-permute-done((f32[8,16,128]{2,1,0:T(8,128)S(1)}, f32[8,16,128]{2,1,0:T(8,128)S(1)}, u32[]{:S(2)}, u32[]{:S(2)}) %collective-permute-start.11) | collective-permute-done | bytes 65568 | tf_op jit(solution)/shard_map/ppermute | solution.py:515
  33.3 0.8 %shard_map.81 = (f32[128,256]{1,0:T(8,128)}, f32[128,256]{1,0:T(8,128)}) custom-call(f32[2,128,128]{2,1,0:T(8,128)S(1)} %get-tuple-element.26.home, f32[8,16,128]{2,1,0:T(8,128)S(1)} %get-tuple-element.54.keep, f32[8,16,128]{2,1,0:T(8,128)S(1)} %collective-permute-done.9.core, f32[8,16,128]{2,1,0:T(8,128)S(1)} %collective-permute-done.10.flip, ...), custom_call_target="tpu_custom_call" | custom-call | bytes 1048576 | tf_op jit(solution)/shard_map/pallas_call | solution.py:517
  (3 shorter events, 0.0 us)
Async XLA Ops:
  2.1 11.3 %collective-permute-start = (f32[34,16,128]{2,1,0:T(8,128)S(1)}, f32[34,16,128]{2,1,0:T(8,128)S(1)}, u32[]{:S(2)}, u32[]{:S(2)}) collective-permute-start(f32[34,16,128]{2,1,0:T(8,128)S(1)} %get-tuple-element.28), channel_id=1, source_target_pairs={{0,8},{4,12},{8,0},{12,4},{1,9},{5,13},{9,1},{13,5},{2,10},{6,14},... | collective-permute-start | bytes 835592 | tf_op jit(solution)/shard_map/ppermute | solution.py:467
  5.2 8.2 %collective-permute-start.1 = (f32[9,16,128]{2,1,0:T(8,128)S(1)}, f32[9,16,128]{2,1,0:T(8,128)S(1)}, u32[]{:S(2)}, u32[]{:S(2)}) collective-permute-start(f32[9,16,128]{2,1,0:T(8,128)S(1)} %get-tuple-element.29), channel_id=1, source_target_pairs={{0,1},{1,2},{2,3},{3,11},{4,5},{5,6},{6,7},{7,15},{8,0},{9,8},{10,... | collective-permute-start | bytes 221192 | tf_op jit(solution)/shard_map/ppermute | solution.py:468
  6.7 6.7 %collective-permute-start.2 = (f32[9,16,128]{2,1,0:T(8,128)S(1)}, f32[9,16,128]{2,1,0:T(8,128)S(1)}, u32[]{:S(2)}, u32[]{:S(2)}) collective-permute-start(f32[9,16,128]{2,1,0:T(8,128)S(1)} %get-tuple-element.30), channel_id=1, source_target_pairs={{0,4},{1,8},{2,9},{3,10},{4,0},{5,12},{6,13},{7,14},{8,1},{9,2},{1... | collective-permute-start | bytes 221192 | tf_op jit(solution)/shard_map/ppermute | solution.py:469
  6.7 4.5 %collective-permute-start.3 = (f32[8,16,128]{2,1,0:T(8,128)S(1)}, f32[8,16,128]{2,1,0:T(8,128)S(1)}, u32[]{:S(2)}, u32[]{:S(2)}) collective-permute-start(f32[8,16,128]{2,1,0:T(8,128)S(1)} %slice.3), channel_id=1, source_target_pairs={{16,0},{0,16},{17,1},{1,17},{18,2},{2,18},{19,3},{3,19},{20,4},{4,... | collective-permute-start | bytes 196616 | tf_op jit(solution)/shard_map/ppermute | solution.py:471
  14.4 2.3 %collective-permute-start.4 = (f32[2,33,16,128]{3,2,1,0:T(8,128)S(1)}, f32[2,33,16,128]{3,2,1,0:T(8,128)S(1)}, u32[]{:S(2)}, u32[]{:S(2)}) collective-permute-start(f32[2,33,16,128]{3,2,1,0:T(8,128)S(1)} %get-tuple-element.35), channel_id=1, source_target_pairs={{0,4},{4,0},{8,12},{12,8},{1,5},{5,1},{9,13},{13,9},{2,6},{6,2},{1... | collective-permute-start | bytes 1622024 | tf_op jit(solution)/shard_map/ppermute | solution.py:480
  14.5 2.2 %collective-permute-start.5 = (f32[8,16,128]{2,1,0:T(8,128)S(1)}, f32[8,16,128]{2,1,0:T(8,128)S(1)}, u32[]{:S(2)}, u32[]{:S(2)}) collective-permute-start(f32[8,16,128]{2,1,0:T(8,128)S(1)} %collective-permute-done.3.own), channel_id=1, source_target_pairs={{0,4},{4,0},{8,12},{12,8},{1,5},{5,1},{9,13},{13,9},{2,6},{6,2},{1... | collective-permute-start | bytes 196616 | tf_op jit(solution)/shard_map/ppermute | solution.py:482
  15.0 8.0 %collective-permute-start.6 = (f32[16,16,128]{2,1,0:T(8,128)S(1)}, f32[16,16,128]{2,1,0:T(8,128)S(1)}, u32[]{:S(2)}, u32[]{:S(2)}) collective-permute-start(f32[16,16,128]{2,1,0:T(8,128)S(1)} %get-tuple-element.39), channel_id=1, source_target_pairs={{16,0},{0,16},{17,1},{1,17},{18,2},{2,18},{19,3},{3,19},{20,4},{4,... | collective-permute-start | bytes 393224 | tf_op jit(solution)/shard_map/ppermute | solution.py:483
  16.7 6.3 %collective-permute-start.7 = (f32[16,16,128]{2,1,0:T(8,128)S(1)}, f32[16,16,128]{2,1,0:T(8,128)S(1)}, u32[]{:S(2)}, u32[]{:S(2)}) collective-permute-start(f32[16,16,128]{2,1,0:T(8,128)S(1)} %get-tuple-element.39), channel_id=1, source_target_pairs={{0,20},{4,16},{8,28},{12,24},{16,4},{20,0},{24,12},{28,8},{1,21},{... | collective-permute-start | bytes 393224 | tf_op jit(solution)/shard_map/ppermute | solution.py:484
  21.4 5.9 %collective-permute-start.8 = (f32[2,8,16,128]{3,2,1,0:T(8,128)S(1)}, f32[2,8,16,128]{3,2,1,0:T(8,128)S(1)}, u32[]{:S(2)}, u32[]{:S(2)}) collective-permute-start(f32[2,8,16,128]{3,2,1,0:T(8,128)S(1)} %get-tuple-element.47), channel_id=1, source_target_pairs={{0,16},{16,0},{1,17},{17,1},{2,18},{18,2},{3,19},{19,3},{4,20},{20... | collective-permute-start | bytes 393224 | tf_op jit(solution)/shard_map/ppermute | solution.py:501
  27.3 1.9 %collective-permute-start.9 = (f32[8,16,128]{2,1,0:T(8,128)S(1)}, f32[8,16,128]{2,1,0:T(8,128)S(1)}, u32[]{:S(2)}, u32[]{:S(2)}) collective-permute-start(f32[8,16,128]{2,1,0:T(8,128)S(1)} %get-tuple-element.55), channel_id=1, source_target_pairs={{0,4},{4,0},{8,12},{12,8},{1,5},{5,1},{9,13},{13,9},{2,6},{6,2},{1... | collective-permute-start | bytes 196616 | tf_op jit(solution)/shard_map/ppermute | solution.py:516
  27.4 4.5 %collective-permute-start.10 = (f32[8,16,128]{2,1,0:T(8,128)S(1)}, f32[8,16,128]{2,1,0:T(8,128)S(1)}, u32[]{:S(2)}, u32[]{:S(2)}) collective-permute-start(f32[8,16,128]{2,1,0:T(8,128)S(1)} %get-tuple-element.51), channel_id=1, source_target_pairs={{0,8},{4,12},{8,0},{12,4},{1,9},{5,13},{9,1},{13,5},{2,10},{6,14},... | collective-permute-start | bytes 196616 | tf_op jit(solution)/shard_map/ppermute | solution.py:514
  29.2 4.0 %collective-permute-start.11 = (f32[8,16,128]{2,1,0:T(8,128)S(1)}, f32[8,16,128]{2,1,0:T(8,128)S(1)}, u32[]{:S(2)}, u32[]{:S(2)}) collective-permute-start(f32[8,16,128]{2,1,0:T(8,128)S(1)} %get-tuple-element.50), channel_id=1, source_target_pairs={{0,12},{4,8},{8,4},{12,0},{1,13},{5,9},{9,5},{13,1},{2,14},{6,10},... | collective-permute-start | bytes 196616 | tf_op jit(solution)/shard_map/ppermute | solution.py:515

commit v5 on v4

--- a/solution.py
+++ b/solution.py
@@ -283,7 +283,7 @@
             north[p, at, :] = jnp.where(has_north, n, 0.0)
             east[p, at, :] = wests[p + 1]
 
-    def newton(from_previous):
+    def newton(from_previous, store):
         for first in chunks(lines):
             at = pl.ds(first, CHUNK)
             sink_here = sink[at, :]
@@ -302,32 +302,35 @@
 
             def right(p):
                 current, tangent = state(p)
-                side = edge[p, at, :]
-                below = jnp.where(is_first, side, roll(current, 1))
-                above = jnp.where(is_last, side, roll(current, -1))
+                below, above = roll(current, 1), roll(current, -1)
+                if from_previous:
+                    side = edge[p, at, :]
+                    below, above = jnp.where(is_first, side, below), jnp.where(is_last, side, above)
                 behind = padded(level, p - 1, first) if p else shifted(level, BLOCK - 1, first, -1)
                 ahead = padded(level, p + 1, first) if p < BLOCK - 1 else shifted(level, 0, first, 1)
                 behind_edge = east[p - 1, at, :] if p else west[at, :]
                 pulled = (south[p, at, :] * below + north[p, at, :] * above + behind_edge * behind + east[p, at, :] * ahead)
                 if from_previous:
-                    held = (1.0 - base[p, at, :]) * current
+                    held = current + forcing[p, at, :]
+                    previous[p, at, :] = held
                 else:
-                    held = previous[p, at, :] - base[p, at, :] * current
-                return held + pulled - sink_here * tangent + forcing[p, at, :]
+                    held = previous[p, at, :]
+                return held - base[p, at, :] * current + pulled - sink_here * tangent
 
             factor_and_solve(first, diagonal, right, south, north, east, west, scaled, old)
         sweep(lines, scaled, old, put_into(new))
         sweep(lines, scaled, new, put_into(old))
-        sweep(lines, scaled, old, lambda first, p, z: put_padded(level, p, first, padded(level, p, first) + z))
+        sweep(lines, scaled, old, store)
 
     def step(number, carry):
-        for p in range(BLOCK):
-            previous[p] = level[p, pl.ds(BLOCK, lines), :]
-        newton(True)
-        for _ in range(1, NEWTON):
-            newton(False)
-        for p in range(BLOCK):
-            states[number * BLOCK + p] = level[p, pl.ds(BLOCK, lines), :]
+        def store(keep, first, p, z):
+            value = padded(level, p, first) + z
+            put_padded(level, p, first, value)
+            if keep:
+                states[number * BLOCK + p, pl.ds(first, CHUNK), :] = value
+
+        for turn in range(NEWTON):
+            newton(turn == 0, functools.partial(store, turn == NEWTON - 1))
         return carry
 
     lax.fori_loop(0, STEPS, step, 0)
@@ -475,7 +478,7 @@
         [shape(2, WIDE, count, LANES)] * 2 + [shape(2 * BLOCK, count, LANES)],
         "vvvv",
         [pltpu.VMEM((BLOCK, count, LANES), F32), pltpu.SemaphoreType.DMA((2,))],
-        out_specs=[VMEM, VMEM, HBM],
+
     )(own, other, along, across)
     theirs = lax.ppermute(send, "sx", core_pairs)
 

time: 34.3 us -> 34.2 us (level)
  no operation moved by 1% of the time
where the time goes in v5:
time: 34.2 us; the launch traced here: 34 us
  starting transfers between devices  12 us (35%)
  waiting for transfers between devices  10.9 us (32%)
  Pallas kernels  10.4 us (30%)
  between operations  0.71 us (2%)
    pallas_call x1, Pallas kernels, per_device(): call(functools.partial(forward_kernel, 4 * strips_y), [shape(STEPS * BLOC...  4.64 us
    ppermute x1, starting transfers between devices, per_device(): other = lax.ppermute(flip, 'sx', flip_pairs)  3.03 us
    ppermute x1, waiting for transfers between devices, per_device(): next_own = lax.ppermute(own[:BLOCK], 'slab', back)  2.95 us
    ppermute x1, waiting for transfers between devices, per_device(): flip = lax.ppermute(flip, 'sx', flip_pairs)  2.64 us
    pallas_call x1, Pallas kernels, per_device(): call(adjoint_kernel, [strip], 'v' * 11, [buffer, buffer, plain] + scaled,...  2.46 us
    ppermute x1, waiting for transfers between devices, per_device(): along = lax.ppermute(along, ('sx', 'sy'), along_pairs)  2.14 us
    ppermute x1, waiting for transfers between devices, per_device(): previous = lax.ppermute(ends, 'slab', forth)  1.84 us
    ppermute x1, starting transfers between devices, per_device(): flip = lax.ppermute(flip, 'sx', flip_pairs)  1.78 us
  transfers between devices with their start and end apart: 12, of which 5 were waited for; matrix products, arithmetic and copies ran while one was open for 0% of the time, Pallas kernels for 21%

profile of v5, /device:TPU:0, one launch (start us, length us, event | category | flops | bytes accessed | tf_op | source)
XLA Modules:
  0.0 34.0 jit_solution(14287624431794855026)
XLA Ops:
  0.6 1.5 %shard_map.77 = (f32[34,16,128]{2,1,0:T(8,128)S(1)}, f32[34,16,128]{2,1,0:T(8,128)S(1)}, f32[9,16,128]{2,1,0:T(8,128)S(1)}, f32[9,16,128]{2,1,0:T(8,128)S(1)}, f32[2,128,128]{2,1,0:T(8,128)S(1)}) custom-call(f32[2]{0:T(128)} %scales.1, f32[2]{0:T(128)} %rates.1, f32[128,256]{1,0:T(8,128)} %bitcast.16, f32[128,256]{1,0:T(8,128)} %bitcast.17, ...), custom_call_target="tpu_custom_call" | custom-call | bytes 1048576 | tf_op jit(solution)/shard_map/pallas_call | solution.py:464
  2.1 3.0 %collective-permute-start = (f32[34,16,128]{2,1,0:T(8,128)S(1)}, f32[34,16,128]{2,1,0:T(8,128)S(1)}, u32[]{:S(2)}, u32[]{:S(2)}) collective-permute-start(f32[34,16,128]{2,1,0:T(8,128)S(1)} %get-tuple-element.28), channel_id=1, source_target_pairs={{0,8},{4,12},{8,0},{12,4},{1,9},{5,13},{9,1},{13,5},{2,10},{6,14},... | collective-permute-start | bytes 835592 | tf_op jit(solution)/shard_map/ppermute | solution.py:470
  5.2 1.6 %collective-permute-start.1 = (f32[9,16,128]{2,1,0:T(8,128)S(1)}, f32[9,16,128]{2,1,0:T(8,128)S(1)}, u32[]{:S(2)}, u32[]{:S(2)}) collective-permute-start(f32[9,16,128]{2,1,0:T(8,128)S(1)} %get-tuple-element.29), channel_id=1, source_target_pairs={{0,1},{1,2},{2,3},{3,11},{4,5},{5,6},{6,7},{7,15},{8,0},{9,8},{10,... | collective-permute-start | bytes 221192 | tf_op jit(solution)/shard_map/ppermute | solution.py:471
  6.7 0.0 collective-permute-start.2
  6.7 1.6 %collective-permute-start.3 = (f32[8,16,128]{2,1,0:T(8,128)S(1)}, f32[8,16,128]{2,1,0:T(8,128)S(1)}, u32[]{:S(2)}, u32[]{:S(2)}) collective-permute-start(f32[8,16,128]{2,1,0:T(8,128)S(1)} %slice.3), channel_id=1, source_target_pairs={{16,0},{0,16},{17,1},{1,17},{18,2},{2,18},{19,3},{3,19},{20,4},{4,... | collective-permute-start | bytes 196616 | tf_op jit(solution)/shard_map/ppermute | solution.py:474
  8.3 2.9 %collective-permute-done.3.own = f32[8,16,128]{2,1,0:T(8,128)S(1)} collective-permute-done((f32[8,16,128]{2,1,0:T(8,128)S(1)}, f32[8,16,128]{2,1,0:T(8,128)S(1)}, u32[]{:S(2)}, u32[]{:S(2)}) %collective-permute-start.3) | collective-permute-done | bytes 65568 | tf_op jit(solution)/shard_map/ppermute | solution.py:474
  11.2 2.1 %collective-permute-done.1.along = f32[9,16,128]{2,1,0:T(8,128)S(1)} collective-permute-done((f32[9,16,128]{2,1,0:T(8,128)S(1)}, f32[9,16,128]{2,1,0:T(8,128)S(1)}, u32[]{:S(2)}, u32[]{:S(2)}) %collective-permute-start.1) | collective-permute-done | bytes 73760 | tf_op jit(solution)/shard_map/ppermute | solution.py:471
  13.4 0.0 collective-permute-done.2.across
  13.4 0.0 collective-permute-done.other
  13.4 1.0 %shard_map.78 = (f32[2,33,16,128]{3,2,1,0:T(8,128)S(1)}, f32[2,33,16,128]{3,2,1,0:T(8,128)S(1)}, f32[16,16,128]{2,1,0:T(8,128)S(1)}) custom-call(f32[34,16,128]{2,1,0:T(8,128)S(1)} %get-tuple-element.27.own, f32[34,16,128]{2,1,0:T(8,128)S(1)} %collective-permute-done.other, f32[9,16,128]{2,1,0:T(8,128)S(1)} %collective-permute-done.1.along, ...), custom_call_target="tpu_custom_call" | custom-call | bytes 1048576 | tf_op jit(solution)/shard_map/pallas_call | solution.py:476
  14.4 0.1 collective-permute-start.4
  14.5 0.5 %collective-permute-start.5 = (f32[8,16,128]{2,1,0:T(8,128)S(1)}, f32[8,16,128]{2,1,0:T(8,128)S(1)}, u32[]{:S(2)}, u32[]{:S(2)}) collective-permute-start(f32[8,16,128]{2,1,0:T(8,128)S(1)} %collective-permute-done.3.own), channel_id=1, source_target_pairs={{0,4},{4,0},{8,12},{12,8},{1,5},{5,1},{9,13},{13,9},{2,6},{6,2},{1... | collective-permute-start | bytes 196616 | tf_op jit(solution)/shard_map/ppermute | solution.py:485
  15.0 1.7 %collective-permute-start.6 = (f32[16,16,128]{2,1,0:T(8,128)S(1)}, f32[16,16,128]{2,1,0:T(8,128)S(1)}, u32[]{:S(2)}, u32[]{:S(2)}) collective-permute-start(f32[16,16,128]{2,1,0:T(8,128)S(1)} %get-tuple-element.39), channel_id=1, source_target_pairs={{16,0},{0,16},{17,1},{1,17},{18,2},{2,18},{19,3},{3,19},{20,4},{4,... | collective-permute-start | bytes 393224 | tf_op jit(solution)/shard_map/ppermute | solution.py:486
  16.7 0.0 collective-permute-start.7
  16.7 0.0 collective-permute-done.5.their_own
  16.7 0.0 collective-permute-done.4.theirs
  16.7 4.6 %shard_map.79 = (f32[24,64,128]{2,1,0:T(8,128)S(1)}, f32[2,8,16,128]{3,2,1,0:T(8,128)S(1)}, f32[8,64,128]{2,1,0:T(8,128)S(1)}, f32[8,64,128]{2,1,0:T(8,128)S(1)}...) custom-call(f32[2,33,16,128]{3,2,1,0:T(8,128)S(1)} %get-tuple-element.34, ...), custom_call_target="tpu_custom_call" | custom-call | flops 20000000 | bytes 1048576 | tf_op jit(solution)/shard_map/pallas_call | solution.py:497
  21.4 1.6 %collective-permute-start.8 = (f32[2,8,16,128]{3,2,1,0:T(8,128)S(1)}, f32[2,8,16,128]{3,2,1,0:T(8,128)S(1)}, u32[]{:S(2)}, u32[]{:S(2)}) collective-permute-start(f32[2,8,16,128]{3,2,1,0:T(8,128)S(1)} %get-tuple-element.47), channel_id=1, source_target_pairs={{0,16},{16,0},{1,17},{17,1},{2,18},{18,2},{3,19},{19,3},{4,20},{20... | collective-permute-start | bytes 393224 | tf_op jit(solution)/shard_map/ppermute | solution.py:504
  22.9 0.0 collective-permute-done.6.rest
  22.9 0.0 collective-permute-done.7.their_rest
  23.0 2.5 %shard_map.80 = f32[2,8,16,128]{3,2,1,0:T(8,128)S(1)} custom-call(f32[24,64,128]{2,1,0:T(8,128)S(1)} %get-tuple-element.38.states, f32[8,16,128]{2,1,0:T(8,128)S(1)} %collective-permute-done.3.own, f32[16,16,128]{2,1,0:T(8,128)S(1)} %collective-permute-done.6.rest, f32[8,16,128]{2,1,0:T(8,128)S(1)} %collective-permute-done.5.their_own, ...), custom_call_target="tpu_custom_call" | custom-call | flops 10000000 | bytes 1048576 | tf_op jit(solution)/shard_map/pallas_call | solution.py:505
  25.4 1.8 %collective-permute-done.8 = f32[2,8,16,128]{3,2,1,0:T(8,128)S(1)} collective-permute-done((f32[2,8,16,128]{3,2,1,0:T(8,128)S(1)}, f32[2,8,16,128]{3,2,1,0:T(8,128)S(1)}, u32[]{:S(2)}, u32[]{:S(2)}) %collective-permute-start.8) | collective-permute-done | bytes 131104 | tf_op jit(solution)/shard_map/ppermute | solution.py:504
  27.3 0.1 collective-permute-start.9
  27.4 1.8 %collective-permute-start.10 = (f32[8,16,128]{2,1,0:T(8,128)S(1)}, f32[8,16,128]{2,1,0:T(8,128)S(1)}, u32[]{:S(2)}, u32[]{:S(2)}) collective-permute-start(f32[8,16,128]{2,1,0:T(8,128)S(1)} %get-tuple-element.51), channel_id=1, source_target_pairs={{0,8},{4,12},{8,0},{12,4},{1,9},{5,13},{9,1},{13,5},{2,10},{6,14},... | collective-permute-start | bytes 196616 | tf_op jit(solution)/shard_map/ppermute | solution.py:517
  29.1 0.1 collective-permute-start.11
  29.2 0.0 collective-permute-done.9.core
  29.2 2.6 %collective-permute-done.10.flip = f32[8,16,128]{2,1,0:T(8,128)S(1)} collective-permute-done((f32[8,16,128]{2,1,0:T(8,128)S(1)}, f32[8,16,128]{2,1,0:T(8,128)S(1)}, u32[]{:S(2)}, u32[]{:S(2)}) %collective-permute-start.10) | collective-permute-done | bytes 65568 | tf_op jit(solution)/shard_map/ppermute | solution.py:517
  31.9 1.3 %collective-permute-done.11.both = f32[8,16,128]{2,1,0:T(8,128)S(1)} collective-permute-done((f32[8,16,128]{2,1,0:T(8,128)S(1)}, f32[8,16,128]{2,1,0:T(8,128)S(1)}, u32[]{:S(2)}, u32[]{:S(2)}) %collective-permute-start.11) | collective-permute-done | bytes 65568 | tf_op jit(solution)/shard_map/ppermute | solution.py:518
  33.2 0.8 %shard_map.81 = (f32[128,256]{1,0:T(8,128)}, f32[128,256]{1,0:T(8,128)}) custom-call(f32[2,128,128]{2,1,0:T(8,128)S(1)} %get-tuple-element.26.home, f32[8,16,128]{2,1,0:T(8,128)S(1)} %get-tuple-element.54.keep, f32[8,16,128]{2,1,0:T(8,128)S(1)} %collective-permute-done.9.core, f32[8,16,128]{2,1,0:T(8,128)S(1)} %collective-permute-done.10.flip, ...), custom_call_target="tpu_custom_call" | custom-call | bytes 1048576 | tf_op jit(solution)/shard_map/pallas_call | solution.py:520
  (3 shorter events, 0.0 us)
Async XLA Ops:
  2.1 11.3 %collective-permute-start = (f32[34,16,128]{2,1,0:T(8,128)S(1)}, f32[34,16,128]{2,1,0:T(8,128)S(1)}, u32[]{:S(2)}, u32[]{:S(2)}) collective-permute-start(f32[34,16,128]{2,1,0:T(8,128)S(1)} %get-tuple-element.28), channel_id=1, source_target_pairs={{0,8},{4,12},{8,0},{12,4},{1,9},{5,13},{9,1},{13,5},{2,10},{6,14},... | collective-permute-start | bytes 835592 | tf_op jit(solution)/shard_map/ppermute | solution.py:470
  5.2 8.2 %collective-permute-start.1 = (f32[9,16,128]{2,1,0:T(8,128)S(1)}, f32[9,16,128]{2,1,0:T(8,128)S(1)}, u32[]{:S(2)}, u32[]{:S(2)}) collective-permute-start(f32[9,16,128]{2,1,0:T(8,128)S(1)} %get-tuple-element.29), channel_id=1, source_target_pairs={{0,1},{1,2},{2,3},{3,11},{4,5},{5,6},{6,7},{7,15},{8,0},{9,8},{10,... | collective-permute-start | bytes 221192 | tf_op jit(solution)/shard_map/ppermute | solution.py:471
  6.7 6.7 %collective-permute-start.2 = (f32[9,16,128]{2,1,0:T(8,128)S(1)}, f32[9,16,128]{2,1,0:T(8,128)S(1)}, u32[]{:S(2)}, u32[]{:S(2)}) collective-permute-start(f32[9,16,128]{2,1,0:T(8,128)S(1)} %get-tuple-element.30), channel_id=1, source_target_pairs={{0,4},{1,8},{2,9},{3,10},{4,0},{5,12},{6,13},{7,14},{8,1},{9,2},{1... | collective-permute-start | bytes 221192 | tf_op jit(solution)/shard_map/ppermute | solution.py:472
  6.7 4.5 %collective-permute-start.3 = (f32[8,16,128]{2,1,0:T(8,128)S(1)}, f32[8,16,128]{2,1,0:T(8,128)S(1)}, u32[]{:S(2)}, u32[]{:S(2)}) collective-permute-start(f32[8,16,128]{2,1,0:T(8,128)S(1)} %slice.3), channel_id=1, source_target_pairs={{16,0},{0,16},{17,1},{1,17},{18,2},{2,18},{19,3},{3,19},{20,4},{4,... | collective-permute-start | bytes 196616 | tf_op jit(solution)/shard_map/ppermute | solution.py:474
  14.4 2.3 %collective-permute-start.4 = (f32[2,33,16,128]{3,2,1,0:T(8,128)S(1)}, f32[2,33,16,128]{3,2,1,0:T(8,128)S(1)}, u32[]{:S(2)}, u32[]{:S(2)}) collective-permute-start(f32[2,33,16,128]{3,2,1,0:T(8,128)S(1)} %get-tuple-element.35), channel_id=1, source_target_pairs={{0,4},{4,0},{8,12},{12,8},{1,5},{5,1},{9,13},{13,9},{2,6},{6,2},{1... | collective-permute-start | bytes 1622024 | tf_op jit(solution)/shard_map/ppermute | solution.py:483
  14.5 2.2 %collective-permute-start.5 = (f32[8,16,128]{2,1,0:T(8,128)S(1)}, f32[8,16,128]{2,1,0:T(8,128)S(1)}, u32[]{:S(2)}, u32[]{:S(2)}) collective-permute-start(f32[8,16,128]{2,1,0:T(8,128)S(1)} %collective-permute-done.3.own), channel_id=1, source_target_pairs={{0,4},{4,0},{8,12},{12,8},{1,5},{5,1},{9,13},{13,9},{2,6},{6,2},{1... | collective-permute-start | bytes 196616 | tf_op jit(solution)/shard_map/ppermute | solution.py:485
  15.0 8.0 %collective-permute-start.6 = (f32[16,16,128]{2,1,0:T(8,128)S(1)}, f32[16,16,128]{2,1,0:T(8,128)S(1)}, u32[]{:S(2)}, u32[]{:S(2)}) collective-permute-start(f32[16,16,128]{2,1,0:T(8,128)S(1)} %get-tuple-element.39), channel_id=1, source_target_pairs={{16,0},{0,16},{17,1},{1,17},{18,2},{2,18},{19,3},{3,19},{20,4},{4,... | collective-permute-start | bytes 393224 | tf_op jit(solution)/shard_map/ppermute | solution.py:486
  16.7 6.2 %collective-permute-start.7 = (f32[16,16,128]{2,1,0:T(8,128)S(1)}, f32[16,16,128]{2,1,0:T(8,128)S(1)}, u32[]{:S(2)}, u32[]{:S(2)}) collective-permute-start(f32[16,16,128]{2,1,0:T(8,128)S(1)} %get-tuple-element.39), channel_id=1, source_target_pairs={{0,20},{4,16},{8,28},{12,24},{16,4},{20,0},{24,12},{28,8},{1,21},{... | collective-permute-start | bytes 393224 | tf_op jit(solution)/shard_map/ppermute | solution.py:487
  21.4 5.9 %collective-permute-start.8 = (f32[2,8,16,128]{3,2,1,0:T(8,128)S(1)}, f32[2,8,16,128]{3,2,1,0:T(8,128)S(1)}, u32[]{:S(2)}, u32[]{:S(2)}) collective-permute-start(f32[2,8,16,128]{3,2,1,0:T(8,128)S(1)} %get-tuple-element.47), channel_id=1, source_target_pairs={{0,16},{16,0},{1,17},{17,1},{2,18},{18,2},{3,19},{19,3},{4,20},{20... | collective-permute-start | bytes 393224 | tf_op jit(solution)/shard_map/ppermute | solution.py:504
  27.3 1.9 %collective-permute-start.9 = (f32[8,16,128]{2,1,0:T(8,128)S(1)}, f32[8,16,128]{2,1,0:T(8,128)S(1)}, u32[]{:S(2)}, u32[]{:S(2)}) collective-permute-start(f32[8,16,128]{2,1,0:T(8,128)S(1)} %get-tuple-element.55), channel_id=1, source_target_pairs={{0,4},{4,0},{8,12},{12,8},{1,5},{5,1},{9,13},{13,9},{2,6},{6,2},{1... | collective-permute-start | bytes 196616 | tf_op jit(solution)/shard_map/ppermute | solution.py:519
  27.4 4.5 %collective-permute-start.10 = (f32[8,16,128]{2,1,0:T(8,128)S(1)}, f32[8,16,128]{2,1,0:T(8,128)S(1)}, u32[]{:S(2)}, u32[]{:S(2)}) collective-permute-start(f32[8,16,128]{2,1,0:T(8,128)S(1)} %get-tuple-element.51), channel_id=1, source_target_pairs={{0,8},{4,12},{8,0},{12,4},{1,9},{5,13},{9,1},{13,5},{2,10},{6,14},... | collective-permute-start | bytes 196616 | tf_op jit(solution)/shard_map/ppermute | solution.py:517
  29.1 4.0 %collective-permute-start.11 = (f32[8,16,128]{2,1,0:T(8,128)S(1)}, f32[8,16,128]{2,1,0:T(8,128)S(1)}, u32[]{:S(2)}, u32[]{:S(2)}) collective-permute-start(f32[8,16,128]{2,1,0:T(8,128)S(1)} %get-tuple-element.50), channel_id=1, source_target_pairs={{0,12},{4,8},{8,4},{12,0},{1,13},{5,9},{9,5},{13,1},{2,14},{6,10},... | collective-permute-start | bytes 196616 | tf_op jit(solution)/shard_map/ppermute | solution.py:518

commit v6 on v5

--- a/solution.py
+++ b/solution.py
@@ -109,7 +109,7 @@
     place(BLOCK, None, (m0, roll(m0, 32), m1, roll(m1, 32)))
 
 
-def window_kernel(own, other, along, across, mine, theirs, rest, beside, done):
+def window_kernel(own, other, along, across, next_own, mine, theirs, rest, beside, done):
     y, c, _ = position()
     lower, even = y == 0, c == 0
     at = lax.broadcasted_iota(jnp.int32, own.shape[1:], 1)
@@ -127,6 +127,8 @@
     copies = [pltpu.make_async_copy(part, rest.at[pl.ds(i * BLOCK, BLOCK)], done.at[i]) for part, i in parts]
     for copy in copies:
         copy.start()
+    for p in range(BLOCK):
+        theirs[p // 4, WIDE + p % 4] = next_own[p]
     for slot, (tile, outer) in enumerate(((own, along), (other, across))):
         for p in range(BLOCK + 1):
             inner, far = tile[TILE + p], outer[p]
@@ -348,7 +350,7 @@
             out[core, p] = jnp.where(at < STRIP, roll(low, -HALO), roll(high, HALO))
 
 
-def adjoint_kernel(states, own, rest, their_own, their_rest, south, north, east, west, base, sink, out, old, new, given, *scaled):
+def adjoint_kernel(states, own, rest, theirs, their_rest, south, north, east, west, base, sink, out, old, new, given, *scaled):
     y, c, _ = position()
     lines = base.shape[1]
     count = own.shape[1]
@@ -359,13 +361,13 @@
     turn = jnp.where(even, HALO, LANES - HALO)
     edge = jnp.where(even, lane, lane - (LANES - HALO))
     from_side = (edge >= 0) & (edge < HALO)
-    for first_tile, others, core in ((own, rest, c), (their_own, their_rest, 1 - c)):
+    for others, core in ((rest, c), (their_rest, 1 - c)):
         for slot in range(2):
             chip = y if slot == 0 else 1 - y
             at = pl.ds(pl.multiple_of((2 * chip + core) * count, BLOCK), count)
             side_turn = jnp.where(even, (LANES - 2 * HALO * slot) % LANES, (2 * LANES - 2 * HALO - 2 * HALO * slot) % LANES)
             for p in range(BLOCK):
-                tile = pltpu.roll((others if slot else first_tile)[p], turn, axis=1)
+                tile = pltpu.roll(others[p] if slot else own[p] if others is rest else theirs[p // 4, WIDE + p % 4], turn, axis=1)
                 side = pltpu.roll(others[BLOCK + p], side_turn, axis=1)
                 start = jnp.where(from_side, side, tile)
                 given[p, at, :] = states[(STEPS - 1) * BLOCK + p, at, :] - start
@@ -472,21 +474,17 @@
     across = lax.ppermute(across, ("sx", "sy"), across_pairs)
 
     next_own = lax.ppermute(own[:BLOCK], "slab", back)
-    other, along, across, next_own = lax.optimization_barrier((other, along, across, next_own))
     mine, send, rest = call(
         window_kernel,
-        [shape(2, WIDE, count, LANES)] * 2 + [shape(2 * BLOCK, count, LANES)],
-        "vvvv",
+        [shape(2, WIDE, count, LANES), shape(2, WIDE + 4, count, LANES), shape(2 * BLOCK, count, LANES)],
+        "vvvvv",
         [pltpu.VMEM((BLOCK, count, LANES), F32), pltpu.SemaphoreType.DMA((2,))],
 
-    )(own, other, along, across)
+    )(own, other, along, across, next_own)
     theirs = lax.ppermute(send, "sx", core_pairs)
 
-    their_own = lax.ppermute(next_own, "sx", core_pairs)
     next_rest = lax.ppermute(rest, "slab", back)
     their_rest = lax.ppermute(rest, ("slab", "sx"), both_pairs)
-
-    theirs, their_own = lax.optimization_barrier((theirs, their_own))
 
     whole = shape(BLOCK, lines, LANES)
     flat = shape(lines, LANES)
@@ -503,7 +501,7 @@
     )(mine, theirs)
     previous = lax.ppermute(ends, "slab", forth)
     (adjoint,) = call(adjoint_kernel, [strip], "v" * 11, [buffer, buffer, plain] + scaled, flops=10_000_000)(
-        states, next_own, next_rest, their_own, their_rest, south, north, east, west, base, sink
+        states, next_own, next_rest, theirs, their_rest, south, north, east, west, base, sink
     )
 
     low_lanes = lax.broadcasted_iota(jnp.int32, (BLOCK, count, LANES), 2) < STRIP

time: 34.2 us -> 33.8 us (0.988)
    ppermute x1 -> x0, starting transfers between devices: 0.5 us -> none  [per_device(): their_own = lax.ppermute(next_own, 'sx', core_pairs)]
    ppermute x1, waiting for transfers between devices: 1.84 us -> 1.41 us  [per_device(): previous = lax.ppermute(ends, 'slab', forth)]
  transfers between devices with their start and end apart: 12 -> 11, of which waited for: 5 -> 6; matrix products, arithmetic and copies ran while one was open for 0% -> 0% of each run, Pallas kernels for 21% -> 21%
where the time goes in v6:
time: 33.8 us; the launch traced here: 33.6 us
  starting transfers between devices  11.8 us (35%)
  waiting for transfers between devices  10.6 us (31%)
  Pallas kernels  10.4 us (31%)
  between operations  0.71 us (2%)
    pallas_call x1, Pallas kernels, per_device(): call(functools.partial(forward_kernel, 4 * strips_y), [shape(STEPS * BLOC...  4.64 us
    ppermute x1, starting transfers between devices, per_device(): other = lax.ppermute(flip, 'sx', flip_pairs)  3.03 us
    ppermute x1, waiting for transfers between devices, per_device(): next_own = lax.ppermute(own[:BLOCK], 'slab', back)  2.95 us
    ppermute x1, waiting for transfers between devices, per_device(): flip = lax.ppermute(flip, 'sx', flip_pairs)  2.63 us
    pallas_call x1, Pallas kernels, per_device(): call(adjoint_kernel, [strip], 'v' * 11, [buffer, buffer, plain] + scaled,...  2.46 us
    ppermute x1, waiting for transfers between devices, per_device(): along = lax.ppermute(along, ('sx', 'sy'), along_pairs)  2.14 us
    ppermute x1, starting transfers between devices, per_device(): flip = lax.ppermute(flip, 'sx', flip_pairs)  1.79 us
    ppermute x1, starting transfers between devices, per_device(): previous = lax.ppermute(ends, 'slab', forth)  1.78 us
  transfers between devices with their start and end apart: 11, of which 6 were waited for; matrix products, arithmetic and copies ran while one was open for 0% of the time, Pallas kernels for 21%

profile of v6, /device:TPU:0, one launch (start us, length us, event | category | flops | bytes accessed | tf_op | source)
XLA Modules:
  0.0 33.6 jit_solution(16450430216315402421)
XLA Ops:
  0.6 1.5 %shard_map.77 = (f32[34,16,128]{2,1,0:T(8,128)S(1)}, f32[34,16,128]{2,1,0:T(8,128)S(1)}, f32[9,16,128]{2,1,0:T(8,128)S(1)}, f32[9,16,128]{2,1,0:T(8,128)S(1)}, f32[2,128,128]{2,1,0:T(8,128)S(1)}) custom-call(f32[2]{0:T(128)} %scales.1, f32[2]{0:T(128)} %rates.1, f32[128,256]{1,0:T(8,128)} %bitcast.16, f32[128,256]{1,0:T(8,128)} %bitcast.17, ...), custom_call_target="tpu_custom_call" | custom-call | bytes 1048576 | tf_op jit(solution)/shard_map/pallas_call | solution.py:466
  2.1 3.0 %collective-permute-start = (f32[34,16,128]{2,1,0:T(8,128)S(1)}, f32[34,16,128]{2,1,0:T(8,128)S(1)}, u32[]{:S(2)}, u32[]{:S(2)}) collective-permute-start(f32[34,16,128]{2,1,0:T(8,128)S(1)} %get-tuple-element.22), channel_id=1, source_target_pairs={{0,8},{4,12},{8,0},{12,4},{1,9},{5,13},{9,1},{13,5},{2,10},{6,14},... | collective-permute-start | bytes 835592 | tf_op jit(solution)/shard_map/ppermute | solution.py:472
  5.2 1.6 %collective-permute-start.1 = (f32[9,16,128]{2,1,0:T(8,128)S(1)}, f32[9,16,128]{2,1,0:T(8,128)S(1)}, u32[]{:S(2)}, u32[]{:S(2)}) collective-permute-start(f32[9,16,128]{2,1,0:T(8,128)S(1)} %get-tuple-element.23), channel_id=1, source_target_pairs={{0,1},{1,2},{2,3},{3,11},{4,5},{5,6},{6,7},{7,15},{8,0},{9,8},{10,... | collective-permute-start | bytes 221192 | tf_op jit(solution)/shard_map/ppermute | solution.py:473
  6.7 0.0 collective-permute-start.2
  6.7 1.6 %collective-permute-start.3 = (f32[8,16,128]{2,1,0:T(8,128)S(1)}, f32[8,16,128]{2,1,0:T(8,128)S(1)}, u32[]{:S(2)}, u32[]{:S(2)}) collective-permute-start(f32[8,16,128]{2,1,0:T(8,128)S(1)} %slice.3), channel_id=1, source_target_pairs={{16,0},{0,16},{17,1},{1,17},{18,2},{2,18},{19,3},{3,19},{20,4},{4,... | collective-permute-start | bytes 196616 | tf_op jit(solution)/shard_map/ppermute | solution.py:476
  8.3 2.9 %collective-permute-done.3.next_own.own = f32[8,16,128]{2,1,0:T(8,128)S(1)} collective-permute-done((f32[8,16,128]{2,1,0:T(8,128)S(1)}, f32[8,16,128]{2,1,0:T(8,128)S(1)}, u32[]{:S(2)}, u32[]{:S(2)}) %collective-permute-start.3) | collective-permute-done | bytes 65568 | tf_op jit(solution)/shard_map/ppermute | solution.py:476
  11.2 2.1 %collective-permute-done.1.along = f32[9,16,128]{2,1,0:T(8,128)S(1)} collective-permute-done((f32[9,16,128]{2,1,0:T(8,128)S(1)}, f32[9,16,128]{2,1,0:T(8,128)S(1)}, u32[]{:S(2)}, u32[]{:S(2)}) %collective-permute-start.1) | collective-permute-done | bytes 73760 | tf_op jit(solution)/shard_map/ppermute | solution.py:473
  13.4 0.0 collective-permute-done.2.across
  13.4 0.0 collective-permute-done.other
  13.4 1.0 %shard_map.78 = (f32[2,33,16,128]{3,2,1,0:T(8,128)S(1)}, f32[2,37,16,128]{3,2,1,0:T(8,128)S(1)}, f32[16,16,128]{2,1,0:T(8,128)S(1)}) custom-call(f32[34,16,128]{2,1,0:T(8,128)S(1)} %get-tuple-element.21.own, f32[34,16,128]{2,1,0:T(8,128)S(1)} %collective-permute-done.other, f32[9,16,128]{2,1,0:T(8,128)S(1)} %collective-permute-done.1.along, ...), custom_call_target="tpu_custom_call" | custom-call | bytes 1048576 | tf_op jit(solution)/shard_map/pallas_call | solution.py:477
  14.4 0.1 collective-permute-start.4
  14.5 1.8 %collective-permute-start.5 = (f32[16,16,128]{2,1,0:T(8,128)S(1)}, f32[16,16,128]{2,1,0:T(8,128)S(1)}, u32[]{:S(2)}, u32[]{:S(2)}) collective-permute-start(f32[16,16,128]{2,1,0:T(8,128)S(1)} %get-tuple-element.28), channel_id=1, source_target_pairs={{16,0},{0,16},{17,1},{1,17},{18,2},{2,18},{19,3},{3,19},{20,4},{4,... | collective-permute-start | bytes 393224 | tf_op jit(solution)/shard_map/ppermute | solution.py:486
  16.3 0.1 collective-permute-start.6
  16.4 0.2 collective-permute-done.4.theirs
  16.5 4.6 %shard_map.79 = (f32[24,64,128]{2,1,0:T(8,128)S(1)}, f32[2,8,16,128]{3,2,1,0:T(8,128)S(1)}, f32[8,64,128]{2,1,0:T(8,128)S(1)}, f32[8,64,128]{2,1,0:T(8,128)S(1)}...) custom-call(f32[2,33,16,128]{3,2,1,0:T(8,128)S(1)} %get-tuple-element.25, ...), custom_call_target="tpu_custom_call" | custom-call | flops 20000000 | bytes 1048576 | tf_op jit(solution)/shard_map/pallas_call | solution.py:495
  21.1 1.8 %collective-permute-start.7 = (f32[2,8,16,128]{3,2,1,0:T(8,128)S(1)}, f32[2,8,16,128]{3,2,1,0:T(8,128)S(1)}, u32[]{:S(2)}, u32[]{:S(2)}) collective-permute-start(f32[2,8,16,128]{3,2,1,0:T(8,128)S(1)} %get-tuple-element.35), channel_id=1, source_target_pairs={{0,16},{16,0},{1,17},{17,1},{2,18},{18,2},{3,19},{19,3},{4,20},{20... | collective-permute-start | bytes 393224 | tf_op jit(solution)/shard_map/ppermute | solution.py:502
  22.9 0.0 collective-permute-done.5.rest
  22.9 0.0 collective-permute-done.6.their_rest
  22.9 2.5 %shard_map.80 = f32[2,8,16,128]{3,2,1,0:T(8,128)S(1)} custom-call(f32[24,64,128]{2,1,0:T(8,128)S(1)} %get-tuple-element.27.states, f32[8,16,128]{2,1,0:T(8,128)S(1)} %collective-permute-done.3.next_own.own, f32[16,16,128]{2,1,0:T(8,128)S(1)} %collective-permute-done.5.rest, f32[2,37,16,128]{3,2,1,0:T(8,128)S(1)} %collective-permute-done.4.theirs, ...), custom_call_target="tpu_custom_call" | custom-call | flops 10000000 | bytes 1048576 | tf_op jit(solution)/shard_map/pallas_call | solution.py:503
  25.4 1.4 %collective-permute-done.7 = f32[2,8,16,128]{3,2,1,0:T(8,128)S(1)} collective-permute-done((f32[2,8,16,128]{3,2,1,0:T(8,128)S(1)}, f32[2,8,16,128]{3,2,1,0:T(8,128)S(1)}, u32[]{:S(2)}, u32[]{:S(2)}) %collective-permute-start.7) | collective-permute-done | bytes 131104 | tf_op jit(solution)/shard_map/ppermute | solution.py:502
  26.8 0.1 collective-permute-start.8
  26.9 1.8 %collective-permute-start.9 = (f32[8,16,128]{2,1,0:T(8,128)S(1)}, f32[8,16,128]{2,1,0:T(8,128)S(1)}, u32[]{:S(2)}, u32[]{:S(2)}) collective-permute-start(f32[8,16,128]{2,1,0:T(8,128)S(1)} %get-tuple-element.39), channel_id=1, source_target_pairs={{0,8},{4,12},{8,0},{12,4},{1,9},{5,13},{9,1},{13,5},{2,10},{6,14},... | collective-permute-start | bytes 196616 | tf_op jit(solution)/shard_map/ppermute | solution.py:515
  28.7 0.1 collective-permute-start.10
  28.8 0.0 collective-permute-done.8.core
  28.8 2.6 %collective-permute-done.9.flip = f32[8,16,128]{2,1,0:T(8,128)S(1)} collective-permute-done((f32[8,16,128]{2,1,0:T(8,128)S(1)}, f32[8,16,128]{2,1,0:T(8,128)S(1)}, u32[]{:S(2)}, u32[]{:S(2)}) %collective-permute-start.9) | collective-permute-done | bytes 65568 | tf_op jit(solution)/shard_map/ppermute | solution.py:515
  31.4 1.3 %collective-permute-done.10.both = f32[8,16,128]{2,1,0:T(8,128)S(1)} collective-permute-done((f32[8,16,128]{2,1,0:T(8,128)S(1)}, f32[8,16,128]{2,1,0:T(8,128)S(1)}, u32[]{:S(2)}, u32[]{:S(2)}) %collective-permute-start.10) | collective-permute-done | bytes 65568 | tf_op jit(solution)/shard_map/ppermute | solution.py:516
  32.8 0.8 %shard_map.81 = (f32[128,256]{1,0:T(8,128)}, f32[128,256]{1,0:T(8,128)}) custom-call(f32[2,128,128]{2,1,0:T(8,128)S(1)} %get-tuple-element.20.home, f32[8,16,128]{2,1,0:T(8,128)S(1)} %get-tuple-element.42.keep, f32[8,16,128]{2,1,0:T(8,128)S(1)} %collective-permute-done.8.core, f32[8,16,128]{2,1,0:T(8,128)S(1)} %collective-permute-done.9.flip, ...), custom_call_target="tpu_custom_call" | custom-call | bytes 1048576 | tf_op jit(solution)/shard_map/pallas_call | solution.py:518
  (3 shorter events, 0.0 us)
Async XLA Ops:
  2.1 11.3 %collective-permute-start = (f32[34,16,128]{2,1,0:T(8,128)S(1)}, f32[34,16,128]{2,1,0:T(8,128)S(1)}, u32[]{:S(2)}, u32[]{:S(2)}) collective-permute-start(f32[34,16,128]{2,1,0:T(8,128)S(1)} %get-tuple-element.22), channel_id=1, source_target_pairs={{0,8},{4,12},{8,0},{12,4},{1,9},{5,13},{9,1},{13,5},{2,10},{6,14},... | collective-permute-start | bytes 835592 | tf_op jit(solution)/shard_map/ppermute | solution.py:472
  5.2 8.2 %collective-permute-start.1 = (f32[9,16,128]{2,1,0:T(8,128)S(1)}, f32[9,16,128]{2,1,0:T(8,128)S(1)}, u32[]{:S(2)}, u32[]{:S(2)}) collective-permute-start(f32[9,16,128]{2,1,0:T(8,128)S(1)} %get-tuple-element.23), channel_id=1, source_target_pairs={{0,1},{1,2},{2,3},{3,11},{4,5},{5,6},{6,7},{7,15},{8,0},{9,8},{10,... | collective-permute-start | bytes 221192 | tf_op jit(solution)/shard_map/ppermute | solution.py:473
  6.7 6.7 %collective-permute-start.2 = (f32[9,16,128]{2,1,0:T(8,128)S(1)}, f32[9,16,128]{2,1,0:T(8,128)S(1)}, u32[]{:S(2)}, u32[]{:S(2)}) collective-permute-start(f32[9,16,128]{2,1,0:T(8,128)S(1)} %get-tuple-element.24), channel_id=1, source_target_pairs={{0,4},{1,8},{2,9},{3,10},{4,0},{5,12},{6,13},{7,14},{8,1},{9,2},{1... | collective-permute-start | bytes 221192 | tf_op jit(solution)/shard_map/ppermute | solution.py:474
  6.7 4.5 %collective-permute-start.3 = (f32[8,16,128]{2,1,0:T(8,128)S(1)}, f32[8,16,128]{2,1,0:T(8,128)S(1)}, u32[]{:S(2)}, u32[]{:S(2)}) collective-permute-start(f32[8,16,128]{2,1,0:T(8,128)S(1)} %slice.3), channel_id=1, source_target_pairs={{16,0},{0,16},{17,1},{1,17},{18,2},{2,18},{19,3},{3,19},{20,4},{4,... | collective-permute-start | bytes 196616 | tf_op jit(solution)/shard_map/ppermute | solution.py:476
  14.4 2.1 %collective-permute-start.4 = (f32[2,37,16,128]{3,2,1,0:T(8,128)S(1)}, f32[2,37,16,128]{3,2,1,0:T(8,128)S(1)}, u32[]{:S(2)}, u32[]{:S(2)}) collective-permute-start(f32[2,37,16,128]{3,2,1,0:T(8,128)S(1)} %get-tuple-element.26), channel_id=1, source_target_pairs={{0,4},{4,0},{8,12},{12,8},{1,5},{5,1},{9,13},{13,9},{2,6},{6,2},{1... | collective-permute-start | bytes 1818632 | tf_op jit(solution)/shard_map/ppermute | solution.py:484
  14.5 8.4 %collective-permute-start.5 = (f32[16,16,128]{2,1,0:T(8,128)S(1)}, f32[16,16,128]{2,1,0:T(8,128)S(1)}, u32[]{:S(2)}, u32[]{:S(2)}) collective-permute-start(f32[16,16,128]{2,1,0:T(8,128)S(1)} %get-tuple-element.28), channel_id=1, source_target_pairs={{16,0},{0,16},{17,1},{1,17},{18,2},{2,18},{19,3},{3,19},{20,4},{4,... | collective-permute-start | bytes 393224 | tf_op jit(solution)/shard_map/ppermute | solution.py:486
  16.3 6.7 %collective-permute-start.6 = (f32[16,16,128]{2,1,0:T(8,128)S(1)}, f32[16,16,128]{2,1,0:T(8,128)S(1)}, u32[]{:S(2)}, u32[]{:S(2)}) collective-permute-start(f32[16,16,128]{2,1,0:T(8,128)S(1)} %get-tuple-element.28), channel_id=1, source_target_pairs={{0,20},{4,16},{8,28},{12,24},{16,4},{20,0},{24,12},{28,8},{1,21},{... | collective-permute-start | bytes 393224 | tf_op jit(solution)/shard_map/ppermute | solution.py:487
  21.1 5.7 %collective-permute-start.7 = (f32[2,8,16,128]{3,2,1,0:T(8,128)S(1)}, f32[2,8,16,128]{3,2,1,0:T(8,128)S(1)}, u32[]{:S(2)}, u32[]{:S(2)}) collective-permute-start(f32[2,8,16,128]{3,2,1,0:T(8,128)S(1)} %get-tuple-element.35), channel_id=1, source_target_pairs={{0,16},{16,0},{1,17},{17,1},{2,18},{18,2},{3,19},{19,3},{4,20},{20... | collective-permute-start | bytes 393224 | tf_op jit(solution)/shard_map/ppermute | solution.py:502
  26.8 2.0 %collective-permute-start.8 = (f32[8,16,128]{2,1,0:T(8,128)S(1)}, f32[8,16,128]{2,1,0:T(8,128)S(1)}, u32[]{:S(2)}, u32[]{:S(2)}) collective-permute-start(f32[8,16,128]{2,1,0:T(8,128)S(1)} %get-tuple-element.43), channel_id=1, source_target_pairs={{0,4},{4,0},{8,12},{12,8},{1,5},{5,1},{9,13},{13,9},{2,6},{6,2},{1... | collective-permute-start | bytes 196616 | tf_op jit(solution)/shard_map/ppermute | solution.py:517
  26.9 4.5 %collective-permute-start.9 = (f32[8,16,128]{2,1,0:T(8,128)S(1)}, f32[8,16,128]{2,1,0:T(8,128)S(1)}, u32[]{:S(2)}, u32[]{:S(2)}) collective-permute-start(f32[8,16,128]{2,1,0:T(8,128)S(1)} %get-tuple-element.39), channel_id=1, source_target_pairs={{0,8},{4,12},{8,0},{12,4},{1,9},{5,13},{9,1},{13,5},{2,10},{6,14},... | collective-permute-start | bytes 196616 | tf_op jit(solution)/shard_map/ppermute | solution.py:515
  28.7 4.0 %collective-permute-start.10 = (f32[8,16,128]{2,1,0:T(8,128)S(1)}, f32[8,16,128]{2,1,0:T(8,128)S(1)}, u32[]{:S(2)}, u32[]{:S(2)}) collective-permute-start(f32[8,16,128]{2,1,0:T(8,128)S(1)} %get-tuple-element.38), channel_id=1, source_target_pairs={{0,12},{4,8},{8,4},{12,0},{1,13},{5,9},{9,5},{13,1},{2,14},{6,10},... | collective-permute-start | bytes 196616 | tf_op jit(solution)/shard_map/ppermute | solution.py:516

commit v7 on v6

--- a/solution.py
+++ b/solution.py
@@ -109,7 +109,7 @@
     place(BLOCK, None, (m0, roll(m0, 32), m1, roll(m1, 32)))
 
 
-def window_kernel(own, other, along, across, next_own, mine, theirs, rest, beside, done):
+def window_kernel(own, other, along, across, next_own, mine, theirs, rest):
     y, c, _ = position()
     lower, even = y == 0, c == 0
     at = lax.broadcasted_iota(jnp.int32, own.shape[1:], 1)
@@ -122,11 +122,8 @@
         west0, east0 = pick(lower, along[p], own[TILE + p]), pick(lower, own[TILE + p], along[p])
         west1, east1 = pick(lower, across[p], other[TILE + p]), pick(lower, other[TILE + p], across[p])
         high = jnp.where(at < 96, roll(west1, 64), roll(east1, 96))
-        beside[p] = jnp.where(at < 32, west0, jnp.where(at < 64, roll(east0, 32), high))
-    parts = ((other.at[pl.ds(0, BLOCK)], 0), (beside, 1))
-    copies = [pltpu.make_async_copy(part, rest.at[pl.ds(i * BLOCK, BLOCK)], done.at[i]) for part, i in parts]
-    for copy in copies:
-        copy.start()
+        rest[p] = other[p]
+        rest[BLOCK + p] = jnp.where(at < 32, west0, jnp.where(at < 64, roll(east0, 32), high))
     for p in range(BLOCK):
         theirs[p // 4, WIDE + p % 4] = next_own[p]
     for slot, (tile, outer) in enumerate(((own, along), (other, across))):
@@ -145,8 +142,6 @@
             left = jnp.where(at < 2, roll(west, 32), jnp.where(at == 127, roll(s, 31), roll(k, 30)))
             right = jnp.where(at == 0, roll(s, 97), jnp.where(at == 1, roll(k, 98), jnp.where(at == 127, roll(east, 31), roll(east, 29))))
             put(slot, 3 * BLOCK + p, left, right)
-    for copy in copies:
-        copy.wait()
 
 
 def chunks(lines):
@@ -478,7 +473,6 @@
         window_kernel,
         [shape(2, WIDE, count, LANES), shape(2, WIDE + 4, count, LANES), shape(2 * BLOCK, count, LANES)],
         "vvvvv",
-        [pltpu.VMEM((BLOCK, count, LANES), F32), pltpu.SemaphoreType.DMA((2,))],
 
     )(own, other, along, across, next_own)
     theirs = lax.ppermute(send, "sx", core_pairs)

time: 33.8 us -> 33.5 us (level)
  no operation moved by 1% of the time
where the time goes in v7:
time: 33.5 us; the launch traced here: 33.4 us
  starting transfers between devices  11.8 us (35%)
  waiting for transfers between devices  10.6 us (32%)
  Pallas kernels  10.2 us (30%)
  between operations  0.71 us (2%)
    pallas_call x1, Pallas kernels, per_device(): call(functools.partial(forward_kernel, 4 * strips_y), [shape(STEPS * BLOC...  4.64 us
    ppermute x1, starting transfers between devices, per_device(): other = lax.ppermute(flip, 'sx', flip_pairs)  3.03 us
    ppermute x1, waiting for transfers between devices, per_device(): next_own = lax.ppermute(own[:BLOCK], 'slab', back)  2.95 us
    ppermute x1, waiting for transfers between devices, per_device(): flip = lax.ppermute(flip, 'sx', flip_pairs)  2.63 us
    pallas_call x1, Pallas kernels, per_device(): call(adjoint_kernel, [strip], 'v' * 11, [buffer, buffer, plain] + scaled,...  2.46 us
    ppermute x1, waiting for transfers between devices, per_device(): along = lax.ppermute(along, ('sx', 'sy'), along_pairs)  2.14 us
    ppermute x1, starting transfers between devices, per_device(): flip = lax.ppermute(flip, 'sx', flip_pairs)  1.79 us
    ppermute x1, starting transfers between devices, per_device(): previous = lax.ppermute(ends, 'slab', forth)  1.78 us
  transfers between devices with their start and end apart: 11, of which 6 were waited for; matrix products, arithmetic and copies ran while one was open for 0% of the time, Pallas kernels for 21%

profile of v7, /device:TPU:0, one launch (start us, length us, event | category | flops | bytes accessed | tf_op | source)
XLA Modules:
  0.0 33.4 jit_solution(1887141060448262136)
XLA Ops:
  0.6 1.5 %shard_map.77 = (f32[34,16,128]{2,1,0:T(8,128)S(1)}, f32[34,16,128]{2,1,0:T(8,128)S(1)}, f32[9,16,128]{2,1,0:T(8,128)S(1)}, f32[9,16,128]{2,1,0:T(8,128)S(1)}, f32[2,128,128]{2,1,0:T(8,128)S(1)}) custom-call(f32[2]{0:T(128)} %scales.1, f32[2]{0:T(128)} %rates.1, f32[128,256]{1,0:T(8,128)} %bitcast.16, f32[128,256]{1,0:T(8,128)} %bitcast.17, ...), custom_call_target="tpu_custom_call" | custom-call | bytes 1048576 | tf_op jit(solution)/shard_map/pallas_call | solution.py:461
  2.1 3.0 %collective-permute-start = (f32[34,16,128]{2,1,0:T(8,128)S(1)}, f32[34,16,128]{2,1,0:T(8,128)S(1)}, u32[]{:S(2)}, u32[]{:S(2)}) collective-permute-start(f32[34,16,128]{2,1,0:T(8,128)S(1)} %get-tuple-element.22), channel_id=1, source_target_pairs={{0,8},{4,12},{8,0},{12,4},{1,9},{5,13},{9,1},{13,5},{2,10},{6,14},... | collective-permute-start | bytes 835592 | tf_op jit(solution)/shard_map/ppermute | solution.py:467
  5.2 1.6 %collective-permute-start.1 = (f32[9,16,128]{2,1,0:T(8,128)S(1)}, f32[9,16,128]{2,1,0:T(8,128)S(1)}, u32[]{:S(2)}, u32[]{:S(2)}) collective-permute-start(f32[9,16,128]{2,1,0:T(8,128)S(1)} %get-tuple-element.23), channel_id=1, source_target_pairs={{0,1},{1,2},{2,3},{3,11},{4,5},{5,6},{6,7},{7,15},{8,0},{9,8},{10,... | collective-permute-start | bytes 221192 | tf_op jit(solution)/shard_map/ppermute | solution.py:468
  6.7 0.0 collective-permute-start.2
  6.7 1.6 %collective-permute-start.3 = (f32[8,16,128]{2,1,0:T(8,128)S(1)}, f32[8,16,128]{2,1,0:T(8,128)S(1)}, u32[]{:S(2)}, u32[]{:S(2)}) collective-permute-start(f32[8,16,128]{2,1,0:T(8,128)S(1)} %slice.3), channel_id=1, source_target_pairs={{16,0},{0,16},{17,1},{1,17},{18,2},{2,18},{19,3},{3,19},{20,4},{4,... | collective-permute-start | bytes 196616 | tf_op jit(solution)/shard_map/ppermute | solution.py:471
  8.3 2.9 %collective-permute-done.3.next_own.own = f32[8,16,128]{2,1,0:T(8,128)S(1)} collective-permute-done((f32[8,16,128]{2,1,0:T(8,128)S(1)}, f32[8,16,128]{2,1,0:T(8,128)S(1)}, u32[]{:S(2)}, u32[]{:S(2)}) %collective-permute-start.3) | collective-permute-done | bytes 65568 | tf_op jit(solution)/shard_map/ppermute | solution.py:471
  11.2 2.1 %collective-permute-done.1.along = f32[9,16,128]{2,1,0:T(8,128)S(1)} collective-permute-done((f32[9,16,128]{2,1,0:T(8,128)S(1)}, f32[9,16,128]{2,1,0:T(8,128)S(1)}, u32[]{:S(2)}, u32[]{:S(2)}) %collective-permute-start.1) | collective-permute-done | bytes 73760 | tf_op jit(solution)/shard_map/ppermute | solution.py:468
  13.4 0.0 collective-permute-done.2.across
  13.4 0.0 collective-permute-done.other
  13.4 0.7 %shard_map.78 = (f32[2,33,16,128]{3,2,1,0:T(8,128)S(1)}, f32[2,37,16,128]{3,2,1,0:T(8,128)S(1)}, f32[16,16,128]{2,1,0:T(8,128)S(1)}) custom-call(f32[34,16,128]{2,1,0:T(8,128)S(1)} %get-tuple-element.21.own, f32[34,16,128]{2,1,0:T(8,128)S(1)} %collective-permute-done.other, f32[9,16,128]{2,1,0:T(8,128)S(1)} %collective-permute-done.1.along, ...), custom_call_target="tpu_custom_call" | custom-call | bytes 1048576 | tf_op jit(solution)/shard_map/pallas_call | solution.py:472
  14.2 0.1 collective-permute-start.4
  14.2 1.8 %collective-permute-start.5 = (f32[16,16,128]{2,1,0:T(8,128)S(1)}, f32[16,16,128]{2,1,0:T(8,128)S(1)}, u32[]{:S(2)}, u32[]{:S(2)}) collective-permute-start(f32[16,16,128]{2,1,0:T(8,128)S(1)} %get-tuple-element.28), channel_id=1, source_target_pairs={{16,0},{0,16},{17,1},{1,17},{18,2},{2,18},{19,3},{3,19},{20,4},{4,... | collective-permute-start | bytes 393224 | tf_op jit(solution)/shard_map/ppermute | solution.py:480
  16.0 0.1 collective-permute-start.6
  16.1 0.2 collective-permute-done.4.theirs
  16.2 4.6 %shard_map.79 = (f32[24,64,128]{2,1,0:T(8,128)S(1)}, f32[2,8,16,128]{3,2,1,0:T(8,128)S(1)}, f32[8,64,128]{2,1,0:T(8,128)S(1)}, f32[8,64,128]{2,1,0:T(8,128)S(1)}...) custom-call(f32[2,33,16,128]{3,2,1,0:T(8,128)S(1)} %get-tuple-element.25, ...), custom_call_target="tpu_custom_call" | custom-call | flops 20000000 | bytes 1048576 | tf_op jit(solution)/shard_map/pallas_call | solution.py:489
  20.9 1.8 %collective-permute-start.7 = (f32[2,8,16,128]{3,2,1,0:T(8,128)S(1)}, f32[2,8,16,128]{3,2,1,0:T(8,128)S(1)}, u32[]{:S(2)}, u32[]{:S(2)}) collective-permute-start(f32[2,8,16,128]{3,2,1,0:T(8,128)S(1)} %get-tuple-element.35), channel_id=1, source_target_pairs={{0,16},{16,0},{1,17},{17,1},{2,18},{18,2},{3,19},{19,3},{4,20},{20... | collective-permute-start | bytes 393224 | tf_op jit(solution)/shard_map/ppermute | solution.py:496
  22.7 0.0 collective-permute-done.5.rest
  22.7 0.0 collective-permute-done.6.their_rest
  22.7 2.5 %shard_map.80 = f32[2,8,16,128]{3,2,1,0:T(8,128)S(1)} custom-call(f32[24,64,128]{2,1,0:T(8,128)S(1)} %get-tuple-element.27.states, f32[8,16,128]{2,1,0:T(8,128)S(1)} %collective-permute-done.3.next_own.own, f32[16,16,128]{2,1,0:T(8,128)S(1)} %collective-permute-done.5.rest, f32[2,37,16,128]{3,2,1,0:T(8,128)S(1)} %collective-permute-done.4.theirs, ...), custom_call_target="tpu_custom_call" | custom-call | flops 10000000 | bytes 1048576 | tf_op jit(solution)/shard_map/pallas_call | solution.py:497
  25.2 1.4 %collective-permute-done.7 = f32[2,8,16,128]{3,2,1,0:T(8,128)S(1)} collective-permute-done((f32[2,8,16,128]{3,2,1,0:T(8,128)S(1)}, f32[2,8,16,128]{3,2,1,0:T(8,128)S(1)}, u32[]{:S(2)}, u32[]{:S(2)}) %collective-permute-start.7) | collective-permute-done | bytes 131104 | tf_op jit(solution)/shard_map/ppermute | solution.py:496
  26.6 0.1 collective-permute-start.8
  26.7 1.8 %collective-permute-start.9 = (f32[8,16,128]{2,1,0:T(8,128)S(1)}, f32[8,16,128]{2,1,0:T(8,128)S(1)}, u32[]{:S(2)}, u32[]{:S(2)}) collective-permute-start(f32[8,16,128]{2,1,0:T(8,128)S(1)} %get-tuple-element.39), channel_id=1, source_target_pairs={{0,8},{4,12},{8,0},{12,4},{1,9},{5,13},{9,1},{13,5},{2,10},{6,14},... | collective-permute-start | bytes 196616 | tf_op jit(solution)/shard_map/ppermute | solution.py:509
  28.5 0.1 collective-permute-start.10
  28.5 0.0 collective-permute-done.8.core
  28.5 2.6 %collective-permute-done.9.flip = f32[8,16,128]{2,1,0:T(8,128)S(1)} collective-permute-done((f32[8,16,128]{2,1,0:T(8,128)S(1)}, f32[8,16,128]{2,1,0:T(8,128)S(1)}, u32[]{:S(2)}, u32[]{:S(2)}) %collective-permute-start.9) | collective-permute-done | bytes 65568 | tf_op jit(solution)/shard_map/ppermute | solution.py:509
  31.2 1.3 %collective-permute-done.10.both = f32[8,16,128]{2,1,0:T(8,128)S(1)} collective-permute-done((f32[8,16,128]{2,1,0:T(8,128)S(1)}, f32[8,16,128]{2,1,0:T(8,128)S(1)}, u32[]{:S(2)}, u32[]{:S(2)}) %collective-permute-start.10) | collective-permute-done | bytes 65568 | tf_op jit(solution)/shard_map/ppermute | solution.py:510
  32.5 0.8 %shard_map.81 = (f32[128,256]{1,0:T(8,128)}, f32[128,256]{1,0:T(8,128)}) custom-call(f32[2,128,128]{2,1,0:T(8,128)S(1)} %get-tuple-element.20.home, f32[8,16,128]{2,1,0:T(8,128)S(1)} %get-tuple-element.42.keep, f32[8,16,128]{2,1,0:T(8,128)S(1)} %collective-permute-done.8.core, f32[8,16,128]{2,1,0:T(8,128)S(1)} %collective-permute-done.9.flip, ...), custom_call_target="tpu_custom_call" | custom-call | bytes 1048576 | tf_op jit(solution)/shard_map/pallas_call | solution.py:512
  (3 shorter events, 0.0 us)
Async XLA Ops:
  2.1 11.3 %collective-permute-start = (f32[34,16,128]{2,1,0:T(8,128)S(1)}, f32[34,16,128]{2,1,0:T(8,128)S(1)}, u32[]{:S(2)}, u32[]{:S(2)}) collective-permute-start(f32[34,16,128]{2,1,0:T(8,128)S(1)} %get-tuple-element.22), channel_id=1, source_target_pairs={{0,8},{4,12},{8,0},{12,4},{1,9},{5,13},{9,1},{13,5},{2,10},{6,14},... | collective-permute-start | bytes 835592 | tf_op jit(solution)/shard_map/ppermute | solution.py:467
  5.2 8.2 %collective-permute-start.1 = (f32[9,16,128]{2,1,0:T(8,128)S(1)}, f32[9,16,128]{2,1,0:T(8,128)S(1)}, u32[]{:S(2)}, u32[]{:S(2)}) collective-permute-start(f32[9,16,128]{2,1,0:T(8,128)S(1)} %get-tuple-element.23), channel_id=1, source_target_pairs={{0,1},{1,2},{2,3},{3,11},{4,5},{5,6},{6,7},{7,15},{8,0},{9,8},{10,... | collective-permute-start | bytes 221192 | tf_op jit(solution)/shard_map/ppermute | solution.py:468
  6.7 6.7 %collective-permute-start.2 = (f32[9,16,128]{2,1,0:T(8,128)S(1)}, f32[9,16,128]{2,1,0:T(8,128)S(1)}, u32[]{:S(2)}, u32[]{:S(2)}) collective-permute-start(f32[9,16,128]{2,1,0:T(8,128)S(1)} %get-tuple-element.24), channel_id=1, source_target_pairs={{0,4},{1,8},{2,9},{3,10},{4,0},{5,12},{6,13},{7,14},{8,1},{9,2},{1... | collective-permute-start | bytes 221192 | tf_op jit(solution)/shard_map/ppermute | solution.py:469
  6.7 4.5 %collective-permute-start.3 = (f32[8,16,128]{2,1,0:T(8,128)S(1)}, f32[8,16,128]{2,1,0:T(8,128)S(1)}, u32[]{:S(2)}, u32[]{:S(2)}) collective-permute-start(f32[8,16,128]{2,1,0:T(8,128)S(1)} %slice.3), channel_id=1, source_target_pairs={{16,0},{0,16},{17,1},{1,17},{18,2},{2,18},{19,3},{3,19},{20,4},{4,... | collective-permute-start | bytes 196616 | tf_op jit(solution)/shard_map/ppermute | solution.py:471
  14.2 2.1 %collective-permute-start.4 = (f32[2,37,16,128]{3,2,1,0:T(8,128)S(1)}, f32[2,37,16,128]{3,2,1,0:T(8,128)S(1)}, u32[]{:S(2)}, u32[]{:S(2)}) collective-permute-start(f32[2,37,16,128]{3,2,1,0:T(8,128)S(1)} %get-tuple-element.26), channel_id=1, source_target_pairs={{0,4},{4,0},{8,12},{12,8},{1,5},{5,1},{9,13},{13,9},{2,6},{6,2},{1... | collective-permute-start | bytes 1818632 | tf_op jit(solution)/shard_map/ppermute | solution.py:478
  14.2 8.4 %collective-permute-start.5 = (f32[16,16,128]{2,1,0:T(8,128)S(1)}, f32[16,16,128]{2,1,0:T(8,128)S(1)}, u32[]{:S(2)}, u32[]{:S(2)}) collective-permute-start(f32[16,16,128]{2,1,0:T(8,128)S(1)} %get-tuple-element.28), channel_id=1, source_target_pairs={{16,0},{0,16},{17,1},{1,17},{18,2},{2,18},{19,3},{3,19},{20,4},{4,... | collective-permute-start | bytes 393224 | tf_op jit(solution)/shard_map/ppermute | solution.py:480
  16.0 6.7 %collective-permute-start.6 = (f32[16,16,128]{2,1,0:T(8,128)S(1)}, f32[16,16,128]{2,1,0:T(8,128)S(1)}, u32[]{:S(2)}, u32[]{:S(2)}) collective-permute-start(f32[16,16,128]{2,1,0:T(8,128)S(1)} %get-tuple-element.28), channel_id=1, source_target_pairs={{0,20},{4,16},{8,28},{12,24},{16,4},{20,0},{24,12},{28,8},{1,21},{... | collective-permute-start | bytes 393224 | tf_op jit(solution)/shard_map/ppermute | solution.py:481
  20.9 5.7 %collective-permute-start.7 = (f32[2,8,16,128]{3,2,1,0:T(8,128)S(1)}, f32[2,8,16,128]{3,2,1,0:T(8,128)S(1)}, u32[]{:S(2)}, u32[]{:S(2)}) collective-permute-start(f32[2,8,16,128]{3,2,1,0:T(8,128)S(1)} %get-tuple-element.35), channel_id=1, source_target_pairs={{0,16},{16,0},{1,17},{17,1},{2,18},{18,2},{3,19},{19,3},{4,20},{20... | collective-permute-start | bytes 393224 | tf_op jit(solution)/shard_map/ppermute | solution.py:496
  26.6 2.0 %collective-permute-start.8 = (f32[8,16,128]{2,1,0:T(8,128)S(1)}, f32[8,16,128]{2,1,0:T(8,128)S(1)}, u32[]{:S(2)}, u32[]{:S(2)}) collective-permute-start(f32[8,16,128]{2,1,0:T(8,128)S(1)} %get-tuple-element.43), channel_id=1, source_target_pairs={{0,4},{4,0},{8,12},{12,8},{1,5},{5,1},{9,13},{13,9},{2,6},{6,2},{1... | collective-permute-start | bytes 196616 | tf_op jit(solution)/shard_map/ppermute | solution.py:511
  26.7 4.5 %collective-permute-start.9 = (f32[8,16,128]{2,1,0:T(8,128)S(1)}, f32[8,16,128]{2,1,0:T(8,128)S(1)}, u32[]{:S(2)}, u32[]{:S(2)}) collective-permute-start(f32[8,16,128]{2,1,0:T(8,128)S(1)} %get-tuple-element.39), channel_id=1, source_target_pairs={{0,8},{4,12},{8,0},{12,4},{1,9},{5,13},{9,1},{13,5},{2,10},{6,14},... | collective-permute-start | bytes 196616 | tf_op jit(solution)/shard_map/ppermute | solution.py:509
  28.5 4.0 %collective-permute-start.10 = (f32[8,16,128]{2,1,0:T(8,128)S(1)}, f32[8,16,128]{2,1,0:T(8,128)S(1)}, u32[]{:S(2)}, u32[]{:S(2)}) collective-permute-start(f32[8,16,128]{2,1,0:T(8,128)S(1)} %get-tuple-element.38), channel_id=1, source_target_pairs={{0,12},{4,8},{8,4},{12,0},{1,13},{5,9},{9,5},{13,1},{2,14},{6,10},... | collective-permute-start | bytes 196616 | tf_op jit(solution)/shard_map/ppermute | solution.py:510
